TPU v7x, 32 devices: a whole 2x2x4 slice. The times are simulated.
32 devices in a mesh: dp: 8 (over y, x, core), tp: 4 (over z).
Axes of the slice: x: 2, y: 2, z: 4, core: 2. Of those that a mesh axis runs over, the one named last changes fastest.
Arguments:
- layer_in: bfloat16 [32768, 768], P(('dp', 'tp')), may hold values from -6 to 6
- out_grad: bfloat16 [32768, 768], P(('dp', 'tp')), may hold values from -6 to 6
- lengths: int32 [8], P('dp'), may hold values from 2049 to 4096, as said below
- w_query: bfloat16 [768, 768], replicated, may hold values from -0.875 to 0.875
- b_query: bfloat16 [768], replicated, may hold values from -6 to 6
- w_key: bfloat16 [768, 768], replicated, may hold values from -0.21875 to 0.21875
- b_key: bfloat16 [768], replicated, may hold values from -3 to 3
- w_value: bfloat16 [768, 768], replicated, may hold values from -0.21875 to 0.21875
- b_value: bfloat16 [768], replicated, may hold values from -3 to 3
- w_out: bfloat16 [768, 768], replicated, may hold values from -0.875 to 0.875
- b_out: bfloat16 [768], replicated, may hold values from -3 to 3
- seq_proj: bfloat16 [256, 4096], replicated, may hold values from -0.09375 to 0.09375
- attn_gain: bfloat16 [768], replicated, may hold values from 0.5 to 1.5
- attn_shift: bfloat16 [768], replicated, may hold values from -3 to 3
- w_up: bfloat16 [768, 3072], P(None, 'tp'), may hold values from -0.21875 to 0.21875
- b_up: bfloat16 [3072], P('tp'), may hold values from -3 to 3
- w_down: bfloat16 [3072, 768], P('tp'), may hold values from -0.109375 to 0.109375
- b_down: bfloat16 [768], replicated, may hold values from -3 to 3
- ffn_gain: bfloat16 [768], replicated, may hold values from 0.5 to 1.5
- ffn_shift: bfloat16 [768], replicated, may hold values from -3 to 3
Outputs:
- layer_out: bfloat16 [32768, 768], P(('dp', 'tp'))
- grad_in: bfloat16 [32768, 768], P(('dp', 'tp'))
- grad_w_query: float32 [768, 768], replicated
- grad_b_query: float32 [768], replicated
- grad_w_key: float32 [768, 768], replicated
- grad_b_key: float32 [768], replicated
- grad_w_value: float32 [768, 768], replicated
- grad_b_value: float32 [768], replicated
- grad_w_out: float32 [768, 768], replicated
- grad_b_out: float32 [768], replicated
- grad_seq_proj: float32 [256, 4096], replicated
- grad_attn_gain: float32 [768], replicated
- grad_attn_shift: float32 [768], replicated
- grad_w_up: float32 [768, 3072], P(None, 'tp')
- grad_b_up: float32 [3072], P('tp')
- grad_w_down: float32 [3072, 768], P('tp')
- grad_b_down: float32 [768], replicated
- grad_ffn_gain: float32 [768], replicated
- grad_ffn_shift: float32 [768], replicated
Inputs may be any that keep to these rules, and one draw needn't show every extreme that they name: `lengths`: rows from a sequence's length on are padding; some sequence has exactly 4096 rows.
All inputs are finite; a program needn't handle non-finite values.
Results may differ from a plain program's by a relative error of at most 0.022.
The roundings to bfloat16 on the way count: a program that leaves them out, or rounds other values in their place, can miss the bound.
Values may be sent and summed in bfloat16 or wider, within the bound.
A program may use at most 192 MiB of HBM per device.

v0:
```python
import jax
import jax.numpy as jnp
from jax import lax
from jax.sharding import PartitionSpec as P

HEADS = 12
HEAD = 64


def layer_norm(hidden, gain, shift):
    center = hidden - jnp.mean(hidden, axis=-1, keepdims=True)
    spread = jnp.mean(center * center, axis=-1, keepdims=True)
    return center * lax.rsqrt(spread + 1e-05) * gain + shift


def matmul(left, right):
    return jnp.dot(left, right, preferred_element_type=jnp.float32)


def contract_rows(left, right):
    return lax.dot_general(
        left, right, (((0,), (0,)), ((), ())), preferred_element_type=jnp.float32
    )


def times_transpose(left, right):
    return lax.dot_general(
        left, right, (((1,), (1,)), ((), ())), preferred_element_type=jnp.float32
    )


def exact_gelu(value):
    return jax.nn.gelu(value, approximate=False)


def on_device(
    layer_in,
    out_grad,
    lengths,
    w_query,
    b_query,
    w_key,
    b_key,
    w_value,
    b_value,
    w_out,
    b_out,
    seq_proj,
    attn_gain,
    attn_shift,
    w_up,
    b_up,
    w_down,
    b_down,
    ffn_gain,
    ffn_shift,
):
    row_count = layer_in.shape[0]
    width = layer_in.shape[1]
    slots = seq_proj.shape[0]
    tp_parts = lax.axis_size("tp")
    tp_index = lax.axis_index("tp")
    total_rows = row_count * tp_parts
    own_first = tp_index * row_count
    own_positions = own_first + jnp.arange(row_count, dtype=jnp.int32)
    own_live = (own_positions < lengths[0]).astype(jnp.float32)
    own_keys = (matmul(layer_in, w_key) + b_key.astype(jnp.float32)).astype(jnp.bfloat16)
    own_values = (matmul(layer_in, w_value) + b_value.astype(jnp.float32)).astype(jnp.bfloat16)
    own_cols = lax.dynamic_slice_in_dim(seq_proj, own_first, row_count, 1)
    own_proj = (own_cols.astype(jnp.float32) * own_live[None, :]).astype(jnp.bfloat16)
    share_keys = matmul(own_proj, own_keys)
    share_values = matmul(own_proj, own_values)
    proj_keys, proj_values = lax.psum((share_keys, share_values), "tp")
    proj_keys = proj_keys.astype(jnp.bfloat16)
    proj_values = proj_values.astype(jnp.bfloat16)
    queries = (matmul(layer_in, w_query) + b_query.astype(jnp.float32)).astype(jnp.bfloat16)
    block_rows = min(512, row_count)
    block_count = row_count // block_rows
    query_blocks = queries.reshape(block_count, block_rows, HEADS, HEAD)
    key_heads = proj_keys.reshape(slots, HEADS, HEAD)
    value_heads = proj_values.reshape(slots, HEADS, HEAD)

    def attend(query_block):
        logits = (
            jnp.einsum("rhd,khd->rhk", query_block, key_heads, preferred_element_type=jnp.float32)
            * 0.125
        )
        summit = jax.scipy.special.logsumexp(logits, axis=-1)
        weights_b = jnp.exp(logits - summit[..., None]).astype(jnp.bfloat16)
        result = jnp.einsum(
            "rhk,khd->rhd", weights_b, value_heads, preferred_element_type=jnp.float32
        )
        return (result.astype(jnp.bfloat16), summit)

    mixed_blocks, summits = lax.map(attend, query_blocks)
    mixed = mixed_blocks.reshape(row_count, width)
    attn = matmul(mixed, w_out) + b_out.astype(jnp.float32)
    res_one = layer_in.astype(jnp.float32) + attn
    normed, norm_one_pull = jax.vjp(
        layer_norm, res_one, attn_gain.astype(jnp.float32), attn_shift.astype(jnp.float32)
    )
    normed_b = normed.astype(jnp.bfloat16)
    ffn_rows = lax.all_gather(normed_b, "tp", axis=0, tiled=True)
    pre_act = matmul(ffn_rows, w_up) + b_up.astype(jnp.float32)
    hidden_act, gelu_pull = jax.vjp(exact_gelu, pre_act)
    hidden_b = hidden_act.astype(jnp.bfloat16)
    branch = lax.psum_scatter(
        matmul(hidden_b, w_down).astype(jnp.bfloat16), "tp", scatter_dimension=0, tiled=True
    ).astype(jnp.float32)
    branch = branch + b_down.astype(jnp.float32)
    res_two = normed + branch
    final, norm_two_pull = jax.vjp(
        layer_norm, res_two, ffn_gain.astype(jnp.float32), ffn_shift.astype(jnp.float32)
    )
    layer_out = final.astype(jnp.bfloat16)
    d_res_two, g_ffn_gain, g_ffn_shift = norm_two_pull(out_grad.astype(jnp.float32))
    d_branch = d_res_two.astype(jnp.bfloat16)
    g_b_down = jnp.sum(d_branch.astype(jnp.float32), axis=0)
    d_rows = lax.all_gather(d_branch, "tp", axis=0, tiled=True)
    g_w_down = contract_rows(hidden_b, d_rows)
    (d_hidden,) = gelu_pull(times_transpose(d_rows, w_down))
    d_pre = d_hidden.astype(jnp.bfloat16)
    g_b_up = jnp.sum(d_pre.astype(jnp.float32), axis=0)
    g_w_up = contract_rows(ffn_rows, d_pre)
    d_normed_ffn = lax.psum_scatter(
        times_transpose(d_pre, w_up).astype(jnp.bfloat16), "tp", scatter_dimension=0, tiled=True
    ).astype(jnp.float32)
    d_normed = d_res_two + d_normed_ffn
    d_res_one, g_attn_gain, g_attn_shift = norm_one_pull(d_normed)
    d_attn = d_res_one.astype(jnp.bfloat16)
    g_b_out = jnp.sum(d_attn.astype(jnp.float32), axis=0)
    g_w_out = contract_rows(mixed, d_attn)
    d_mixed = times_transpose(d_attn, w_out).astype(jnp.bfloat16)
    d_mixed_blocks = d_mixed.reshape(block_count, block_rows, HEADS, HEAD)

    def attend_back(running, element):
        key_total, value_total = running
        query_block, summit, d_block = element
        logits = (
            jnp.einsum("rhd,khd->rhk", query_block, key_heads, preferred_element_type=jnp.float32)
            * 0.125
        )
        probs = jnp.exp(logits - summit[..., None])
        probs_b = probs.astype(jnp.bfloat16)
        d_probs = jnp.einsum(
            "rhd,khd->rhk", d_block, value_heads, preferred_element_type=jnp.float32
        )
        d_logits = (probs * (d_probs - jnp.sum(probs * d_probs, axis=-1, keepdims=True))).astype(
            jnp.bfloat16
        )
        d_query = (
            jnp.einsum("rhk,khd->rhd", d_logits, key_heads, preferred_element_type=jnp.float32)
            * 0.125
        )
        key_total = (
            key_total
            + jnp.einsum("rhk,rhd->khd", d_logits, query_block, preferred_element_type=jnp.float32)
            * 0.125
        )
        value_total = value_total + jnp.einsum(
            "rhk,rhd->khd", probs_b, d_block, preferred_element_type=jnp.float32
        )
        return ((key_total, value_total), d_query.astype(jnp.bfloat16))

    zero_heads = jnp.zeros((slots, HEADS, HEAD), jnp.float32)
    (key_part, value_part), d_query_blocks = lax.scan(
        attend_back, (zero_heads, zero_heads), (query_blocks, summits, d_mixed_blocks)
    )
    d_queries = d_query_blocks.reshape(row_count, width)
    d_proj_keys, d_proj_values = (
        lax.psum(key_part.reshape(slots, width).astype(jnp.bfloat16), "tp").astype(jnp.float32),
        lax.psum(value_part.reshape(slots, width).astype(jnp.bfloat16), "tp").astype(jnp.float32),
    )
    d_proj_keys = d_proj_keys.astype(jnp.bfloat16)
    d_proj_values = d_proj_values.astype(jnp.bfloat16)
    d_keys = contract_rows(own_proj, d_proj_keys).astype(jnp.bfloat16)
    d_values = contract_rows(own_proj, d_proj_values).astype(jnp.bfloat16)
    own_proj_grad = (
        times_transpose(d_proj_keys, own_keys) + times_transpose(d_proj_values, own_values)
    ) * own_live[None, :]
    g_seq_proj = lax.dynamic_update_slice_in_dim(
        jnp.zeros((slots, total_rows), jnp.float32), own_proj_grad, own_first, 1
    )
    g_w_query = contract_rows(layer_in, d_queries)
    g_b_query = jnp.sum(d_queries.astype(jnp.float32), axis=0)
    g_w_key = contract_rows(layer_in, d_keys)
    g_b_key = jnp.sum(d_keys.astype(jnp.float32), axis=0)
    g_w_value = contract_rows(layer_in, d_values)
    g_b_value = jnp.sum(d_values.astype(jnp.float32), axis=0)
    grad_in = (
        d_res_one
        + times_transpose(d_queries, w_query)
        + times_transpose(d_keys, w_key)
        + times_transpose(d_values, w_value)
    ).astype(jnp.bfloat16)
    (
        g_w_query,
        g_w_key,
        g_w_value,
        g_w_out,
        g_seq_proj,
        g_b_query,
        g_b_key,
        g_b_value,
        g_b_out,
        g_attn_gain,
        g_attn_shift,
        g_ffn_gain,
        g_ffn_shift,
        g_b_down,
    ) = lax.psum(
        (
            g_w_query,
            g_w_key,
            g_w_value,
            g_w_out,
            g_seq_proj,
            g_b_query,
            g_b_key,
            g_b_value,
            g_b_out,
            g_attn_gain,
            g_attn_shift,
            g_ffn_gain,
            g_ffn_shift,
            g_b_down,
        ),
        ("dp", "tp"),
    )
    g_w_up, g_b_up, g_w_down = lax.psum((g_w_up, g_b_up, g_w_down), "dp")
    return (
        layer_out,
        grad_in,
        g_w_query,
        g_b_query,
        g_w_key,
        g_b_key,
        g_w_value,
        g_b_value,
        g_w_out,
        g_b_out,
        g_seq_proj,
        g_attn_gain,
        g_attn_shift,
        g_w_up,
        g_b_up,
        g_w_down,
        g_b_down,
        g_ffn_gain,
        g_ffn_shift,
    )


def solution(mesh):
    in_specs = (
        P(("dp", "tp"), None),
        P(("dp", "tp"), None),
        P("dp"),
        P(),
        P(),
        P(),
        P(),
        P(),
        P(),
        P(),
        P(),
        P(),
        P(),
        P(),
        P(None, "tp"),
        P("tp"),
        P("tp", None),
        P(),
        P(),
        P(),
    )
    out_specs = (
        P(("dp", "tp"), None),
        P(("dp", "tp"), None),
        P(),
        P(),
        P(),
        P(),
        P(),
        P(),
        P(),
        P(),
        P(),
        P(),
        P(),
        P(None, "tp"),
        P("tp"),
        P("tp", None),
        P(),
        P(),
        P(),
    )
    return jax.shard_map(
        on_device, mesh=mesh, in_specs=in_specs, out_specs=out_specs, check_vma=False
    )
```

profile of v0, /device:TPU:0, one launch (start us, length us, event | category | flops | bytes accessed | tf_op | source)
XLA Modules:
  0.0 1117.3 jit_solution(10581152237849772163)
XLA Ops:
  18.0 62.3 %all-reduce.15 = (bf16[256,768]{1,0:T(8,128)(2,1)S(1)}, bf16[256,768]{1,0:T(8,128)(2,1)}) all-reduce(f32[256,768]{1,0:T(8,128)S(1)} %fusion.73, f32[256,768]{1,0:T(8,128)S(1)} %fusion.72), channel_id=1, replica_groups=mesh['dp'=8,'tp'=4] {'tp'}, use_global_device_ids=true, to_apply=%region_0.0 | all-reduce | flops 393216 | bytes 2359296 | tf_op jit(solution)/shard_map/psum | solution.py:73
  81.7 4.3 add_convert_fusion.5
  93.1 9.8 while.27
  102.9 3.9 copy.71
  112.9 113.9 %all-gather.3.cloned.1.call-done = bf16[4096,768]{0,1:T(8,128)(2,1)} async-done(((bf16[1024,768]{0,1:T(8,128)(2,1)}), bf16[4096,768]{0,1:T(8,128)(2,1)}) %all-gather.3.cloned.1.call-update) | async-done | bytes 6291472 | tf_op jit(solution)/shard_map/all_gather | solution.py:103
  226.8 34.7 %multiply_convert_fusion.1 = (bf16[4096,768]{1,0:T(8,128)(2,1)S(1)}, f32[4096,768]{1,0:T(8,128)}, f32[4096,768]{1,0:T(8,128)}) fusion(f32[768]{0:T(1024)S(1)} %convert_element_type.178, bf16[4096,768]{0,1:T(8,128)(2,1)} %all-gather.3.cloned.1.call-done, bf16[768,768]{1,0:T(8,128)(2,1)S(1)} %copy-done), kind=kOutput, calls=%fused_computation.63 | convolution fusion | flops 5039456256 | bytes 38931456 | tf_op jit(solution)/shard_map/dot_general | solution.py:17
  264.2 7.0 convolution_convert_fusion.1
  273.7 106.7 %reduce-scatter.3.cloned.1.call-done = bf16[1024,768]{0,1:T(8,128)(2,1)} async-done(((bf16[4096,768]{0,1:T(8,128)(2,1)}), bf16[1024,768]{0,1:T(8,128)(2,1)}) %reduce-scatter.3.cloned.1.call-update) | async-done | bytes 1572880 | tf_op jit(solution)/shard_map/reduce_scatter | solution.py:107
  380.3 3.2 fusion.84
  392.1 116.0 %all-gather.5.cloned.1.call-done = bf16[4096,768]{0,1:T(8,128)(2,1)} async-done(((bf16[1024,768]{0,1:T(8,128)(2,1)}), bf16[4096,768]{0,1:T(8,128)(2,1)}) %all-gather.5.cloned.1.call-update) | async-done | bytes 6291472 | tf_op jit(solution)/shard_map/all_gather | solution.py:119
  508.1 18.6 %convert_reduce_fusion = (f32[768]{0:T(1024)}, bf16[4096,768]{1,0:T(8,128)(2,1)}) fusion(f32[4096,768]{1,0:T(8,128)} %get-tuple-element.273, f32[4096,768]{1,0:T(8,128)} %get-tuple-element.281, f32[768]{0:T(1024)S(1)} %convert_element_type.178, bf16[4096,768]{0,1:T(8,128)(2,1)} %all-gather.5.cloned.1.call-done, bf16[768,768]{1,0:T(8,128)(2,1)S(1)} %copy-done.66), kind=kOutput, calls=%fused_computation.61 | convolution fusion | flops 4885314560 | bytes 38934528 | tf_op jit(solution)/shard_map/dot_general | solution.py:27
  526.7 9.8 convolution_convert_fusion
  536.7 108.8 %reduce-scatter.5.cloned.1.call-done = bf16[1024,768]{0,1:T(8,128)(2,1)} async-done(((bf16[4096,768]{0,1:T(8,128)(2,1)}), bf16[1024,768]{0,1:T(8,128)(2,1)}) %reduce-scatter.5.cloned.1.call-update) | async-done | bytes 1572880 | tf_op jit(solution)/shard_map/reduce_scatter | solution.py:125
  645.5 5.4 multiply_reduce_fusion
  662.1 3.0 copy.77
  666.5 33.9 %while.28 = (s32[]{:T(128)}, f32[256,12,64]{0,2,1:T(8,128)}, f32[256,12,64]{0,2,1:T(8,128)S(1)}, bf16[2,512,12,64]{1,3,2,0:T(8,128)(2,1)}, bf16[2,512,12,64]{1,3...) while((s32[]{:T(128)}, f32[256,12,64]{0,2,1:T(8,128)}, ...), condition=%wide.region_18.19_spmd.clone, body=%wide.region_16.18_spmd.clone.sunk | while | flops 1027270656 | bytes 112255784 | solution.py:166
  675.3 4.0 fusion.185
  679.3 4.1 fusion.186
  692.2 4.1 fusion.185
  696.3 4.1 fusion.186
  711.2 36.7 %all-reduce.14.cloned.1.call-done = (bf16[256,768]{0,1:T(8,128)(2,1)}, bf16[256,768]{0,1:T(8,128)(2,1)}) async-done(((bf16[256,768]{0,1:T(8,128)(2,1)}, bf16[256,768]{0,1:T(8,128)(2,1)}), (bf16[256,768]{0,1:T(8,128)(2,1)}, bf16[256,768]{0,1:T(8,128)(2,1)})) %all-reduce.14.cloned.1.call-update) | async-done | bytes 786448 | tf_op jit(solution)/shard_map/psum | solution.py:172
  753.6 2.9 convolution_bitcast_fusion.1
  756.5 2.9 convolution_bitcast_fusion
  763.8 10.1 fusion.92
  773.9 10.2 fusion.91
  786.9 14.2 %psum.163 = f32[768]{0:T(1024)} all-reduce(f32[768]{0:T(1024)S(1)} %copy-done.55), channel_id=1, replica_groups=mesh['dp'=8,'tp'=4] {'dp'}, use_global_device_ids=true, to_apply=%region_40.41 | all-reduce | flops 768 | bytes 6144 | tf_op jit(solution)/shard_map/psum | solution.py:230
  801.4 3.1 fusion.87
  810.8 40.6 %all-reduce = (f32[768]{0:T(1024)}, f32[768]{0:T(1024)}, f32[768]{0:T(1024)}, f32[768]{0:T(1024)}, f32[768]{0:T(1024)}, /*index=5*/f32[768]{0:T(1024)}, f32[768]{0:T(1024)}, f32[768]{0:T(1024)}, f32[768]{0:T(1024)}) all-reduce(f32[768]{0:T(1024)S(1)} %reduce_sum.197, ...), channel_id=1, replica_groups=mesh['dp'=8,'tp'=4] {'dp','tp'}, use_global_device_ids=true, to_apply=%region_23.24 | all-reduce | flops 6912 | bytes 55296 | tf_op jit(solution)/shard_map/psum | solution.py:211
  851.4 157.9 %all-reduce.10.cloned.1.call-done = (f32[768,768]{0,1:T(8,128)}, f32[768,768]{0,1:T(8,128)}, f32[768,768]{0,1:T(8,128)}, f32[768,768]{1,0:T(8,128)}, f32[256,4096]{1,0:T(8,128)}) async-done(((f32[768,768]{0,1:T(8,128)}, f32[768,768]{0,1:T(8,128)}, f32[768,768]{0,1:T(8,128)}, f32[768,768]{1,0:T(8,128)}, f32[256,4096]{1,0:T(8,128)}), (f32[768,768]{0,1:T(8,128)}, f32[768,768]{0,1:T(8,128)}, ...) | async-done | bytes 13631504 | tf_op jit(solution)/shard_map/psum | solution.py:211
  1009.3 3.2 copy.84
  1014.4 3.2 copy.86
  1017.6 82.2 %all-reduce.12.cloned.1.call-done = (f32[768,768]{1,0:T(8,128)}, f32[768,768]{1,0:T(8,128)}) async-done(((f32[768,768]{1,0:T(8,128)}, f32[768,768]{1,0:T(8,128)}), (f32[768,768]{1,0:T(8,128)}, f32[768,768]{1,0:T(8,128)})) %all-reduce.12.cloned.1.call-update) | async-done | bytes 4718608 | tf_op jit(solution)/shard_map/psum | solution.py:230
  (272 shorter events, 119.7 us)
Async XLA Ops:
  7.2 219.6 %copy-start = (bf16[768,768]{1,0:T(8,128)(2,1)S(1)}, bf16[768,768]{1,0:T(8,128)(2,1)}, u32[]{:S(2)}) copy-start(bf16[768,768]{1,0:T(8,128)(2,1)} %param.38) | copy-start | bytes 3538948
  7.2 4.2 copy-start.32
  7.2 219.6 %all-gather.3.cloned.1.call-start = ((), (), s32[]{:S(2)}) async-start(), calls=%async_computation.2 | async-start | bytes 7864320 | tf_op jit(solution)/shard_map/all_gather | solution.py:103
  8.1 8.2 copy-start.46
  17.4 64.2 %copy-start.57 = (bf16[768]{0:T(1024)(128)(2,1)S(1)}, bf16[768]{0:T(1024)(128)(2,1)}, u32[]{:S(2)}) copy-start(bf16[768]{0:T(1024)(128)(2,1)} %param.28) | copy-start | bytes 4612
  102.9 4.4 copy-start.4
  102.9 4.4 copy-start.7
  102.9 4.4 copy-start.15
  102.9 4.4 copy-start.58
  102.9 4.4 copy-start.37
  102.9 4.4 copy-start.67
  112.4 268.0 %reduce-scatter.3.cloned.1.call-start = ((), (), s32[]{:S(2)}) async-start(), calls=%async_computation.3 | async-start | bytes 7864320 | tf_op jit(solution)/shard_map/reduce_scatter | solution.py:107
  112.9 151.3 %copy-start.65 = (bf16[768,768]{1,0:T(8,128)(2,1)S(1)}, bf16[768,768]{1,0:T(8,128)(2,1)}, u32[]{:S(2)}) copy-start(bf16[768,768]{1,0:T(8,128)(2,1)} %param.40) | copy-start | bytes 3538948
  271.3 236.8 %all-gather.5.cloned.1.call-start = ((), (), s32[]{:S(2)}) async-start(), calls=%async_computation.4 | async-start | bytes 7864320 | tf_op jit(solution)/shard_map/all_gather | solution.py:119
  390.0 118.1 %copy-start.66 = (bf16[768,768]{1,0:T(8,128)(2,1)S(1)}, bf16[768,768]{1,0:T(8,128)(2,1)}, u32[]{:S(2)}) copy-start(bf16[768,768]{1,0:T(8,128)(2,1)} %param.40) | copy-start | bytes 3538948
  392.1 253.5 %reduce-scatter.5.cloned.1.call-start = ((), (), s32[]{:S(2)}) async-start(), calls=%async_computation.5 | async-start | bytes 7864320 | tf_op jit(solution)/shard_map/reduce_scatter | solution.py:125
  536.5 211.4 %all-reduce.14.cloned.1.call-start = ((), (), s32[]{:S(2)}) async-start(), calls=%async_computation.8 | async-start | bytes 1572864 | tf_op jit(solution)/shard_map/psum | solution.py:172
  536.7 114.3 %copy-start.49 = (f32[1024]{0:T(1024)S(1)}, f32[1024]{0:T(1024)}, u32[]{:S(2)}) copy-start(f32[1024]{0:T(1024)} %copy-done.48) | copy-start | bytes 12292
  645.5 5.5 copy-start.10
  645.5 5.5 copy-start.14
  645.5 5.6 copy-start.26
  662.1 4.4 copy-start.5
  662.1 4.4 copy-start.8
  662.1 4.4 copy-start.16
  662.1 4.4 copy-start.44
  692.2 4.2 copy-start.12
  703.1 306.1 %all-reduce.10.cloned.1.call-start = ((), (), s32[]{:S(2)}) async-start(), calls=%async_computation.6 | async-start | bytes 27262976 | tf_op jit(solution)/shard_map/psum | solution.py:211
  708.4 39.5 %copy-start.47 = (f32[1024]{0:T(1024)S(1)}, f32[1024]{0:T(1024)}, u32[]{:S(2)}) copy-start(f32[1024]{0:T(1024)} %copy-done.46) | copy-start | bytes 12292
  749.8 6.6 copy-start.72
  763.5 336.4 %all-reduce.12.cloned.1.call-start = ((), (), s32[]{:S(2)}) async-start(), calls=%async_computation.7 | async-start | bytes 9437184 | tf_op jit(solution)/shard_map/psum | solution.py:230
  784.2 17.3 %copy-start.70 = (bf16[768,768]{1,0:T(8,128)(2,1)S(1)}, bf16[768,768]{1,0:T(8,128)(2,1)}, u32[]{:S(2)}) copy-start(bf16[768,768]{1,0:T(8,128)(2,1)} %param.29) | copy-start | bytes 3538948
  1014.4 85.4 %copy-start.28 = (f32[768,768]{1,0:T(8,128)S(1)}, f32[768,768]{1,0:T(8,128)}, u32[]{:S(2)}) copy-start(f32[768,768]{1,0:T(8,128)} %get-tuple-element.448) | copy-start | bytes 7077892
  (58 other events, 132.1 us)
Sparse Core Ops, SparseCore 0:
  112.5 114.2 all-gather.2
  271.4 108.9 reduce-scatter.2
  392.2 115.8 all-gather.4
  536.6 108.9 reduce-scatter.4
  703.3 44.5 all-reduce.13
  763.6 245.6 all-reduce.9
  1013.0 86.8 all-reduce.11
where the time goes:
time: 1120 us
  waiting for transfers between devices  722 us (64%)
  matrix products  160 us (14%)
  blocking collectives  117 us (10%)
  local copies, waits for them, and re-layouts  70.9 us (6%)
  other arithmetic  28.8 us (3%)
  between operations  16.3 us (1%)
    psum x1, waiting for transfers between devices, on_device(): lax.psum((g_w_query, g_w_key, g_w_value, g_w_out, g_seq_proj, g_b_query,...  158 us
    all_gather x1, waiting for transfers between devices, on_device(): d_rows = lax.all_gather(d_branch, 'tp', axis=0, tiled=True)  116 us
    all_gather x1, waiting for transfers between devices, on_device(): ffn_rows = lax.all_gather(normed_b, 'tp', axis=0, tiled=True)  114 us
    reduce_scatter x1, waiting for transfers between devices, on_device(): lax.psum_scatter(times_transpose(d_pre, w_up).astype(jnp.bfloat16), 'tp',...  109 us
    reduce_scatter x1, waiting for transfers between devices, on_device(): lax.psum_scatter(matmul(hidden_b, w_down).astype(jnp.bfloat16), 'tp', sca...  107 us
    psum x1, waiting for transfers between devices, on_device(): g_w_up, g_b_up, g_w_down = lax.psum((g_w_up, g_b_up, g_w_down), 'dp')  82.2 us
    psum x1, blocking collectives, on_device(): proj_keys, proj_values = lax.psum((share_keys, share_values), 'tp')  62.3 us
    dot_general x8, matrix products, matmul(): return jnp.dot(left, right, preferred_element_type=jnp.float32)  53 us
  transfers between devices with their start and end apart: 7, of which 7 were waited for; matrix products, arithmetic and copies ran while one was open for 4% of the time, Pallas kernels for 0%

commit v1 on v0

v1 whole, which is shorter than its diff:
```python
import jax
import jax.numpy as jnp
from jax import lax
from jax.sharding import PartitionSpec as P

HEADS = 12
HEAD = 64
BF = jnp.bfloat16
F32 = jnp.float32


def layer_norm(hidden, gain, shift):
    center = hidden - jnp.mean(hidden, axis=-1, keepdims=True)
    spread = jnp.mean(center * center, axis=-1, keepdims=True)
    return center * lax.rsqrt(spread + 1e-05) * gain + shift


def dot(left, right, left_dim, right_dim):
    return lax.dot_general(
        left, right, (((left_dim,), (right_dim,)), ((), ())), preferred_element_type=F32
    )


def exact_gelu(value):
    return jax.nn.gelu(value, approximate=False)


def on_device(
    layer_in,
    out_grad,
    lengths,
    w_query,
    b_query,
    w_key,
    b_key,
    w_value,
    b_value,
    w_out,
    b_out,
    seq_proj,
    attn_gain,
    attn_shift,
    w_up,
    b_up,
    w_down,
    b_down,
    ffn_gain,
    ffn_shift,
):
    row_count, width = layer_in.shape
    slots = seq_proj.shape[0]
    tp_index = lax.axis_index("tp")
    own_first = tp_index * row_count
    own_positions = own_first + jnp.arange(row_count, dtype=jnp.int32)
    own_live = (own_positions < lengths[0]).astype(F32)
    own_cols = lax.dynamic_slice_in_dim(seq_proj, own_first, row_count, 1)
    own_proj = (own_cols.astype(F32) * own_live[None, :]).astype(BF)
    total_rows = seq_proj.shape[1]
    live = (jnp.arange(total_rows, dtype=jnp.int32) < lengths[0]).astype(F32)
    slot_sum = jnp.sum(seq_proj.astype(F32) * live[None, :], axis=1)[:, None]

    folded = lax.psum(dot(own_proj, layer_in, 1, 0), "tp")
    up_all = lax.all_gather(w_up.T, "tp", axis=0, tiled=True)
    down_all = lax.all_gather(w_down, "tp", axis=0, tiled=True)
    bias_up = lax.all_gather(b_up, "tp", axis=0, tiled=True)
    folded_b = folded.astype(BF)
    folded_low = (folded - folded_b.astype(F32)).astype(BF)

    def project(weight, bias):
        full = dot(folded_b, weight, 1, 0) + dot(folded_low, weight, 1, 0)
        return (full + slot_sum * bias.astype(F32)[None, :]).astype(BF)

    proj_keys = project(w_key, b_key)
    proj_values = project(w_value, b_value)
    queries = (dot(layer_in, w_query, 1, 0) + b_query.astype(F32)).astype(BF)
    mixed_parts, prob_parts = [], []
    for h in range(HEADS):
        cols = slice(h * HEAD, (h + 1) * HEAD)
        logits = dot(queries[:, cols], proj_keys[:, cols], 1, 1) * 0.125
        peak = jnp.max(logits, axis=-1, keepdims=True)
        raised = jnp.exp(logits - peak)
        probs = raised / jnp.sum(raised, axis=-1, keepdims=True)
        prob_parts.append(probs)
        mixed_parts.append(dot(probs.astype(BF), proj_values[:, cols], 1, 0).astype(BF))
    mixed = jnp.concatenate(mixed_parts, axis=1)
    attn = dot(mixed, w_out, 1, 0) + b_out.astype(F32)
    res_one = layer_in.astype(F32) + attn
    normed, norm_one_pull = jax.vjp(
        layer_norm, res_one, attn_gain.astype(F32), attn_shift.astype(F32)
    )
    normed_b = normed.astype(BF)
    pre_act = dot(normed_b, up_all, 1, 1) + bias_up.astype(F32)
    hidden_act, gelu_pull = jax.vjp(exact_gelu, pre_act)
    hidden_b = hidden_act.astype(BF)
    branch = dot(hidden_b, down_all, 1, 0) + b_down.astype(F32)
    res_two = normed + branch
    final, norm_two_pull = jax.vjp(
        layer_norm, res_two, ffn_gain.astype(F32), ffn_shift.astype(F32)
    )
    layer_out = final.astype(BF)
    d_res_two, g_ffn_gain, g_ffn_shift = norm_two_pull(out_grad.astype(F32))
    d_branch = d_res_two.astype(BF)
    g_b_down = jnp.sum(d_branch.astype(F32), axis=0)
    g_w_down = dot(hidden_b, d_branch, 0, 0).astype(BF)
    (d_hidden,) = gelu_pull(dot(d_branch, down_all, 1, 1))
    d_pre = d_hidden.astype(BF)
    g_b_up = jnp.sum(d_pre.astype(F32), axis=0)
    g_w_up = dot(d_pre, normed_b, 0, 0).astype(BF)
    d_normed = d_res_two + dot(d_pre, up_all, 1, 0)
    d_res_one, g_attn_gain, g_attn_shift = norm_one_pull(d_normed)
    d_attn = d_res_one.astype(BF)
    g_b_out = jnp.sum(d_attn.astype(F32), axis=0)
    g_w_out = dot(mixed, d_attn, 0, 0).astype(BF)
    d_mixed = dot(d_attn, w_out, 1, 1).astype(BF)
    d_query_parts, d_key_parts, d_value_parts = [], [], []
    for h in range(HEADS):
        cols = slice(h * HEAD, (h + 1) * HEAD)
        probs = prob_parts[h]
        d_probs = dot(d_mixed[:, cols], proj_values[:, cols], 1, 1)
        d_logits = (probs * (d_probs - jnp.sum(probs * d_probs, axis=-1, keepdims=True))).astype(BF)
        d_query_parts.append((dot(d_logits, proj_keys[:, cols], 1, 0) * 0.125).astype(BF))
        d_key_parts.append((dot(queries[:, cols], d_logits, 0, 0) * 0.125).astype(BF))
        d_value_parts.append(dot(d_mixed[:, cols], probs.astype(BF), 0, 0).astype(BF))
    d_queries = jnp.concatenate(d_query_parts, axis=1)
    part_keys = jnp.concatenate(d_key_parts, axis=0)
    part_values = jnp.concatenate(d_value_parts, axis=0)
    own_dk = lax.psum_scatter(part_keys, "tp", scatter_dimension=0, tiled=True)
    own_dv = lax.psum_scatter(part_values, "tp", scatter_dimension=0, tiled=True)
    d_proj_keys = lax.all_gather(own_dk, "tp", axis=0, tiled=True)
    d_proj_values = lax.all_gather(own_dv, "tp", axis=0, tiled=True)
    g_w_key = dot(own_dk, folded_b, 1, 0)
    g_w_value = dot(own_dv, folded_b, 1, 0)
    g_b_key = dot(d_proj_keys.astype(F32), slot_sum, 1, 0)[:, 0]
    g_b_value = dot(d_proj_values.astype(F32), slot_sum, 1, 0)[:, 0]
    back = dot(d_proj_keys, w_key, 0, 1) + dot(d_proj_values, w_value, 0, 1)
    back_b = back.astype(BF)
    bias_back = dot(d_proj_keys.astype(F32), b_key.astype(F32)[:, None], 0, 0) + dot(
        d_proj_values.astype(F32), b_value.astype(F32)[:, None], 0, 0
    )
    own_proj_grad = (dot(back_b, layer_in, 1, 1) + bias_back) * own_live[None, :]
    g_w_query = dot(layer_in, d_queries, 0, 0)
    g_b_query = jnp.sum(d_queries.astype(F32), axis=0)
    grad_in = (
        d_res_one + dot(d_queries, w_query, 1, 1) + dot(own_proj, back_b, 0, 0)
    ).astype(BF)
    g_w_query, g_w_out = lax.psum((g_w_query.astype(BF), g_w_out), ("dp", "tp"))
    g_w_key, g_w_value, own_proj_grad = lax.psum(
        (g_w_key.astype(BF), g_w_value.astype(BF), own_proj_grad.astype(BF)), "dp"
    )
    g_w_key = lax.all_gather(g_w_key, "tp", axis=0, tiled=True).T
    g_w_value = lax.all_gather(g_w_value, "tp", axis=0, tiled=True).T
    g_seq_proj = lax.all_gather(own_proj_grad, "tp", axis=1, tiled=True)
    g_b_key, g_b_value = g_b_key / lax.axis_size("tp"), g_b_value / lax.axis_size("tp")
    (
        g_b_query,
        g_b_key,
        g_b_value,
        g_b_out,
        g_attn_gain,
        g_attn_shift,
        g_ffn_gain,
        g_ffn_shift,
        g_b_down,
        g_b_up,
    ) = lax.psum(
        (
            g_b_query,
            g_b_key,
            g_b_value,
            g_b_out,
            g_attn_gain,
            g_attn_shift,
            g_ffn_gain,
            g_ffn_shift,
            g_b_down,
            g_b_up,
        ),
        ("dp", "tp"),
    )
    own_ff = b_up.shape[0]
    g_b_up = lax.dynamic_slice_in_dim(g_b_up, tp_index * own_ff, own_ff, 0)
    g_w_up, g_w_down = (
        lax.psum_scatter(g_w_up, "tp", scatter_dimension=0, tiled=True),
        lax.psum_scatter(g_w_down, "tp", scatter_dimension=0, tiled=True),
    )
    g_w_up, g_w_down = lax.psum((g_w_up, g_w_down), "dp")
    up = lambda v: v.astype(F32)
    return (
        layer_out,
        grad_in,
        up(g_w_query),
        g_b_query,
        up(g_w_key),
        g_b_key,
        up(g_w_value),
        g_b_value,
        up(g_w_out),
        g_b_out,
        up(g_seq_proj),
        g_attn_gain,
        g_attn_shift,
        up(g_w_up.T),
        g_b_up,
        up(g_w_down),
        g_b_down,
        g_ffn_gain,
        g_ffn_shift,
    )


def solution(mesh):
    in_specs = (
        P(("dp", "tp"), None),
        P(("dp", "tp"), None),
        P("dp"),
        *([P()] * 11),
        P(None, "tp"),
        P("tp"),
        P("tp", None),
        P(),
        P(),
        P(),
    )
    out_specs = (
        P(("dp", "tp"), None),
        P(("dp", "tp"), None),
        *([P()] * 11),
        P(None, "tp"),
        P("tp"),
        P("tp", None),
        P(),
        P(),
        P(),
    )
    return jax.shard_map(
        on_device, mesh=mesh, in_specs=in_specs, out_specs=out_specs, check_vma=False
    )
```

time: 1120 us -> 896 us (0.80)
  waiting for transfers between devices: 722 us -> 512 us
  local copies, waits for them, and re-layouts: 70.9 us -> 26.5 us
  matrix products: 160 us -> 197 us
  blocking collectives: 117 us -> 97.7 us
    psum x3, waiting for transfers between devices: 277 us -> 175 us  [the longest x1 88.2 us: on_device(): g_w_query, g_w_out = lax.psum((g_w_query.astype(BF), g_w_out), ('dp', 'tp'))]
    reduce_scatter x2 -> x4, waiting for transfers between devices: 215 us -> 125 us  [the longest x1 88 us: on_device(): lax.psum_scatter(g_w_down, 'tp', scatter_dimension=0, tiled=True)]
    psum x3 -> x1, blocking collectives: 117 us -> 41.2 us  [on_device(): lax.psum((g_b_query, g_b_key, g_b_value, g_b_out, g_attn_gain, g_attn_shi...]
    all_gather x0 -> x3, blocking collectives: none -> 56.5 us  [the longest x1 21 us: on_device(): d_proj_keys = lax.all_gather(own_dk, 'tp', axis=0, tiled=True)]
    dot_general x38 -> x99, matrix products: 160 us -> 197 us  [dot(): lax.dot_general(left, right, (((left_dim,), (right_dim,)), ((), ())), pre...]
    all_gather x2 -> x5, waiting for transfers between devices: 230 us -> 210 us  [the longest x1 65.8 us: on_device(): up_all = lax.all_gather(w_up.T, 'tp', axis=0, tiled=True)]
    unnamed x152 -> x329, local copies, waits for them, and re-layouts: 43 us -> 25.9 us
    while x31 -> x0, local copies, waits for them, and re-layouts: 13.1 us -> none
  transfers between devices with their start and end apart: 7 -> 12, of which waited for: 7 -> 10; matrix products, arithmetic and copies ran while one was open for 4% -> 18% of each run, Pallas kernels for 0% -> 0%
where the time goes in v1:
time: 896 us; the launch traced here: 884 us
  waiting for transfers between devices  512 us (57%)
  matrix products  197 us (22%)
  blocking collectives  97.7 us (11%)
  other arithmetic  33 us (4%)
  local copies, waits for them, and re-layouts  26.5 us (3%)
  between operations  17 us (2%)
    dot_general x99, matrix products, dot(): lax.dot_general(left, right, (((left_dim,), (right_dim,)), ((), ())), pre...  197 us
    psum x1, waiting for transfers between devices, on_device(): g_w_query, g_w_out = lax.psum((g_w_query.astype(BF), g_w_out), ('dp', 'tp'))  88.2 us
    reduce_scatter x1, waiting for transfers between devices, on_device(): lax.psum_scatter(g_w_down, 'tp', scatter_dimension=0, tiled=True)  88 us
    psum x1, waiting for transfers between devices, on_device(): g_w_up, g_w_down = lax.psum((g_w_up, g_w_down), 'dp')  66.4 us
    all_gather x1, waiting for transfers between devices, on_device(): up_all = lax.all_gather(w_up.T, 'tp', axis=0, tiled=True)  65.8 us
    all_gather x1, waiting for transfers between devices, on_device(): down_all = lax.all_gather(w_down, 'tp', axis=0, tiled=True)  51.7 us
    all_gather x1, waiting for transfers between devices, on_device(): g_seq_proj = lax.all_gather(own_proj_grad, 'tp', axis=1, tiled=True)  43.2 us
    psum x1, blocking collectives, on_device(): lax.psum((g_b_query, g_b_key, g_b_value, g_b_out, g_attn_gain, g_attn_shi...  41.2 us
  transfers between devices with their start and end apart: 12, of which 10 were waited for; matrix products, arithmetic and copies ran while one was open for 18% of the time, Pallas kernels for 0%

profile of v1, /device:TPU:0, one launch (start us, length us, event | category | flops | bytes accessed | tf_op | source)
XLA Modules:
  0.0 884.2 jit_solution(18094855990932414574)
XLA Ops:
  8.1 3.0 fusion.115
  14.4 2.1 multiply_reduce_fusion
  16.7 15.0 %all-gather = bf16[4,1,768]{2,1,0:T(2,128)(2,1)S(1)} all-gather(bf16[1,1,768]{2,1,0:T(2,128)(2,1)S(1)} %reshape.172), channel_id=1, replica_groups=mesh['dp'=8,'tp'=4] {'tp'}, dimensions={0}, use_global_device_ids=true | all-gather | bytes 7680 | tf_op jit(solution)/shard_map/all_gather | solution.py:65
  33.5 4.3 add_convert_fusion.3
  37.8 20.0 %all-reduce.7.cloned.1.call-done = f32[256,768]{1,0:T(8,128)} async-done(((f32[256,768]{1,0:T(8,128)}), f32[256,768]{1,0:T(8,128)}) %all-reduce.7.cloned.1.call-update) | async-done | bytes 786448 | tf_op jit(solution)/shard_map/psum | solution.py:62
  60.0 2.2 fusion.16
  82.4 65.8 %all-gather.7.cloned.1.call-done = bf16[3072,768]{0,1:T(8,128)(2,1)} async-done(((bf16[768,768]{0,1:T(8,128)(2,1)}), bf16[3072,768]{0,1:T(8,128)(2,1)}) %all-gather.7.cloned.1.call-update) | async-done | bytes 4718608 | tf_op jit(solution)/shard_map/all_gather | solution.py:63
  148.2 37.8 %multiply_convert_fusion = (bf16[1024,3072]{1,0:T(8,128)(2,1)}, f32[1024,3072]{1,0:T(8,128)}, f32[1024,3072]{1,0:T(8,128)}) fusion(f32[3072]{0:T(1024)S(1)} %bitcast.88, bf16[3072,768]{0,1:T(8,128)(2,1)} %all-gather.7.cloned.1.call-done, f32[1024,768]{0,1:T(8,128)} %copy-done.5, f32[768]{0:T(1024)S(1)} %convert_element_type.445, ...), kind=kOutput, calls=%fused_computation.4 | convolution fusion | flops 5043388416 | bytes 39348224 | tf_op jit(solution)/shard_map/dot_general | solution.py:19
  186.0 51.7 %all-gather.9.cloned.1.call-done = bf16[3072,768]{1,0:T(8,128)(2,1)} async-done(((bf16[768,768]{1,0:T(8,128)(2,1)}), bf16[3072,768]{1,0:T(8,128)(2,1)}) %all-gather.9.cloned.1.call-update) | async-done | bytes 4718608 | tf_op jit(solution)/shard_map/all_gather | solution.py:64
  237.7 9.6 %fusion.305 = (f32[1024]{0:T(1024)S(1)}, f32[1024,768]{0,1:T(8,128)S(1)}) fusion(f32[768]{0:T(1024)S(1)} %convert_element_type.449, bf16[1024,3072]{1,0:T(8,128)(2,1)} %get-tuple-element.88, bf16[3072,768]{1,0:T(8,128)(2,1)} %all-gather.9.cloned.1.call-done, f32[768]{0:T(1024)S(1)} %convert_element_type.445, f32[768]{0:T(1024)S(1)} %convert_element_type.444, ...), kind=kOutput, calls=%fused_computation.437 | convolution fusion | flops 4837342208 | bytes 17323008 | tf_op jit(solution)/shard_map/dot_general | solution.py:19
  250.6 3.0 convert_reduce_fusion.2
  253.6 19.1 %convert_reduce_fusion = (f32[3072]{0:T(1024)}, bf16[1024,3072]{1,0:T(8,128)(2,1)}) fusion(f32[1024,3072]{1,0:T(8,128)} %get-tuple-element.89, bf16[1024,768]{0,1:T(8,128)(2,1)} %get-tuple-element.83, bf16[3072,768]{1,0:T(8,128)(2,1)} %all-gather.9.cloned.1.call-done, f32[1024,3072]{1,0:T(8,128)} %get-tuple-element.119, f32[3072]{0:T(1024)S(1)} %bitcast.89), kind=kOutput, calls=%fused_computation.2 | convolution fusion | flops 4885312512 | bytes 37773312 | tf_op jit(solution)/shard_map/dot_general | solution.py:19
  272.7 11.6 %multiply_reduce_fusion.1 = (f32[768]{0:T(1024)}, f32[1024]{0:T(1024)S(1)}, f32[768]{0:T(1024)}, f32[1024,768]{0,1:T(8,128)S(1)}) fusion(f32[1024,768]{0,1:T(8,128)} %copy-done.5, f32[1024]{0:T(1024)S(1)} %fusion.250, f32[1024]{0:T(1024)S(1)} %broadcast_multiply_fusion.3, f32[768]{0:T(1024)S(1)} %convert_element_type.444, ...), kind=kOutput, calls=%fused_computation.31 | convolution fusion | flops 4845204480 | bytes 22061056 | tf_op jit(solution)/shard_map/dot_general | solution.py:19
  335.7 10.2 %convolution_convert_fusion.1 = bf16[3072,768]{1,0:T(8,128)(2,1)} fusion(bf16[1024,3072]{1,0:T(8,128)(2,1)} %get-tuple-element.148, f32[1024,768]{0,1:T(8,128)} %copy-done.5, f32[768]{0:T(1024)S(1)} %convert_element_type.445, f32[768]{0:T(1024)S(1)} %convert_element_type.444, f32[1024]{0:T(1024)S(1)} %fusion.250, f32[1024]{0:T(1024)S(1)} %broadcast_multiply_fusion.3), kind=kOutput, calls=%fused_computation.19 | convolution fusion | flops 4838129664 | bytes 14170112 | tf_op jit(solution)/shard_map/dot_general | solution.py:19
  347.3 9.8 %convolution_convert_fusion = bf16[3072,768]{1,0:T(8,128)(2,1)} fusion(bf16[1024,3072]{1,0:T(8,128)(2,1)} %get-tuple-element.88, bf16[1024,768]{0,1:T(8,128)(2,1)S(1)} %copy-done.78), kind=kOutput, calls=%fused_computation.18 | convolution fusion | flops 4834197504 | bytes 12582912 | tf_op jit(solution)/shard_map/dot_general | solution.py:19
  368.0 20.4 %all_gather.28 = bf16[768,256]{1,0:T(8,128)(2,1)} all-gather(bf16[192,256]{1,0:T(8,128)(2,1)} %reduce-scatter.7.cloned.1.call-done), channel_id=1, replica_groups=mesh['dp'=8,'tp'=4] {'tp'}, dimensions={0}, use_global_device_ids=true | all-gather | bytes 491520 | tf_op jit(solution)/shard_map/all_gather | solution.py:130
  388.5 21.0 %all_gather.27 = bf16[768,256]{1,0:T(8,128)(2,1)S(1)} all-gather(bf16[192,256]{1,0:T(8,128)(2,1)} %reduce-scatter.5.cloned.1.call-done), channel_id=1, replica_groups=mesh['dp'=8,'tp'=4] {'tp'}, dimensions={0}, use_global_device_ids=true | all-gather | bytes 491520 | tf_op jit(solution)/shard_map/all_gather | solution.py:129
  417.4 36.7 %reduce-scatter.9.cloned.1.call-done = bf16[768,768]{1,0:T(8,128)(2,1)} async-done(((bf16[3072,768]{1,0:T(8,128)(2,1)}), bf16[768,768]{1,0:T(8,128)(2,1)}) %reduce-scatter.9.cloned.1.call-update) | async-done | bytes 1179664 | tf_op jit(solution)/shard_map/reduce_scatter | solution.py:183
  454.2 88.0 %reduce-scatter.11.cloned.1.call-done = bf16[768,768]{1,0:T(8,128)(2,1)} async-done(((bf16[3072,768]{1,0:T(8,128)(2,1)}), bf16[768,768]{1,0:T(8,128)(2,1)}) %reduce-scatter.11.cloned.1.call-update) | async-done | bytes 1179664 | tf_op jit(solution)/shard_map/reduce_scatter | solution.py:184
  547.1 4.4 convolution_convert_fusion.3
  551.5 3.8 fusion.11
  555.4 66.4 %all-reduce.11.cloned.1.call-done = (bf16[768,768]{0,1:T(8,128)(2,1)}, bf16[192,768]{1,0:T(8,128)(2,1)}, bf16[192,768]{1,0:T(8,128)(2,1)}, bf16[256,1024]{1,0:T(8,128)(2,1)}, bf16[768,768]{1,0:T(8,128)(2,1)}) async-done(((bf16[768,768]{0,1:T(8,128)(2,1)}, bf16[192,768]{1,0:T(8,128)(2,1)}, bf16[192,768]{1,0:T(8,128)(2,1)}, bf16[256,1024]{1,0:T(8,128)(2,1)}, bf16[768,768]{1,0:T(8,128)(2,1)}), ...) | async-done | bytes 3473424 | tf_op jit(solution)/shard_map/psum | solution.py:186
  624.8 2.3 convert_reduce_fusion.4
  627.1 3.3 fusion.309
  634.3 41.2 %all-reduce = (f32[768]{0:T(1024)}, f32[768]{0:T(1024)}, f32[768]{0:T(1024)}, f32[768]{0:T(1024)}, f32[768]{0:T(1024)}, /*index=5*/f32[768]{0:T(1024)}, f32[3072...) all-reduce(f32[768]{0:T(1024)} %convert_reduce_fusion.4, ...), channel_id=1, replica_groups=mesh['dp'=8,'tp'=4] {'dp','tp'}, use_global_device_ids=true, to_apply=%region_50.0 | all-reduce | flops 9984 | bytes 79872 | tf_op jit(solution)/shard_map/psum | solution.py:165
  676.2 88.2 %all-reduce.9.cloned.1.call-done = (bf16[768,768]{0,1:T(8,128)(2,1)}, bf16[768,768]{1,0:T(8,128)(2,1)}) async-done(((bf16[768,768]{0,1:T(8,128)(2,1)}, bf16[768,768]{1,0:T(8,128)(2,1)}), (bf16[768,768]{0,1:T(8,128)(2,1)}, bf16[768,768]{1,0:T(8,128)(2,1)})) %all-reduce.9.cloned.1.call-update) | async-done | bytes 2359312 | tf_op jit(solution)/shard_map/psum | solution.py:146
  764.4 2.9 convert_element_type.519
  767.3 2.8 copy.57
  773.5 21.7 %all-gather.11.cloned.1.call-done = bf16[768,768]{1,0:T(8,128)(2,1)} async-done(((bf16[192,768]{1,0:T(8,128)(2,1)}), bf16[768,768]{1,0:T(8,128)(2,1)}) %all-gather.11.cloned.1.call-update) | async-done | bytes 1179664 | tf_op jit(solution)/shard_map/all_gather | solution.py:150
  798.6 27.8 %all-gather.13.cloned.1.call-done = bf16[768,768]{1,0:T(8,128)(2,1)} async-done(((bf16[192,768]{1,0:T(8,128)(2,1)}), bf16[768,768]{1,0:T(8,128)(2,1)}) %all-gather.13.cloned.1.call-update) | async-done | bytes 1179664 | tf_op jit(solution)/shard_map/all_gather | solution.py:151
  829.9 43.2 %all-gather.15.cloned.1.call-done = bf16[256,4096]{1,0:T(8,128)(2,1)} async-done(((bf16[256,1024]{1,0:T(8,128)(2,1)}), bf16[256,4096]{1,0:T(8,128)(2,1)}) %all-gather.15.cloned.1.call-update) | async-done | bytes 2097168 | tf_op jit(solution)/shard_map/all_gather | solution.py:152
  873.1 4.1 convert_element_type.522
  (496 shorter events, 123.2 us)
Async XLA Ops:
  7.2 70.5 %copy-start = (bf16[768,768]{1,0:T(8,128)(2,1)S(1)}, bf16[768,768]{1,0:T(8,128)(2,1)}, u32[]{:S(2)}) copy-start(bf16[768,768]{1,0:T(8,128)(2,1)} %param.29) | copy-start | bytes 3538948
  7.2 50.7 %all-reduce.7.cloned.1.call-start = ((), (), s32[]{:S(2)}) async-start(), calls=%async_computation.4 | async-start | bytes 1572864 | tf_op jit(solution)/shard_map/psum | solution.py:62
  11.2 137.1 %all-gather.7.cloned.1.call-start = ((), (), s32[]{:S(2)}) async-start(), calls=%async_computation.5 | async-start | bytes 5898240 | tf_op jit(solution)/shard_map/all_gather | solution.py:63
  12.0 19.7 %copy-start.154 = (bf16[768]{0:T(1024)(128)(2,1)S(1)}, bf16[768]{0:T(1024)(128)(2,1)}, u32[]{:S(2)}) copy-start(bf16[768]{0:T(1024)(128)(2,1)} %param.37) | copy-start | bytes 4612
  12.0 225.7 %all-gather.9.cloned.1.call-start = ((), (), s32[]{:S(2)}) async-start(), calls=%async_computation.6 | async-start | bytes 5898240 | tf_op jit(solution)/shard_map/all_gather | solution.py:64
  12.7 355.3 %reduce-scatter.7.cloned.1.call-start = ((), (), s32[]{:S(2)}) async-start(), calls=%async_computation.8 | async-start | bytes 491520 | tf_op jit(solution)/shard_map/reduce_scatter | solution.py:128
  14.4 19.0 %copy-start.155 = (bf16[768]{0:T(1024)(128)(2,1)S(1)}, bf16[768]{0:T(1024)(128)(2,1)}, u32[]{:S(2)}) copy-start(bf16[768]{0:T(1024)(128)(2,1)} %param.38) | copy-start | bytes 4612
  14.4 19.1 %copy-start.156 = (bf16[768]{0:T(1024)(128)(2,1)S(1)}, bf16[768]{0:T(1024)(128)(2,1)}, u32[]{:S(2)}) copy-start(bf16[768]{0:T(1024)(128)(2,1)} %param.39) | copy-start | bytes 4612
  16.6 52.0 %copy-start.119 = (f32[256]{0:T(256)}, f32[256]{0:T(256)S(1)}, u32[]{:S(2)}) copy-start(f32[256]{0:T(256)S(1)} %multiply_reduce_fusion) | copy-start | bytes 3076
  65.7 10.1 %copy-start.14 = (f32[1024,256]{0,1:T(8,128)}, f32[1024,256]{0,1:T(8,128)S(1)}, u32[]{:S(2)}) copy-start(f32[1024,256]{0,1:T(8,128)S(1)} %get-tuple-element.112) | copy-start | bytes 3145732
  65.7 10.1 %copy-start.99 = (f32[1024]{0:T(1024)}, f32[1024]{0:T(1024)S(1)}, u32[]{:S(2)}) copy-start(f32[1024]{0:T(1024)S(1)} %get-tuple-element.111) | copy-start | bytes 12292
  66.0 10.6 %copy-start.12 = (f32[1024,256]{0,1:T(8,128)}, f32[1024,256]{0,1:T(8,128)S(1)}, u32[]{:S(2)}) copy-start(f32[1024,256]{0,1:T(8,128)S(1)} %get-tuple-element.114) | copy-start | bytes 3145732
  66.0 10.6 %copy-start.97 = (f32[1024]{0:T(1024)}, f32[1024]{0:T(1024)S(1)}, u32[]{:S(2)}) copy-start(f32[1024]{0:T(1024)S(1)} %get-tuple-element.113) | copy-start | bytes 12292
  66.3 11.0 %copy-start.10 = (f32[1024,256]{0,1:T(8,128)}, f32[1024,256]{0,1:T(8,128)S(1)}, u32[]{:S(2)}) copy-start(f32[1024,256]{0,1:T(8,128)S(1)} %get-tuple-element.116) | copy-start | bytes 3145732
  66.4 11.0 %copy-start.95 = (f32[1024]{0:T(1024)}, f32[1024]{0:T(1024)S(1)}, u32[]{:S(2)}) copy-start(f32[1024]{0:T(1024)S(1)} %get-tuple-element.115) | copy-start | bytes 12292
  272.7 11.6 %copy-start.6 = (f32[1024,768]{0,1:T(8,128)S(1)}, f32[1024,768]{0,1:T(8,128)}, u32[]{:S(2)}) copy-start(f32[1024,768]{0,1:T(8,128)} %copy-done.5) | copy-start | bytes 9437188
  315.6 72.9 %reduce-scatter.5.cloned.1.call-start = ((), (), s32[]{:S(2)}) async-start(), calls=%async_computation.7 | async-start | bytes 491520 | tf_op jit(solution)/shard_map/reduce_scatter | solution.py:127
  335.6 118.6 %reduce-scatter.9.cloned.1.call-start = ((), (), s32[]{:S(2)}) async-start(), calls=%async_computation.12 | async-start | bytes 5898240 | tf_op jit(solution)/shard_map/reduce_scatter | solution.py:183
  345.9 196.3 %reduce-scatter.11.cloned.1.call-start = ((), (), s32[]{:S(2)}) async-start(), calls=%async_computation.13 | async-start | bytes 5898240 | tf_op jit(solution)/shard_map/reduce_scatter | solution.py:184
  357.2 264.7 %all-reduce.11.cloned.1.call-start = ((), (), s32[]{:S(2)}) async-start(), calls=%async_computation.15 | async-start | bytes 6946816 | tf_op jit(solution)/shard_map/psum | solution.py:186
  361.4 49.7 %copy-start.4 = (f32[256,768]{1,0:T(8,128)S(1)}, f32[256,768]{1,0:T(8,128)}, u32[]{:S(2)}) copy-start(f32[256,768]{1,0:T(8,128)} %all-reduce.7.cloned.1.call-done) | copy-start | bytes 2359300
  365.2 49.7 %copy-start.7 = (bf16[768,768]{1,0:T(8,128)(2,1)S(1)}, bf16[768,768]{1,0:T(8,128)(2,1)}, u32[]{:S(2)}) copy-start(bf16[768,768]{1,0:T(8,128)(2,1)} %param.25) | copy-start | bytes 3538948
  388.5 26.9 %copy-start.9 = (bf16[768,768]{1,0:T(8,128)(2,1)S(1)}, bf16[768,768]{1,0:T(8,128)(2,1)}, u32[]{:S(2)}) copy-start(bf16[768,768]{1,0:T(8,128)(2,1)} %param.27) | copy-start | bytes 3538948
  388.5 26.9 %copy-start.53 = (bf16[768,256]{1,0:T(8,128)(2,1)S(1)}, bf16[768,256]{1,0:T(8,128)(2,1)}, u32[]{:S(2)}) copy-start(bf16[768,256]{1,0:T(8,128)(2,1)} %all_gather.28) | copy-start | bytes 1179652
  416.0 126.3 %copy-start.56 = (bf16[1024,256]{0,1:T(8,128)(2,1)S(1)}, bf16[1024,256]{0,1:T(8,128)(2,1)}, u32[]{:S(2)}) copy-start(bf16[1024,256]{0,1:T(8,128)(2,1)} %copy-done.55) | copy-start | bytes 1572868
  416.0 127.2 %copy-start.58 = (bf16[1024,256]{0,1:T(8,128)(2,1)S(1)}, bf16[1024,256]{0,1:T(8,128)(2,1)}, u32[]{:S(2)}) copy-start(bf16[1024,256]{0,1:T(8,128)(2,1)} %copy-done.57) | copy-start | bytes 1572868
  417.4 126.7 %copy-start.62 = (bf16[1024,256]{0,1:T(8,128)(2,1)S(1)}, bf16[1024,256]{0,1:T(8,128)(2,1)}, u32[]{:S(2)}) copy-start(bf16[1024,256]{0,1:T(8,128)(2,1)} %copy-done.61) | copy-start | bytes 1572868
  542.2 222.2 %all-reduce.9.cloned.1.call-start = ((), (), s32[]{:S(2)}) async-start(), calls=%async_computation.14 | async-start | bytes 4718592 | tf_op jit(solution)/shard_map/psum | solution.py:146
  555.4 67.9 %copy-start.52 = (bf16[1024,768]{0,1:T(8,128)(2,1)S(1)}, bf16[1024,768]{0,1:T(8,128)(2,1)}, u32[]{:S(2)}) copy-start(bf16[1024,768]{0,1:T(8,128)(2,1)} %get-tuple-element.90) | copy-start | bytes 4718596
  555.4 239.9 %all-gather.11.cloned.1.call-start = ((), (), s32[]{:S(2)}) async-start(), calls=%async_computation.9 | async-start | bytes 1474560 | tf_op jit(solution)/shard_map/all_gather | solution.py:150
  621.9 204.6 %all-gather.13.cloned.1.call-start = ((), (), s32[]{:S(2)}) async-start(), calls=%async_computation.10 | async-start | bytes 1474560 | tf_op jit(solution)/shard_map/all_gather | solution.py:151
  622.6 250.4 %all-gather.15.cloned.1.call-start = ((), (), s32[]{:S(2)}) async-start(), calls=%async_computation.11 | async-start | bytes 2621440 | tf_op jit(solution)/shard_map/all_gather | solution.py:152
  (139 other events, 448.8 us)
Sparse Core Ops, SparseCore 0:
  11.3 46.5 all-reduce.6
  59.4 88.7 all-gather.6
  149.8 87.8 all-gather.8
  315.8 19.0 reduce-scatter.6
  337.1 18.6 reduce-scatter.4
  358.0 96.1 reduce-scatter.8
  456.5 85.6 reduce-scatter.10
  547.2 74.6 all-reduce.10
  628.7 135.6 all-reduce.8
  765.9 29.3 all-gather.10
  796.9 29.5 all-gather.12
  828.0 45.0 all-gather.14

commit v2 on v1

v2 whole, which is shorter than its diff:
```python
import functools

import jax
import jax.numpy as jnp
from jax import lax
from jax.experimental import pallas as pl
from jax.experimental.pallas import tpu as pltpu
from jax.sharding import PartitionSpec as P

HEADS = 12
HEAD = 64
PAIRS = HEADS // 2
PAIR = 2 * HEAD
BF = jnp.bfloat16
F32 = jnp.float32
MESH = pl.DeviceIdType.MESH
VMEM_LIMIT = 67_043_328


def dot(left, right, left_dim, right_dim):
    return lax.dot_general(
        left, right, (((left_dim,), (right_dim,)), ((), ())), preferred_element_type=F32
    )


def place(index, size):
    return pl.ds(pl.multiple_of(index * size, size), size)


def rows_at(first, size, multiple):
    return pl.ds(pl.multiple_of(first, multiple), size)


class Link:
    def __init__(self, dp_size, tp_size, send_sems, recv_sems):
        self.dp_size, self.tp_size = dp_size, tp_size
        self.dp, self.tp = lax.axis_index("dp"), lax.axis_index("tp")
        self.bits = dp_size.bit_length() - 1
        self.low = min(3, self.bits)
        self.send_sems, self.recv_sems = send_sems, recv_sems
        self.used = 0

    def bit(self, b):
        return lax.rem(lax.div(self.dp, 1 << b), 2)

    def partner(self, b):
        return (self.dp + (1 - 2 * self.bit(b)) * (1 << b), self.tp)

    def ahead(self, k):
        return lax.rem(self.tp + k, self.tp_size)

    def behind(self, k):
        return lax.rem(self.tp + self.tp_size - k, self.tp_size)

    def greet(self, dp_bits):
        barrier = pltpu.get_barrier_semaphore()
        peers = [(self.dp, self.ahead(k)) for k in range(1, self.tp_size)]
        peers += [self.partner(b) for b in range(dp_bits)]
        for peer in peers:
            pl.semaphore_signal(barrier, inc=1, device_id=peer, device_id_type=MESH)
        pl.semaphore_wait(barrier, len(peers))

    def send(self, source, target, device):
        copy = pltpu.make_async_remote_copy(
            src_ref=source,
            dst_ref=target,
            send_sem=self.send_sems.at[self.used],
            recv_sem=self.recv_sems.at[self.used],
            device_id=device,
            device_id_type=MESH,
        )
        self.used += 1
        copy.start()
        return copy


def layer_norm(hidden, gain, shift):
    center = hidden - jnp.mean(hidden, axis=-1, keepdims=True)
    spread = jnp.mean(center * center, axis=-1, keepdims=True)
    return center * lax.rsqrt(spread + 1e-05) * gain + shift


def exact_gelu(value):
    return jax.nn.gelu(value, approximate=False)


FRONT_SEMS = 64


def gather_order(name):
    return (1, 2, 0) if name == "up" else (2, 1, 0)


class WeightGather:
    def __init__(self, link, name, shard, whole):
        self.link, self.shard, self.whole = link, shard, whole
        self.rows = shard.shape[0]
        self.order = [b for b in gather_order(name) if b < link.low]
        self.piece = self.rows >> len(self.order)
        offset, size = 0, self.piece
        for b in self.order:
            offset = offset + link.bit(b) * size
            size *= 2
        self.offset = offset
        self.step = {}
        self.waiting = {}

    def across(self, k):
        link = self.link
        rows = rows_at(self.offset, self.piece, self.piece)
        self.waiting[k] = link.send(
            self.shard.at[rows, :], self.whole.at[link.tp, rows, :], (link.dp, link.ahead(k))
        )
        self.step[k] = 0

    def advance(self, k):
        link, done = self.link, self.step[k]
        if done > len(self.order):
            return
        self.waiting[k].wait()
        self.step[k] = done + 1
        if done == len(self.order):
            return
        size = self.piece << done
        first = self.offset - lax.rem(self.offset, size)
        rows = rows_at(first, size, self.piece)
        region = self.whole.at[link.behind(k), rows, :]
        self.waiting[k] = link.send(region, region, link.partner(self.order[done]))


def front_kernel(
    dp_size,
    tp_size,
    len_ref,
    vec,
    bup,
    x,
    wq,
    wk,
    wv,
    wo,
    wup,
    wdn,
    e,
    xhat,
    rstd,
    mixed,
    q,
    probs,
    kb,
    vb,
    yb,
    ssum,
    em,
    bup_all,
    wup_all,
    wdn_all,
    ysend,
    yrecv,
    send_sems,
    recv_sems,
    local_sems,
):
    link = Link(dp_size, tp_size, send_sems, recv_sems)
    rows, width = x.shape
    slots, total = e.shape
    quarter = slots // tp_size
    others = range(1, tp_size)
    link.greet(link.low)

    own_up = pltpu.make_async_copy(wup, wup_all.at[link.tp], local_sems.at[0])
    own_dn = pltpu.make_async_copy(wdn, wdn_all.at[link.tp], local_sems.at[1])
    own_up.start()
    own_dn.start()
    bup_all[link.tp] = bup[...]
    length = len_ref[0]
    own_first = link.tp * rows
    position = lax.broadcasted_iota(jnp.int32, (1, rows), 1) + own_first
    live = (position < length).astype(F32)
    em[...] = (e[:, rows_at(own_first, rows, rows)].astype(F32) * live).astype(BF)
    ysend[...] = dot(em[...], x[...], 1, 0).astype(ysend.dtype)
    reduce = [
        link.send(ysend.at[place(link.ahead(k), quarter), :], yrecv.at[k - 1], (link.dp, link.ahead(k)))
        for k in others
    ]
    biases = [link.send(bup, bup_all.at[link.tp], (link.dp, link.ahead(k))) for k in others]
    q[...] = (dot(x[...], wq[...], 1, 0) + vec[0:1, :]).astype(BF)
    own_slots = place(link.tp, quarter)
    for copy in reduce:
        copy.wait()
    own_y = ysend[own_slots, :].astype(F32)
    for k in others:
        own_y = own_y + yrecv[k - 1].astype(F32)
    yb[own_slots, :] = own_y.astype(BF)
    share = [
        link.send(yb.at[own_slots, :], yb.at[own_slots, :], (link.dp, link.ahead(k))) for k in others
    ]
    gathers = [WeightGather(link, "up", wup, wup_all), WeightGather(link, "down", wdn, wdn_all)]
    for k in others:
        for gather in gathers:
            gather.across(k)
    row_live = (lax.broadcasted_iota(jnp.int32, (total, 128), 0) < length).astype(F32).astype(BF)
    ssum[...] = dot(e[...], row_live, 1, 0)
    for copy in share:
        copy.wait()
    for copy in biases:
        copy.wait()

    lane = lax.broadcasted_iota(jnp.int32, (1, PAIR), 1)
    first_half = (lane < HEAD).astype(F32)

    def project(weight, bias_row, blocks):
        full = dot(yb[...], weight[...], 1, 0)
        for p in range(PAIRS):
            cols = slice(p * PAIR, (p + 1) * PAIR)
            part = full[:, cols] + ssum[...] * vec[bias_row : bias_row + 1, cols]
            blocks[p, 0:slots, :] = (part * first_half).astype(BF)
            blocks[p, slots : 2 * slots, :] = (part * (1.0 - first_half)).astype(BF)

    project(wk, 1, kb)
    project(wv, 2, vb)

    block = min(256, rows)

    def attend(step, carry):
        p = lax.div(step, rows // block)
        here = place(lax.rem(step, rows // block), block)
        cols = place(p, PAIR)
        logits = dot(q[here, cols], kb[p], 1, 1) * 0.125
        halves = []
        for half in range(2):
            part = logits[:, half * slots : (half + 1) * slots]
            peak = jnp.max(part, axis=-1, keepdims=True)
            raised = jnp.exp(part - peak)
            halves.append((raised * (1.0 / jnp.sum(raised, axis=-1, keepdims=True))).astype(BF))
        both = jnp.concatenate(halves, axis=1)
        probs[p, here, :] = both
        mixed[here, cols] = dot(both, vb[p], 1, 0).astype(BF)
        return carry

    def advance(*ks):
        for k in ks:
            for gather in gathers:
                gather.advance(k)

    per_pair = rows // block
    lax.fori_loop(0, 2 * per_pair, attend, 0)
    advance(1)
    lax.fori_loop(2 * per_pair, 4 * per_pair, attend, 0)
    advance(2, 1)
    lax.fori_loop(4 * per_pair, 6 * per_pair, attend, 0)
    advance(3, 2, 1)

    def finish(step, carry):
        here = place(step, block)
        res = x[here, :].astype(F32) + dot(mixed[here, :], wo[...], 1, 0) + vec[3:4, :]
        center = res - jnp.mean(res, axis=-1, keepdims=True)
        inverse = lax.rsqrt(jnp.mean(center * center, axis=-1, keepdims=True) + 1e-05)
        xhat[here, :] = center * inverse
        rstd[here, :] = jnp.broadcast_to(inverse, (block, 128))
        return carry

    lax.fori_loop(0, rows // block, finish, 0)
    advance(3, 2, 3, 1, 2, 3)
    own_up.wait()
    own_dn.wait()


def front(mesh, lengths, vec, bup, x, wq, wk, wv, wo, wup, wdn, e):
    dp_size, tp_size = mesh.shape["dp"], mesh.shape["tp"]
    rows, width = x.shape
    slots = e.shape[0]
    vmem = pl.BlockSpec(memory_space=pltpu.VMEM)
    hbm = pl.BlockSpec(memory_space=pltpu.HBM)
    shape = jax.ShapeDtypeStruct
    return pl.pallas_call(
        functools.partial(front_kernel, dp_size, tp_size),
        out_shape=(
            shape((rows, width), F32),
            shape((rows, 128), F32),
            shape((rows, width), BF),
            shape((rows, width), BF),
            shape((PAIRS, rows, 2 * slots), BF),
            shape((PAIRS, 2 * slots, PAIR), BF),
            shape((PAIRS, 2 * slots, PAIR), BF),
            shape((slots, width), BF),
            shape((slots, 128), F32),
            shape((slots, rows), BF),
            shape((tp_size, 8, width), F32),
            shape((tp_size, *wup.shape), BF),
            shape((tp_size, *wdn.shape), BF),
        ),
        in_specs=[pl.BlockSpec(memory_space=pltpu.SMEM)] + [vmem] * 10,
        out_specs=tuple([vmem] * 11 + [hbm] * 2),
        scratch_shapes=[
            pltpu.VMEM((slots, width), BF),
            pltpu.VMEM((tp_size - 1, slots // tp_size, width), BF),
            pltpu.SemaphoreType.DMA((FRONT_SEMS,)),
            pltpu.SemaphoreType.DMA((FRONT_SEMS,)),
            pltpu.SemaphoreType.DMA((2,)),
        ],
        compiler_params=pltpu.CompilerParams(
            collective_id=0, has_side_effects=True, vmem_limit_bytes=VMEM_LIMIT
        ),
        name="front",
    )(lengths, vec, bup, x, wq, wk, wv, wo, wup, wdn, e)


BACK_SEMS = 160
VECTORS = 16


def add_rows(target, first, left, left_first, right, count):
    block = 96 if count % 96 == 0 else (48 if count % 48 == 0 else (32 if count % 32 == 0 else count))

    def step(i, carry):
        at = i * block
        total = (
            left[rows_at(left_first + at, block, 16), :].astype(F32)
            + right[rows_at(at, block, 16), :].astype(F32)
        )
        target[rows_at(first + at, block, 16), :] = total.astype(target.dtype)
        return carry

    lax.fori_loop(0, count // block, step, 0)


class Spread:
    def __init__(self, link, order, rows, acc, landing):
        self.link, self.acc, self.landing, self.rows = link, acc, landing, rows
        self.order = [b for b in order if b < link.low]
        self.inside = 0
        self.copy = None

    def _landing(self, i):
        first = sum(self.rows >> (j + 1) for j in range(i))
        return self.landing.at[pl.ds(first, self.rows >> (i + 1)), :]

    def start(self, i, source=None, loaded=False):
        if i == 0:
            self.source = None if loaded else source
        link, size = self.link, self.rows >> (i + 1)
        mine = link.bit(self.order[i])
        where, base = (source, 0) if i == 0 else (self.acc, self.inside)
        other = base + (1 - mine) * size
        self.copy = link.send(
            where.at[rows_at(other, size, 16), :], self._landing(i), link.partner(self.order[i])
        )
        if i > 0:
            self.inside = self.inside + mine * size

    def finish(self, i):
        source = self.source
        link, size = self.link, self.rows >> (i + 1)
        self.copy.wait()
        if i == 0:
            if source is None:
                add_rows(self.acc, 0, self.acc, 0, self._landing(0), size)
            else:
                add_rows(self.acc, 0, source, link.bit(self.order[0]) * size, self._landing(0), size)
        else:
            add_rows(self.acc, self.inside, self.acc, self.inside, self._landing(i), size)

    @property
    def piece(self):
        return self.rows >> len(self.order)

    @property
    def offset(self):
        return self.link.bit(self.order[0]) * (self.rows >> 1) + self.inside


class Collect:
    def __init__(self, link, order, offset, piece, region):
        self.link, self.offset, self.piece, self.region = link, offset, piece, region
        self.order = [b for b in order if b < link.low][::-1]
        self.copies = []
        self.stage = 0

    def start(self):
        size = self.piece << self.stage
        first = self.offset - lax.rem(self.offset, size)
        refs = self.region(first, size)
        peer = self.link.partner(self.order[self.stage])
        self.copies = [self.link.send(ref, ref, peer) for ref in refs]

    def finish(self):
        for copy in self.copies:
            copy.wait()
        self.stage += 1


def double_up(link, piece, landing):
    for i, b in enumerate(range(link.low, link.bits)):
        copy = link.send(piece, landing.at[i], link.partner(b))
        copy.wait()
        piece[...] = (piece[...].astype(F32) + landing[i].astype(F32)).astype(piece.dtype)


def back_kernel(
    dp_size,
    tp_size,
    len_ref,
    vec,
    part_vec,
    dnorm,
    xhat,
    rstd,
    x,
    q,
    mixed,
    probs,
    kb,
    vb,
    yb,
    ssum,
    em,
    wq,
    wk,
    wv,
    wo,
    gup,
    gdn,
    grad_in,
    gup_out,
    gdn_out,
    gq_out,
    go_out,
    gkv_out,
    seq_out,
    vec_out,
    dres,
    dmix,
    dq,
    dl,
    prob_slots,
    dpart,
    dland,
    dfull,
    up_acc,
    up_land,
    dn_acc,
    dn_land,
    up_zland,
    dn_zland,
    o_acc,
    o_land,
    q_acc,
    q_land,
    o_zland,
    q_zland,
    kv_send,
    kv_acc,
    kv_land,
    s_send,
    s_acc,
    s_land,
    vec_acc,
    vec_land,
    vec_z,
    wide_ff,
    wide_q,
    wide_kv,
    wide_s,
    wide_vec,
    send_sems,
    recv_sems,
    local_sems,
):
    link = Link(dp_size, tp_size, send_sems, recv_sems)
    rows, width = x.shape
    slots = yb.shape[0]
    others = range(1, tp_size)
    low = link.low
    first_load = pltpu.make_async_copy(dnorm, dres, local_sems.at[2 * tp_size])
    first_load.start()
    link.greet(link.bits)
    chunks = range(tp_size)
    up_order, dn_order = (0, 1, 2), (0, 2, 1)

    ups = [Spread(link, up_order, width, up_acc.at[c], up_land.at[c]) for c in chunks]
    dns = [Spread(link, dn_order, width, dn_acc.at[c], dn_land.at[c]) for c in chunks]
    half = width >> 1
    keep = rows_at(link.bit(0) * half, half, half)
    loads = []
    for c in chunks:
        ups[c].start(0, gup.at[c], loaded=True)
        dns[c].start(0, gdn.at[c], loaded=True)
        for n, (source, acc) in enumerate(((gup, up_acc), (gdn, dn_acc))):
            load = pltpu.make_async_copy(source.at[c, keep, :], acc.at[c], local_sems.at[2 * c + n])
            load.start()
            loads.append(load)

    block = min(256, rows)
    count = rows // block
    gain = vec[4:5, :]

    def norm_back(step, carry):
        g_gain, g_shift, g_out = carry
        here = place(step, block)
        grad, hat = dres[here, :], xhat[here, :]
        g_gain = g_gain + jnp.sum(grad * hat, axis=0, keepdims=True)
        g_shift = g_shift + jnp.sum(grad, axis=0, keepdims=True)
        scaled = grad * gain
        d_res = rstd[here, 0:1] * (
            scaled
            - jnp.mean(scaled, axis=-1, keepdims=True)
            - hat * jnp.mean(scaled * hat, axis=-1, keepdims=True)
        )
        dres[here, :] = d_res
        d_attn = d_res.astype(BF)
        dq[here, :] = d_attn
        g_out = g_out + jnp.sum(d_attn.astype(F32), axis=0, keepdims=True)
        return g_gain, g_shift, g_out

    zero = jnp.zeros((1, width), F32)
    first_load.wait()
    g_gain, g_shift, g_out = lax.fori_loop(0, count, norm_back, (zero, zero, zero))
    vec_acc[...] = part_vec[...]
    vec_acc[3:4, :] = g_out
    vec_acc[4:5, :] = g_gain
    vec_acc[5:6, :] = g_shift
    d_attn = dq

    def weight_grad(left, right, target):
        for m in range(3):
            cols = slice(m * (width // 3), (m + 1) * (width // 3))
            target[cols, :] = dot(left[:, cols], right[...], 0, 0).astype(BF)

    weight_grad(mixed, d_attn, go_out)
    spread_o = Spread(link, (0, 1, 2), width, o_acc, o_land)
    spread_o.start(0, go_out)
    dmix[...] = dot(d_attn[...], wo[...], 1, 1).astype(BF)

    for load in loads:
        load.wait()

    def spread_all(objs, i):
        for s in objs:
            s.finish(i)
        if i + 1 < low:
            for s in objs:
                s.start(i + 1)

    spread_all((ups[0], dns[0]), 0)

    own_half = lax.div(link.tp, 2)
    parity = lax.rem(link.tp, 2)
    lane_half = slots

    three = PAIRS // 2

    def pair_at(n):
        second = lax.div(n, three)
        which = (1 - own_half) * (1 - second) + own_half * second
        return which * three + lax.rem(n, three)

    def fetch(n):
        slot = lax.rem(n, 2)
        return pltpu.make_async_copy(
            probs.at[pair_at(n)], prob_slots.at[slot], local_sems.at[2 * tp_size + 1 + slot]
        )

    fetch(0).start()

    def attend_back(n):
        p = pair_at(n)
        cols = place(p, PAIR)

        @pl.when(n + 1 < PAIRS)
        def _():
            fetch(n + 1).start()

        fetch(n).wait()
        held = prob_slots.at[lax.rem(n, 2)]

        def part(step, carry):
            here = place(step, block)
            d_probs = dot(dmix[here, cols], vb[p], 1, 1)
            weights = held[here, :].astype(F32)
            halves = []
            for h in range(2):
                w = weights[:, h * slots : (h + 1) * slots]
                d = d_probs[:, h * slots : (h + 1) * slots]
                halves.append((w * (d - jnp.sum(w * d, axis=-1, keepdims=True))).astype(BF))
            both = jnp.concatenate(halves, axis=1)
            dl[here, :] = both
            dq[here, cols] = (dot(both, kb[p], 1, 0) * 0.125).astype(BF)
            return carry

        lax.fori_loop(0, count, part, 0)
        top, low_rows = rows_at(p * PAIR, HEAD, HEAD), rows_at(p * PAIR + HEAD, HEAD, HEAD)
        for n, total in enumerate(
            (dot(q[:, cols], dl[...], 0, 0) * 0.125, dot(dmix[:, cols], held[...], 0, 0))
        ):
            dpart[n, top, :] = total[:HEAD, :lane_half].astype(BF)
            dpart[n, low_rows, :] = total[HEAD:, lane_half:].astype(BF)

    def attend_half(first):
        def one(n, carry):
            attend_back(n)
            return carry

        lax.fori_loop(first, first + three, one, 0)

    attend_half(0)
    owned = width // tp_size

    def block_of(peer):
        return dpart.at[:, rows_at(peer * owned, owned, 64), :]

    d_copies = []
    for j in range(2):
        peer = 2 * (1 - own_half) + lax.rem(parity + j, 2)
        d_copies.append(link.send(block_of(peer), dland.at[j], (link.dp, peer)))
    spread_o.finish(0)
    if low > 1:
        spread_o.start(1)
    spread_all((ups[1], dns[1]), 0)
    spread_all((ups[0], dns[0]), 1)
    attend_half(three)
    peer = 2 * own_half + (1 - parity)
    d_copies.append(link.send(block_of(peer), dland.at[2], (link.dp, peer)))
    spread_all((ups[2], dns[2]), 0)
    spread_all((ups[1], dns[1]), 1)

    weight_grad(x, dq, gq_out)
    spread_q = Spread(link, (0, 2, 1), width, q_acc, q_land)
    spread_q.start(0, gq_out)

    for copy in d_copies:
        copy.wait()
    own_block = rows_at(link.tp * owned, owned, 64)
    for n in range(2):
        total = dpart[n, own_block, :].astype(F32)
        for j in range(tp_size - 1):
            total = total + dland[j, n].astype(F32)
        dfull[n, own_block, :] = total.astype(BF)
    d_share = [
        link.send(dfull.at[:, own_block, :], dfull.at[:, own_block, :], (link.dp, link.ahead(k)))
        for k in others
    ]
    for n in range(2):
        kv_send[n * owned : (n + 1) * owned, :] = dot(dfull[n, own_block, :], yb[...], 1, 0).astype(BF)
    spread_kv = Spread(link, (0, 1, 2), 2 * owned, kv_acc, kv_land)
    spread_kv.start(0, kv_send)
    spread_all((ups[3], dns[3]), 0)
    spread_all((ups[2], dns[2]), 1)
    vec_acc[0:1, :] = jnp.sum(dq[...].astype(F32), axis=0, keepdims=True)

    def input_grad(step, carry):
        here = place(step, block)
        dres[here, :] += dot(dq[here, :], wq[...], 1, 1)
        return carry

    lax.fori_loop(0, count, input_grad, 0)
    spread_o.finish(1) if low > 1 else None
    if low > 2:
        spread_o.start(2)
    spread_q.finish(0)
    if low > 1:
        spread_q.start(1)
    for copy in d_share:
        copy.wait()
    backs = dot(wk[...], dfull[0], 1, 0) + dot(wv[...], dfull[1], 1, 0)
    back = backs.T.astype(BF)
    small = vec[0:8, :].astype(BF)
    bias_row = dot(small, dfull[0], 1, 0)[1:2, :] + dot(small, dfull[1], 1, 0)[2:3, :]
    bias_column = jnp.broadcast_to(bias_row, (128, slots)).T[:, 0:1]
    position = lax.broadcasted_iota(jnp.int32, (1, rows), 1) + link.tp * rows
    live = (position < len_ref[0]).astype(F32)
    s_send[...] = ((dot(back, x[...], 1, 1) + bias_column) * live).astype(BF)
    spread_s = Spread(link, (0, 2, 1), slots, s_acc, s_land)
    spread_s.start(0, s_send)
    column = ssum[...].T[0:8, :]
    column_b = column.astype(BF)
    column_low = (column - column_b.astype(F32)).astype(BF)
    for n in range(2):
        total = dot(column_b, dfull[n], 1, 1) + dot(column_low, dfull[n], 1, 1)
        vec_acc[1 + n : 2 + n, :] = total[0:1, :] * (1.0 / tp_size)
    spread_all((ups[3], dns[3]), 1)

    def input_grad_last(step, carry):
        here = place(step, block)
        grad_in[here, :] = (dres[here, :] + dot(em[:, here], back, 0, 0)).astype(BF)
        return carry

    lax.fori_loop(0, count, input_grad_last, 0)

    def vec_step(b):
        copy = link.send(vec_acc, vec_land.at[b], link.partner(b))
        return copy

    tail = [spread_kv, spread_s]
    for i in range(low):
        copy = vec_step(i)
        for s in tail:
            s.finish(i)
            if i + 1 < low:
                s.start(i + 1)
        if i == 0:
            spread_all((ups[0], dns[0], ups[1], dns[1]), 2) if low > 2 else None
            if low > 1:
                spread_q.finish(1)
            if low > 2:
                spread_q.start(2)
                spread_o.finish(2)
        if i == 1:
            spread_all((ups[2], dns[2], ups[3], dns[3]), 2) if low > 2 else None
            if low > 2:
                spread_q.finish(2)
        copy.wait()
        vec_acc[...] = vec_acc[...] + vec_land[i]
    for b in range(low, link.bits):
        copy = vec_step(b)
        copy.wait()
        vec_acc[...] = vec_acc[...] + vec_land[b]

    vec_z[link.tp] = vec_acc[...]
    vec_copies = [link.send(vec_acc, vec_z.at[link.tp], (link.dp, link.ahead(k))) for k in others]

    ff_piece = ups[0].piece
    ff = []
    for accs, spreads, zland in ((up_acc, ups, up_zland), (dn_acc, dns, dn_zland)):
        inside = spreads[0].inside
        for k in others:
            source = accs.at[link.ahead(k), rows_at(inside, ff_piece, 16), :]
            ff.append(link.send(source, zland.at[k - 1], (link.dp, link.ahead(k))))
    lanes = 2
    deep = tp_size // lanes
    q_rows, q_cols = spread_q.piece // deep, width // lanes

    def quarter(first, t):
        return (
            rows_at(first + lax.div(t, lanes) * q_rows, q_rows, 16),
            pl.ds(pl.multiple_of(lax.rem(t, lanes) * q_cols, 128), q_cols),
        )

    quarters = []
    for spread, zland in ((spread_q, q_zland), (spread_o, o_zland)):
        for k in others:
            r, c = quarter(spread.inside, link.ahead(k))
            quarters.append(link.send(spread.acc.at[r, c], zland.at[k - 1], (link.dp, link.ahead(k))))

    kv_rows = rows_at(spread_kv.offset, spread_kv.piece, 16)
    s_rows = rows_at(spread_s.offset, spread_s.piece, 16)
    z_copies = []
    for spread, at, out, wide in (
        (spread_kv, kv_rows, gkv_out, wide_kv),
        (spread_s, s_rows, seq_out, wide_s),
    ):
        out[link.tp, at, :] = spread.acc[rows_at(spread.inside, spread.piece, 16), :]
        double_up(link, out.at[link.tp, at, :], wide)
        for k in others:
            z_copies.append(
                link.send(out.at[link.tp, at, :], out.at[link.tp, at, :], (link.dp, link.ahead(k)))
            )

    for copy in quarters:
        copy.wait()
    back_quarters = []
    for n, (spread, zland, out) in enumerate(((spread_q, q_zland, gq_out), (spread_o, o_zland, go_out))):
        r, c = quarter(spread.inside, link.tp)
        total = spread.acc[r, c].astype(F32)
        for k in others:
            total = total + zland[k - 1].astype(F32)
        r_out, _ = quarter(spread.offset, link.tp)
        out[r_out, c] = total.astype(BF)
        region = out.at[r_out, c]
        double_up(link, region, wide_q.at[n])
        for k in others:
            back_quarters.append(link.send(region, region, (link.dp, link.ahead(k))))

    for copy in ff:
        copy.wait()
    collects = []
    for n, (accs, spreads, zland, out, order) in enumerate(
        ((up_acc, ups, up_zland, gup_out, up_order), (dn_acc, dns, dn_zland, gdn_out, dn_order))
    ):
        inside, offset = spreads[0].inside, spreads[0].offset
        total = accs[link.tp, rows_at(inside, ff_piece, 16), :].astype(F32)
        for k in others:
            total = total + zland[k - 1].astype(F32)
        own = rows_at(offset, ff_piece, 16)
        out[own, :] = total.astype(BF)
        double_up(link, out.at[own, :], wide_ff.at[n])
        collects.append(
            Collect(
                link, order, offset, ff_piece,
                lambda first, size, out=out: [out.at[rows_at(first, size, 16), :]],
            )
        )
        collects[-1].start()
    for copy in z_copies:
        copy.wait()
    for spread, out, order in ((spread_kv, gkv_out, (0, 1, 2)), (spread_s, seq_out, (0, 2, 1))):
        collects.append(
            Collect(
                link, order, spread.offset, spread.piece,
                lambda first, size, out=out: [out.at[:, rows_at(first, size, 16), :]],
            )
        )
        collects[-1].start()
    for copy in back_quarters:
        copy.wait()
    for spread, out, order in ((spread_q, gq_out, (0, 2, 1)), (spread_o, go_out, (0, 1, 2))):
        collects.append(
            Collect(
                link, order, spread.offset, spread.piece,
                lambda first, size, out=out: [out.at[rows_at(first, size, 16), :]],
            )
        )
        collects[-1].start()
    for i in range(low):
        for collect in collects:
            collect.finish()
            if i + 1 < low:
                collect.start()
    for copy in vec_copies:
        copy.wait()
    total = vec_z[0]
    for t in range(1, tp_size):
        total = total + vec_z[t]
    vec_out[...] = total


def back(mesh, lengths, vec, part_vec, dnorm, xhat, rstd, x, q, mixed, probs, kb, vb, yb, ssum, em, wq, wk, wv, wo, gup, gdn):
    dp_size, tp_size = mesh.shape["dp"], mesh.shape["tp"]
    bits = dp_size.bit_length() - 1
    low = min(3, bits)
    wide = max(1, bits - low)
    rows, width = x.shape
    slots = yb.shape[0]
    owned = width // tp_size
    others = tp_size - 1
    vmem = pl.BlockSpec(memory_space=pltpu.VMEM)
    hbm = pl.BlockSpec(memory_space=pltpu.HBM)
    shape = jax.ShapeDtypeStruct

    def landing(total):
        return sum(total >> (i + 1) for i in range(low))

    def buf(*dims, dtype=BF):
        return pltpu.VMEM(dims, dtype)

    ff_piece, kv_piece, s_piece = width >> low, 2 * owned >> low, slots >> low
    return pl.pallas_call(
        functools.partial(back_kernel, dp_size, tp_size),
        out_shape=(
            shape((rows, width), BF),
            shape((width, width), BF),
            shape((width, width), BF),
            shape((width, width), BF),
            shape((width, width), BF),
            shape((tp_size, 2 * owned, width), BF),
            shape((tp_size, slots, rows), BF),
            shape((VECTORS, width), F32),
        ),
        in_specs=[pl.BlockSpec(memory_space=pltpu.SMEM)] + [vmem] * 2 + [hbm] + [vmem] * 5 + [hbm] + [vmem] * 9 + [hbm] * 2,
        out_specs=tuple([vmem] * 8),
        scratch_shapes=[
            buf(rows, width, dtype=F32),
            buf(rows, width),
            buf(rows, width),
            buf(rows, 2 * slots),
            buf(2, rows, 2 * slots),
            buf(2, width, slots),
            buf(others, 2, owned, slots),
            buf(2, width, slots),
            buf(tp_size, width // 2, width),
            buf(tp_size, landing(width), width),
            buf(tp_size, width // 2, width),
            buf(tp_size, landing(width), width),
            buf(others, ff_piece, width),
            buf(others, ff_piece, width),
            buf(width // 2, width),
            buf(landing(width), width),
            buf(width // 2, width),
            buf(landing(width), width),
            buf(others, ff_piece // (tp_size // 2), width // 2),
            buf(others, ff_piece // (tp_size // 2), width // 2),
            buf(2 * owned, width),
            buf(owned, width),
            buf(landing(2 * owned), width),
            buf(slots, rows),
            buf(slots // 2, rows),
            buf(landing(slots), rows),
            buf(VECTORS, width, dtype=F32),
            buf(max(1, bits), VECTORS, width, dtype=F32),
            buf(tp_size, VECTORS, width, dtype=F32),
            buf(2, wide, ff_piece, width),
            buf(2, wide, ff_piece // (tp_size // 2), width // 2),
            buf(wide, kv_piece, width),
            buf(wide, s_piece, rows),
            buf(wide, VECTORS, width, dtype=F32),
            pltpu.SemaphoreType.DMA((BACK_SEMS,)),
            pltpu.SemaphoreType.DMA((BACK_SEMS,)),
            pltpu.SemaphoreType.DMA((2 * tp_size + 3,)),
        ],
        compiler_params=pltpu.CompilerParams(
            collective_id=1, has_side_effects=True, vmem_limit_bytes=VMEM_LIMIT
        ),
        name="back",
    )(lengths, vec, part_vec, dnorm, xhat, rstd, x, q, mixed, probs, kb, vb, yb, ssum, em, wq, wk, wv, wo, gup, gdn)


def finish_kernel(
    tp_size, gup, gdn, gq, go, gkv, seq, vec,
    o_up, o_dn, o_q, o_o, o_k, o_v, o_seq, *rest,
):
    vectors, (in_up, in_dn, in_q, in_o, in_kv, in_seq, f_up, f_dn, f_q, f_o, f_k, f_v, f_seq, turn, in_sems, out_sems) = rest[:10], rest[10:]
    pairs = [(gq, in_q), (go, in_o), (gup, in_up), (gdn, in_dn), (gkv, in_kv), (seq, in_seq)]
    loads = []
    for n, (source, target) in enumerate(pairs):
        loads.append(pltpu.make_async_copy(source, target, in_sems.at[n]))
        loads[-1].start()
    stores = []

    def put(staged, out):
        copy = pltpu.make_async_copy(staged, out, out_sems.at[len(stores)])
        copy.start()
        stores.append(copy)

    for n, row in enumerate((0, 1, 2, 3, 4, 5, 6, 7, 8)):
        vectors[n][...] = vec[row, :]
    vectors[9][...] = vec[pl.ds(9 + lax.axis_index("tp"), 1), :][0]
    width = gq.shape[0]
    for n, (narrow, wide, out) in enumerate(
        ((in_q, f_q, o_q), (in_o, f_o, o_o), (in_up, f_up, o_up), (in_dn, f_dn, o_dn))
    ):
        loads[n].wait()
        wide[...] = narrow[...].astype(F32)
        put(wide, out)
    loads[4].wait()
    owned = width // tp_size
    for n, (wide, out) in enumerate(((f_k, o_k), (f_v, o_v))):
        for c in range(tp_size):
            turn[c * owned : (c + 1) * owned, :] = in_kv[c, n * owned : (n + 1) * owned, :]
        for c in range(3):
            cols = slice(c * (width // 3), (c + 1) * (width // 3))
            wide[:, cols] = turn[cols, :].astype(F32).T
        put(wide, out)
    loads[5].wait()
    rows = in_seq.shape[2]
    for c in range(tp_size):
        f_seq[:, c * rows : (c + 1) * rows] = in_seq[c].astype(F32)
    put(f_seq, o_seq)
    for copy in stores:
        copy.wait()


def finish(tp_size, gup, gdn, gq, go, gkv, seq, vec):
    width = gq.shape[0]
    _, slots, rows = seq.shape
    square, flat = (width, width), (slots, tp_size * rows)
    vmem = pl.BlockSpec(memory_space=pltpu.VMEM)
    hbm = pl.BlockSpec(memory_space=pltpu.HBM)
    shape = jax.ShapeDtypeStruct
    return pl.pallas_call(
        functools.partial(finish_kernel, tp_size),
        out_shape=tuple([shape(square, F32)] * 6 + [shape(flat, F32)] + [shape((width,), F32)] * 10),
        in_specs=[hbm] * 6 + [vmem],
        out_specs=tuple([hbm] * 7 + [vmem] * 10),
        scratch_shapes=[pltpu.VMEM(square, BF)] * 4
        + [pltpu.VMEM(gkv.shape, BF), pltpu.VMEM(seq.shape, BF)]
        + [pltpu.VMEM(square, F32)] * 6
        + [pltpu.VMEM(flat, F32), pltpu.VMEM(square, BF)]
        + [pltpu.SemaphoreType.DMA((6,)), pltpu.SemaphoreType.DMA((7,))],
        compiler_params=pltpu.CompilerParams(vmem_limit_bytes=VMEM_LIMIT),
        name="finish",
    )(gup, gdn, gq, go, gkv, seq, vec)


def on_device(
    mesh,
    layer_in,
    out_grad,
    lengths,
    w_query,
    b_query,
    w_key,
    b_key,
    w_value,
    b_value,
    w_out,
    b_out,
    seq_proj,
    attn_gain,
    attn_shift,
    w_up,
    b_up,
    w_down,
    b_down,
    ffn_gain,
    ffn_shift,
):
    row_count, width = layer_in.shape
    tp_size = mesh.shape["tp"]
    vec = jnp.stack(
        [b_query, b_key, b_value, b_out, attn_gain, attn_shift, b_down, ffn_gain, ffn_shift] + [b_query] * 7
    ).astype(F32)
    bup = jnp.broadcast_to(b_up.astype(F32)[None, :], (8, width))
    xhat, rstd, mixed, queries, probs, kb, vb, folded, ssum, own_proj, bup_all, up_all, down_all = front(
        mesh, lengths, vec, bup, layer_in, w_query, w_key, w_value, w_out, w_up, w_down, seq_proj
    )
    normed = xhat * attn_gain.astype(F32) + attn_shift.astype(F32)
    normed_b = normed.astype(BF)
    pre_act = jnp.concatenate([dot(normed_b, up_all[c], 1, 0) + bup_all[c, 0:1] for c in range(tp_size)], axis=1)
    down_flat = down_all.reshape(-1, width)
    hidden_act, gelu_pull = jax.vjp(exact_gelu, pre_act)
    hidden_b = hidden_act.astype(BF)
    branch = dot(hidden_b, down_flat, 1, 0) + b_down.astype(F32)
    res_two = normed + branch
    final, norm_two_pull = jax.vjp(
        layer_norm, res_two, ffn_gain.astype(F32), ffn_shift.astype(F32)
    )
    layer_out = final.astype(BF)
    d_res_two, g_ffn_gain, g_ffn_shift = norm_two_pull(out_grad.astype(F32))
    d_branch = d_res_two.astype(BF)
    g_b_down = jnp.sum(d_branch.astype(F32), axis=0)
    g_down = dot(hidden_b, d_branch, 0, 0).astype(BF).reshape(tp_size, width, width)
    (d_hidden,) = gelu_pull(dot(d_branch, down_flat, 1, 1))
    d_pre = d_hidden.astype(BF)
    g_b_up = jnp.sum(d_pre.astype(F32), axis=0)
    parts = [d_pre[:, c * width : (c + 1) * width] for c in range(tp_size)]
    g_up = jnp.stack([dot(normed_b, part, 0, 0).astype(BF) for part in parts])
    d_normed = d_res_two + sum(dot(part, up_all[c], 1, 1) for c, part in enumerate(parts))
    none = jnp.zeros((width,), F32)
    part_vec = jnp.stack(
        [none] * 6 + [g_ffn_gain, g_ffn_shift, g_b_down, *g_b_up.reshape(tp_size, width)] + [none] * (7 - tp_size)
    )
    grad_in, g_up, g_down, g_q, g_o, g_kv, g_seq, vec_sum = back(
        mesh, lengths, vec, part_vec, d_normed, xhat, rstd, layer_in, queries, mixed, probs, kb, vb, folded, ssum,
        own_proj, w_query, w_key, w_value, w_out, g_up, g_down
    )
    (
        g_w_up, g_w_down, g_w_query, g_w_out, g_w_key, g_w_value, g_seq_proj,
        g_b_query, g_b_key, g_b_value, g_b_out, g_attn_gain, g_attn_shift, g_ffn_gain, g_ffn_shift, g_b_down, g_b_up,
    ) = finish(tp_size, g_up, g_down, g_q, g_o, g_kv, g_seq, vec_sum)
    return (
        layer_out,
        grad_in,
        g_w_query,
        g_b_query,
        g_w_key,
        g_b_key,
        g_w_value,
        g_b_value,
        g_w_out,
        g_b_out,
        g_seq_proj,
        g_attn_gain,
        g_attn_shift,
        g_w_up,
        g_b_up,
        g_w_down,
        g_b_down,
        g_ffn_gain,
        g_ffn_shift,
    )


def solution(mesh):
    in_specs = (
        P(("dp", "tp"), None),
        P(("dp", "tp"), None),
        P("dp"),
        *([P()] * 11),
        P(None, "tp"),
        P("tp"),
        P("tp", None),
        P(),
        P(),
        P(),
    )
    out_specs = (
        P(("dp", "tp"), None),
        P(("dp", "tp"), None),
        *([P()] * 11),
        P(None, "tp"),
        P("tp"),
        P("tp", None),
        P(),
        P(),
        P(),
    )
    return jax.shard_map(
        functools.partial(on_device, mesh), mesh=mesh, in_specs=in_specs, out_specs=out_specs, check_vma=False
    )
```

time: 896 us -> 381 us (0.43)
  waiting for transfers between devices: 512 us -> 0 us
  Pallas kernels: 0 us -> 271 us
  matrix products: 197 us -> 50.8 us
  blocking collectives: 97.7 us -> 0 us
  between operations: 17 us -> 2 us
  local copies, waits for them, and re-layouts: 26.5 us -> 14.3 us
    pallas_call x0 -> x3, Pallas kernels: none -> 271 us  [the longest x1 175 us: back(): pl.pallas_call(functools.partial(back_kernel, dp_size, tp_size), out_shap...]
    all_gather x5 -> x0, waiting for transfers between devices: 210 us -> none  [the longest x1 65.8 us: on_device(): up_all = lax.all_gather(w_up.T, 'tp', axis=0, tiled=True)]
    psum x3 -> x0, waiting for transfers between devices: 175 us -> none  [the longest x1 88.2 us: on_device(): g_w_query, g_w_out = lax.psum((g_w_query.astype(BF), g_w_out), ('dp', 'tp'))]
    dot_general x99 -> x15, matrix products: 197 us -> 50.8 us  [dot(): lax.dot_general(left, right, (((left_dim,), (right_dim,)), ((), ())), pre...]
    reduce_scatter x4 -> x0, waiting for transfers between devices: 125 us -> none  [the longest x1 88 us: on_device(): lax.psum_scatter(g_w_down, 'tp', scatter_dimension=0, tiled=True)]
    all_gather x3 -> x0, blocking collectives: 56.5 us -> none  [the longest x1 21 us: on_device(): d_proj_keys = lax.all_gather(own_dk, 'tp', axis=0, tiled=True)]
    psum x1 -> x0, blocking collectives: 41.2 us -> none  [on_device(): lax.psum((g_b_query, g_b_key, g_b_value, g_b_out, g_attn_gain, g_attn_shi...]
    unnamed x329 -> x31, local copies, waits for them, and re-layouts: 25.9 us -> 4.43 us
  transfers between devices with their start and end apart: 12 -> 0, of which waited for: 10 -> 0; matrix products, arithmetic and copies ran while one was open for 18% -> 0% of each run, Pallas kernels for 0% -> 0%
where the time goes in v2:
time: 381 us; the launch traced here: 377 us
  Pallas kernels  271 us (71%)
  matrix products  50.8 us (13%)
  other arithmetic  39.5 us (10%)
  local copies, waits for them, and re-layouts  14.3 us (4%)
    pallas_call x1, Pallas kernels, back(): pl.pallas_call(functools.partial(back_kernel, dp_size, tp_size), out_shap...  175 us
    pallas_call x1, Pallas kernels, front(): pl.pallas_call(functools.partial(front_kernel, dp_size, tp_size), out_sha...  85.5 us
    dot_general x15, matrix products, dot(): lax.dot_general(left, right, (((left_dim,), (right_dim,)), ((), ())), pre...  50.8 us
    convert_element_type x1, other arithmetic, on_device(): hidden_b = hidden_act.astype(BF)  27.5 us
    pallas_call x1, Pallas kernels, finish(): pl.pallas_call(functools.partial(finish_kernel, tp_size), out_shape=tuple...  10.6 us

profile of v2, /device:TPU:0, one launch (start us, length us, event | category | flops | bytes accessed | tf_op | source)
XLA Modules:
  0.0 377.2 jit_solution(15948596549364286924)
XLA Ops:
  0.7 0.7 stack.63
  8.2 1.3 broadcast_in_dim.6.bup
  9.5 85.5 %front.1 = (f32[1024,768]{1,0:T(8,128)}, f32[1024,128]{1,0:T(8,128)}, bf16[1024,768]{1,0:T(8,128)(2,1)}, bf16[1024,768]{1,0:T(8,128)(2,1)}, bf16[6,1024,512]{2,1...) custom-call(s32[1]{0:T(128)S(6)} %copy.45.len_ref, ...), custom_call_target="tpu_custom_call" | custom-call | tf_op jit(solution)/shard_map/front/pallas_call | solution.py:276
  95.0 0.8 convert_element_type.62
  95.8 0.9 convert_element_type.63
  96.7 2.2 fusion.10
  98.9 1.0 slice_reduce_fusion.3
  99.9 1.5 convolution_add_fusion.3
  101.3 1.5 convolution_add_fusion.2
  102.8 1.5 convolution_add_fusion.1
  104.4 1.5 convolution_add_fusion
  106.0 27.5 %multiply_convert_fusion = (bf16[1024,3072]{0,1:T(8,128)(2,1)S(1)}, f32[1024,3072]{0,1:T(8,128)S(1)}) fusion(f32[1024,768]{0,1:T(8,128)S(1)} %convolution_add_fusion, f32[1024,768]{0,1:T(8,128)S(1)} %convolution_add_fusion.1, f32[1024,768]{0,1:T(8,128)S(1)} %convolution_add_fusion.2, f32[1024,768]{0,1:T(8,128)S(1)} %convolution_add_fusion.3), kind=kLoop, calls=%fused_computation.5 | loop fusion | flops 213909504 | bytes 31457280 | tf_op jit(solution)/shard_map/convert_element_type | solution.py:1011
  133.5 8.2 %fusion.46 = (f32[1024]{0:T(1024)S(1)}, f32[1024,768]{1,0:T(8,128)S(1)}) fusion(f32[768]{0:T(1024)S(1)} %convert_element_type.66, bf16[1024,3072]{0,1:T(8,128)(2,1)S(1)} %get-tuple-element.106, bf16[3072,768]{1,0:T(8,128)(2,1)} %bitcast.47, f32[768]{0:T(1024)S(1)} %convert_element_type.63, f32[1024,768]{1,0:T(8,128)S(1)} %copy-done, ...), kind=kOutput, calls=%fused_computation.87 | convolution fusion | flops 4835769344 | bytes 17314816 | tf_op jit(solution)/shard_map/dot_general | solution.py:21
  142.4 0.7 copy-done.1
  143.2 1.3 fusion.8
  144.5 2.6 fusion.43
  147.5 6.7 %convolution_convert_fusion = bf16[3072,768]{1,0:T(8,128)(2,1)} fusion(bf16[1024,3072]{0,1:T(8,128)(2,1)S(1)} %get-tuple-element.106, bf16[1024,768]{1,0:T(8,128)(2,1)S(1)} %get-tuple-element.103), kind=kOutput, calls=%fused_computation.19 | convolution fusion | flops 4834197504 | bytes 12582912 | tf_op jit(solution)/shard_map/dot_general | solution.py:21
  154.2 13.8 %convert_reduce_fusion = (f32[3072]{0:T(1024)S(1)}, bf16[1024,3072]{0,1:T(8,128)(2,1)}) fusion(f32[1024,3072]{0,1:T(8,128)S(1)} %get-tuple-element.107, bf16[1024,768]{1,0:T(8,128)(2,1)} %copy-done.7, bf16[3072,768]{1,0:T(8,128)(2,1)} %bitcast.48, f32[1024,768]{0,1:T(8,128)} %copy-done.4, f32[1024,768]{0,1:T(8,128)} %copy-done.3, f32[1024,768]{0,1:T(8,128)} %copy-done.2, ...), kind=kOutput, calls=%fused_computation.3 | convolution fusion | flops 4891603968 | bytes 37761024 | tf_op jit(solution)/shard_map/dot_general | solution.py:21
  167.9 3.5 fusion.11
  171.4 0.7 copy-done.8
  172.1 1.4 fusion.12
  173.6 1.4 fusion.13
  175.0 1.4 fusion.14
  176.5 2.7 pad_maximum_fusion.1.gup
  179.2 1.5 fusion.21
  180.7 1.5 fusion.24
  182.1 1.5 fusion.18
  183.6 4.1 %add_add_fusion.1.dnorm = f32[1024,768]{1,0:T(8,128)} fusion(f32[1024,768]{1,0:T(8,128)S(1)} %fusion.18, f32[1024,768]{1,0:T(8,128)S(1)} %fusion.24, f32[1024,768]{1,0:T(8,128)S(1)} %fusion.21, f32[1024,768]{1,0:T(8,128)S(1)} %get-tuple-element.105, f32[1024]{0:T(1024)S(1)} %negate_multiply_fusion.1, bf16[1024,3072]{0,1:T(8,128)(2,1)S(1)} %copy-done.8, ...), kind=kOutput, calls=%fused_computation.29 | convolution fusion | flops 1211891712 | bytes 18485248 | tf_op jit(solution)/shard_map/dot_general | solution.py:21
  187.8 1.3 stack.75.part_vec
  189.1 174.7 %back.1 = (bf16[1024,768]{1,0:T(8,128)(2,1)}, bf16[768,768]{1,0:T(8,128)(2,1)}, bf16[768,768]{1,0:T(8,128)(2,1)}, bf16[768,768]{1,0:T(8,128)(2,1)}, bf16[768,768...) custom-call(s32[1]{0:T(128)S(6)} %copy.45.len_ref, ...), custom_call_target="tpu_custom_call" | custom-call | tf_op jit(solution)/shard_map/back/pallas_call | solution.py:847
  363.7 10.6 %finish.1 = (f32[768,768]{1,0:T(8,128)}, f32[768,768]{1,0:T(8,128)}, f32[768,768]{1,0:T(8,128)}, f32[768,768]{1,0:T(8,128)}, f32[768,768]{1,0:T(8,128)}, /*index...) custom-call(bf16[768,768]{1,0:T(8,128)(2,1)} %get-tuple-element.71.g, ...), custom_call_target="tpu_custom_call" | custom-call | tf_op jit(solution)/shard_map/finish/pallas_call | solution.py:959
  374.3 2.7 copy.46
  (59 shorter events, 7.4 us)
Async XLA Ops:
  95.0 4.9 %copy-start.9 = (bf16[4,768,768]{2,1,0:T(8,128)(2,1)S(1)}, bf16[4,768,768]{2,1,0:T(8,128)(2,1)}, u32[]{:S(2)}) copy-start(bf16[4,768,768]{2,1,0:T(8,128)(2,1)} %get-tuple-element.58) | copy-start | bytes 14155780
  98.9 5.5 %copy-start.5 = (bf16[1024,768]{1,0:T(8,128)(2,1)}, bf16[1024,768]{1,0:T(8,128)(2,1)S(1)}, u32[]{:S(2)}) copy-start(bf16[1024,768]{1,0:T(8,128)(2,1)S(1)} %fusion.10) | copy-start | bytes 4718596
  102.8 3.0 copy-start.2
  104.3 1.6 copy-start.3
  106.0 27.5 %copy-start.4 = (f32[1024,768]{0,1:T(8,128)}, f32[1024,768]{0,1:T(8,128)S(1)}, u32[]{:S(2)}) copy-start(f32[1024,768]{0,1:T(8,128)S(1)} %convolution_add_fusion) | copy-start | bytes 9437188
  106.0 27.5 %copy-start.10 = (bf16[768]{0:T(1024)(128)(2,1)S(1)}, bf16[768]{0:T(1024)(128)(2,1)}, u32[]{:S(2)}) copy-start(bf16[768]{0:T(1024)(128)(2,1)} %param.37) | copy-start | bytes 4612
  106.0 27.5 %copy-start = (f32[1024,768]{1,0:T(8,128)S(1)}, f32[1024,768]{1,0:T(8,128)}, u32[]{:S(2)}) copy-start(f32[1024,768]{1,0:T(8,128)} %get-tuple-element.57.xhat) | copy-start | bytes 9437188
  141.7 0.7 copy-start.11
  141.7 1.4 copy-start.1
  142.3 2.2 copy-start.12
  147.4 6.7 %copy-start.7 = (bf16[1024,768]{1,0:T(8,128)(2,1)}, bf16[1024,768]{1,0:T(8,128)(2,1)S(1)}, u32[]{:S(2)}) copy-start(bf16[1024,768]{1,0:T(8,128)(2,1)S(1)} %get-tuple-element.103) | copy-start | bytes 4718596
  167.9 3.5 copy-start.6
  167.9 4.2 %copy-start.8 = (bf16[1024,3072]{0,1:T(8,128)(2,1)S(1)}, bf16[1024,3072]{0,1:T(8,128)(2,1)}, u32[]{:S(2)}) copy-start(bf16[1024,3072]{0,1:T(8,128)(2,1)} %get-tuple-element.116) | copy-start | bytes 18874372
  173.6 5.6 %slice-start = ((s8[4718592]{0:T(1024)(128)(4,1)}), s8[4194304]{0:T(1024)(128)(4,1)S(1)}, s32[]{:S(2)}) async-start(s8[4718592]{0:T(1024)(128)(4,1)} %bitcast.45), calls=%async_computation | async-start | bytes 8388608
  175.0 4.2 %slice-start.1 = ((s8[4718592]{0:T(1024)(128)(4,1)}), s8[524288]{0:T(1024)(128)(4,1)S(1)}, s32[]{:S(2)}) async-start(s8[4718592]{0:T(1024)(128)(4,1)} %bitcast.45), calls=%async_computation.1 | async-start | bytes 1048576

commit v3 on v2

v3 whole, which is shorter than its diff:
```python
import functools

import jax
import jax.numpy as jnp
from jax import lax
from jax.experimental import pallas as pl
from jax.experimental.pallas import tpu as pltpu
from jax.sharding import PartitionSpec as P

HEADS = 12
HEAD = 64
PAIRS = HEADS // 2
PAIR = 2 * HEAD
BF = jnp.bfloat16
F32 = jnp.float32
MESH = pl.DeviceIdType.MESH
VMEM_LIMIT = 67_043_328


def dot(left, right, left_dim, right_dim):
    return lax.dot_general(
        left, right, (((left_dim,), (right_dim,)), ((), ())), preferred_element_type=F32
    )


def place(index, size):
    return pl.ds(pl.multiple_of(index * size, size), size)


def rows_at(first, size, multiple):
    return pl.ds(pl.multiple_of(first, multiple), size)


class Link:
    def __init__(self, dp_size, tp_size, send_sems, recv_sems):
        self.dp_size, self.tp_size = dp_size, tp_size
        self.dp, self.tp = lax.axis_index("dp"), lax.axis_index("tp")
        self.bits = dp_size.bit_length() - 1
        self.low = min(3, self.bits)
        self.send_sems, self.recv_sems = send_sems, recv_sems
        self.used = 0

    def bit(self, b):
        return lax.rem(lax.div(self.dp, 1 << b), 2)

    def partner(self, b):
        return (self.dp + (1 - 2 * self.bit(b)) * (1 << b), self.tp)

    def ahead(self, k):
        return lax.rem(self.tp + k, self.tp_size)

    def behind(self, k):
        return lax.rem(self.tp + self.tp_size - k, self.tp_size)

    def greet(self, dp_bits):
        barrier = pltpu.get_barrier_semaphore()
        peers = [(self.dp, self.ahead(k)) for k in range(1, self.tp_size)]
        peers += [self.partner(b) for b in range(dp_bits)]
        for peer in peers:
            pl.semaphore_signal(barrier, inc=1, device_id=peer, device_id_type=MESH)
        pl.semaphore_wait(barrier, len(peers))

    def take(self, count):
        first = self.used
        self.used += count
        assert self.used <= self.send_sems.shape[0]
        return first

    def remote(self, slot, source, target, device):
        return pltpu.make_async_remote_copy(
            src_ref=source,
            dst_ref=target,
            send_sem=self.send_sems.at[slot],
            recv_sem=self.recv_sems.at[slot],
            device_id=device,
            device_id_type=MESH,
        )

    def send(self, source, target, device):
        copy = self.remote(self.take(1), source, target, device)
        copy.start()
        return copy


FRONT_SEMS = 64
VECTORS = 16


def gather_order(name):
    return (1, 2, 0) if name == "up" else (2, 1, 0)


class WeightGather:
    def __init__(self, link, name, shard, whole):
        self.link, self.shard, self.whole = link, shard, whole
        self.rows = shard.shape[0]
        self.order = [b for b in gather_order(name) if b < link.low]
        self.piece = self.rows >> len(self.order)
        offset, size = 0, self.piece
        for b in self.order:
            offset = offset + link.bit(b) * size
            size *= 2
        self.offset = offset
        self.step = {}
        self.waiting = {}

    def across(self, k):
        link = self.link
        rows = rows_at(self.offset, self.piece, self.piece)
        self.waiting[k] = link.send(
            self.shard.at[rows, :], self.whole.at[link.tp, rows, :], (link.dp, link.ahead(k))
        )
        self.step[k] = 0

    def advance(self, k):
        link, done = self.link, self.step[k]
        if done > len(self.order):
            return
        self.waiting[k].wait()
        self.step[k] = done + 1
        if done == len(self.order):
            return
        size = self.piece << done
        first = self.offset - lax.rem(self.offset, size)
        rows = rows_at(first, size, self.piece)
        region = self.whole.at[link.behind(k), rows, :]
        self.waiting[k] = link.send(region, region, link.partner(self.order[done]))


def front_kernel(
    dp_size,
    tp_size,
    len_ref,
    x,
    wq,
    wk,
    wv,
    wo,
    wup,
    wdn,
    e,
    *rest,
):
    names, b_up, rest = rest[:9], rest[9], rest[10:]
    front_body(dp_size, tp_size, len_ref, x, wq, wk, wv, wo, wup, wdn, e, names, b_up, *rest)


def front_body(
    dp_size,
    tp_size,
    len_ref,
    x,
    wq,
    wk,
    wv,
    wo,
    wup,
    wdn,
    e,
    vectors,
    b_up,
    vec,
    xhat,
    rstd,
    mixed,
    q,
    probs,
    kb,
    vb,
    yb,
    ssum,
    em,
    bup_all,
    wup_all,
    wdn_all,
    bup,
    ysend,
    yrecv,
    send_sems,
    recv_sems,
    local_sems,
):
    link = Link(dp_size, tp_size, send_sems, recv_sems)
    rows, width = x.shape
    slots, total = e.shape
    quarter = slots // tp_size
    others = range(1, tp_size)
    link.greet(link.low)

    own_up = pltpu.make_async_copy(wup, wup_all.at[link.tp], local_sems.at[0])
    own_dn = pltpu.make_async_copy(wdn, wdn_all.at[link.tp], local_sems.at[1])
    own_up.start()
    own_dn.start()
    vec[...] = jnp.zeros_like(vec)
    for n, vector in enumerate(vectors):
        vec[n : n + 1, :] = vector[...].astype(F32).reshape(1, width)
    bup[...] = jnp.broadcast_to(b_up[...].astype(F32).reshape(1, width), bup.shape)
    bup_all[link.tp] = bup[...]
    length = len_ref[0]
    own_first = link.tp * rows
    position = lax.broadcasted_iota(jnp.int32, (1, rows), 1) + own_first
    live = (position < length).astype(F32)
    em[...] = (e[:, rows_at(own_first, rows, rows)].astype(F32) * live).astype(BF)
    ysend[...] = dot(em[...], x[...], 1, 0).astype(ysend.dtype)
    reduce = [
        link.send(ysend.at[place(link.ahead(k), quarter), :], yrecv.at[k - 1], (link.dp, link.ahead(k)))
        for k in others
    ]
    biases = [link.send(bup, bup_all.at[link.tp], (link.dp, link.ahead(k))) for k in others]
    q[...] = (dot(x[...], wq[...], 1, 0) + vec[0:1, :]).astype(BF)
    own_slots = place(link.tp, quarter)
    for copy in reduce:
        copy.wait()
    own_y = ysend[own_slots, :].astype(F32)
    for k in others:
        own_y = own_y + yrecv[k - 1].astype(F32)
    yb[own_slots, :] = own_y.astype(BF)
    share = [
        link.send(yb.at[own_slots, :], yb.at[own_slots, :], (link.dp, link.ahead(k))) for k in others
    ]
    gathers = [WeightGather(link, "up", wup, wup_all), WeightGather(link, "down", wdn, wdn_all)]
    for k in others:
        for gather in gathers:
            gather.across(k)
    row_live = (lax.broadcasted_iota(jnp.int32, (total, 128), 0) < length).astype(F32).astype(BF)
    ssum[...] = dot(e[...], row_live, 1, 0)
    for copy in share:
        copy.wait()
    for copy in biases:
        copy.wait()

    lane = lax.broadcasted_iota(jnp.int32, (1, PAIR), 1)
    first_half = (lane < HEAD).astype(F32)

    def project(weight, bias_row, blocks):
        full = dot(yb[...], weight[...], 1, 0)
        for p in range(PAIRS):
            cols = slice(p * PAIR, (p + 1) * PAIR)
            part = full[:, cols] + ssum[...] * vec[bias_row : bias_row + 1, cols]
            blocks[p, 0:slots, :] = (part * first_half).astype(BF)
            blocks[p, slots : 2 * slots, :] = (part * (1.0 - first_half)).astype(BF)

    project(wk, 1, kb)
    project(wv, 2, vb)

    block = min(256, rows)

    def attend(step, carry):
        p = lax.div(step, rows // block)
        here = place(lax.rem(step, rows // block), block)
        cols = place(p, PAIR)
        logits = dot(q[here, cols], kb[p], 1, 1) * 0.125
        halves = []
        for half in range(2):
            part = logits[:, half * slots : (half + 1) * slots]
            peak = jnp.max(part, axis=-1, keepdims=True)
            raised = jnp.exp(part - peak)
            halves.append((raised * (1.0 / jnp.sum(raised, axis=-1, keepdims=True))).astype(BF))
        both = jnp.concatenate(halves, axis=1)
        probs[p, here, :] = both
        mixed[here, cols] = dot(both, vb[p], 1, 0).astype(BF)
        return carry

    def advance(*ks):
        for k in ks:
            for gather in gathers:
                gather.advance(k)

    per_pair = rows // block
    lax.fori_loop(0, 2 * per_pair, attend, 0)
    advance(1)
    lax.fori_loop(2 * per_pair, 4 * per_pair, attend, 0)
    advance(2, 1)
    lax.fori_loop(4 * per_pair, 6 * per_pair, attend, 0)
    advance(3, 2, 1)

    def finish(step, carry):
        here = place(step, block)
        res = x[here, :].astype(F32) + dot(mixed[here, :], wo[...], 1, 0) + vec[3:4, :]
        center = res - jnp.mean(res, axis=-1, keepdims=True)
        inverse = lax.rsqrt(jnp.mean(center * center, axis=-1, keepdims=True) + 1e-05)
        xhat[here, :] = center * inverse
        rstd[here, :] = jnp.broadcast_to(inverse, (block, 128))
        return carry

    lax.fori_loop(0, rows // block, finish, 0)
    advance(3, 2, 3, 1, 2, 3)
    own_up.wait()
    own_dn.wait()


def front(mesh, lengths, x, wq, wk, wv, wo, wup, wdn, e, vectors, b_up):
    dp_size, tp_size = mesh.shape["dp"], mesh.shape["tp"]
    rows, width = x.shape
    slots = e.shape[0]
    vmem = pl.BlockSpec(memory_space=pltpu.VMEM)
    hbm = pl.BlockSpec(memory_space=pltpu.HBM)
    shape = jax.ShapeDtypeStruct
    return pl.pallas_call(
        functools.partial(front_kernel, dp_size, tp_size),
        out_shape=(
            shape((VECTORS, width), F32),
            shape((rows, width), F32),
            shape((rows, 128), F32),
            shape((rows, width), BF),
            shape((rows, width), BF),
            shape((PAIRS, rows, 2 * slots), BF),
            shape((PAIRS, 2 * slots, PAIR), BF),
            shape((PAIRS, 2 * slots, PAIR), BF),
            shape((slots, width), BF),
            shape((slots, 128), F32),
            shape((slots, rows), BF),
            shape((tp_size, 8, width), F32),
            shape((tp_size, *wup.shape), BF),
            shape((tp_size, *wdn.shape), BF),
        ),
        in_specs=[pl.BlockSpec(memory_space=pltpu.SMEM)] + [vmem] * (9 + len(vectors)),
        out_specs=tuple([vmem] * 12 + [hbm] * 2),
        scratch_shapes=[
            pltpu.VMEM((8, width), F32),
            pltpu.VMEM((slots, width), BF),
            pltpu.VMEM((tp_size - 1, slots // tp_size, width), BF),
            pltpu.SemaphoreType.DMA((FRONT_SEMS,)),
            pltpu.SemaphoreType.DMA((FRONT_SEMS,)),
            pltpu.SemaphoreType.DMA((2,)),
        ],
        compiler_params=pltpu.CompilerParams(
            collective_id=0, has_side_effects=True, vmem_limit_bytes=VMEM_LIMIT
        ),
        name="front",
    )(lengths, x, wq, wk, wv, wo, wup, wdn, e, *vectors, b_up)


BACK_SEMS = 128
VECTORS = 16


def add_rows(target, first, left, left_first, right, count):
    block = 96 if count % 96 == 0 else (48 if count % 48 == 0 else (32 if count % 32 == 0 else count))

    def step(i, carry):
        at = i * block
        total = (
            left[rows_at(left_first + at, block, 16), :].astype(F32)
            + right[rows_at(at, block, 16), :].astype(F32)
        )
        target[rows_at(first + at, block, 16), :] = total.astype(target.dtype)
        return carry

    lax.fori_loop(0, count // block, step, 0)


class Spread:
    def __init__(self, link, order, rows, source, acc, landing):
        self.link, self.rows, self.source, self.acc, self.landing = link, rows, source, acc, landing
        self.order = [b for b in order if b < link.low]
        self.stages = len(self.order)
        self.slot = link.take(self.stages)
        self.piece = rows >> self.stages

    def inside(self, i):
        first = 0
        for j in range(1, i + 1):
            first = first + self.link.bit(self.order[j]) * (self.rows >> (j + 1))
        return first

    def kept(self):
        return rows_at(self.inside(self.stages - 1), self.piece, 16)

    def offset(self):
        return self.link.bit(self.order[0]) * (self.rows >> 1) + self.inside(self.stages - 1)

    def landed(self, i):
        first = sum(self.rows >> (j + 1) for j in range(i))
        return self.landing.at[pl.ds(first, self.rows >> (i + 1)), :]

    def copy(self, i):
        link, size = self.link, self.rows >> (i + 1)
        where, base = (self.source, 0) if i == 0 else (self.acc, self.inside(i - 1))
        other = base + (1 - link.bit(self.order[i])) * size
        return link.remote(
            self.slot + i, where.at[rows_at(other, size, 16), :], self.landed(i), link.partner(self.order[i])
        )

    def start(self, i):
        self.copy(i).start()

    def finish(self, i):
        size = self.rows >> (i + 1)
        self.copy(i).wait()
        if i == 0:
            add_rows(self.acc, 0, self.source, self.link.bit(self.order[0]) * size, self.landed(0), size)
        else:
            at = self.inside(i)
            add_rows(self.acc, at, self.acc, at, self.landed(i), size)

    def steps(self):
        yield lambda: self.start(0)
        for i in range(1, self.stages):

            def step(i=i):
                self.finish(i - 1)
                self.start(i)

            yield step


class Collect:
    def __init__(self, link, order, offset, piece, region):
        self.link, self.offset, self.piece, self.region = link, offset, piece, region
        self.order = [b for b in order if b < link.low][::-1]
        self.slot = link.take(len(self.order))

    def copy(self, i):
        size = self.piece << i
        first = self.offset()
        first = first - lax.rem(first, size)
        ref = self.region(first, size)
        return self.link.remote(self.slot + i, ref, ref, self.link.partner(self.order[i]))

    def steps(self):
        yield lambda: self.copy(0).start()
        for i in range(1, len(self.order)):

            def step(i=i):
                self.copy(i - 1).wait()
                self.copy(i).start()

            yield step
        yield lambda: self.copy(len(self.order) - 1).wait()


class Widen:
    def __init__(self, link, landing):
        self.link, self.landing = link, landing
        self.slot = link.take(max(0, link.bits - link.low))

    def run(self, piece):
        link = self.link
        for i, b in enumerate(range(link.low, link.bits)):
            copy = link.remote(self.slot + i, piece, self.landing.at[i], link.partner(b))
            copy.start()
            copy.wait()
            piece[...] = (piece[...].astype(F32) + self.landing[i].astype(F32)).astype(piece.dtype)


class Fan:
    def __init__(self, link, ends):
        self.link, self.ends = link, ends
        self.slot = link.take(link.tp_size - 1)

    def copy(self, k):
        source, target = self.ends(k)
        return self.link.remote(self.slot + k - 1, source, target, (self.link.dp, self.link.ahead(k)))

    def start(self):
        for k in range(1, self.link.tp_size):
            self.copy(k).start()

    def wait(self):
        for k in range(1, self.link.tp_size):
            self.copy(k).wait()


def then(*actions):
    def both():
        for action in actions:
            action()

    return both


class Track:
    def __init__(self):
        self.todo = []

    def add(self, steps, join=False):
        steps = list(steps)
        if join and self.todo:
            steps[0] = then(self.todo.pop(), steps[0])
        self.todo += steps

    def advance(self):
        if self.todo:
            self.todo.pop(0)()


def back_kernel(
    dp_size,
    tp_size,
    len_ref,
    vec,
    part_vec,
    xhat,
    rstd,
    mixed,
    wo,
    ff_pieces,
    dnorm,
    probs,
    x_hbm,
    q_hbm,
    kb_hbm,
    vb_hbm,
    yb_hbm,
    ssum_hbm,
    em_hbm,
    wq_hbm,
    wk_hbm,
    wv_hbm,
    grad_in,
    ff_out,
    gq_out,
    go_out,
    gkv_out,
    seq_out,
    vec_out,
    x,
    q,
    kb,
    vb,
    yb,
    ssum,
    em,
    wq,
    wk,
    wv,
    dres,
    dmix,
    dq,
    dl,
    prob_slots,
    dpart,
    dland,
    dfull,
    ff_zland,
    o_acc,
    o_land,
    q_acc,
    q_land,
    o_zland,
    q_zland,
    kv_send,
    kv_acc,
    kv_land,
    s_send,
    s_acc,
    s_land,
    vec_acc,
    vec_land,
    vec_z,
    wide_ff,
    wide_q,
    wide_kv,
    wide_s,
    send_sems,
    recv_sems,
    local_sems,
):
    link = Link(dp_size, tp_size, send_sems, recv_sems)
    rows, width = x.shape
    slots = yb.shape[0]
    low = link.low
    others = range(1, tp_size)
    first_load = pltpu.make_async_copy(dnorm, dres, local_sems.at[0])
    first_load.start()
    late = []
    for n, (source, target) in enumerate(
        (
            (q_hbm, q), (kb_hbm, kb), (vb_hbm, vb), (x_hbm, x), (yb_hbm, yb),
            (wq_hbm, wq), (wk_hbm, wk), (wv_hbm, wv), (ssum_hbm, ssum), (em_hbm, em),
        )
    ):
        late.append(pltpu.make_async_copy(source, target, local_sems.at[3 + n]))
        late[-1].start()
    link.greet(link.bits)

    lanes = 2
    deep = tp_size // lanes
    third = width // 3
    owned = width // tp_size

    ff_track, ff_orders = Track(), ((0, 1, 2), (0, 2, 1))
    ff_rows = ff_pieces.shape[2]
    ff_fans, ff_joins = [], []
    for m in range(2):

        def ends(k, m=m):
            return ff_pieces.at[m, link.ahead(k)], ff_zland.at[m, k - 1]

        def offset(m=m):
            first, size = 0, width >> 1
            for b in ff_orders[m]:
                if b < low:
                    first = first + link.bit(b) * size
                    size = size >> 1
            return first

        fan = Fan(link, ends)
        widen = Widen(link, wide_ff.at[m])

        def join(m=m, fan=fan, widen=widen, offset=offset):
            fan.wait()
            total = ff_pieces[m, link.tp].astype(F32)
            for k in others:
                total = total + ff_zland[m, k - 1].astype(F32)
            own = rows_at(offset(), ff_rows, 16)
            ff_out[m, own, :] = total.astype(BF)
            widen.run(ff_out.at[m, own, :])

        collect = Collect(
            link, ff_orders[m], offset, ff_rows,
            lambda first, size, m=m: ff_out.at[m, rows_at(first, size, 16), :],
        )
        ff_fans.append(fan)
        ff_joins.append((join, collect))
    for fan in ff_fans:
        fan.start()
    steps = [list(collect.steps()) for _, collect in ff_joins]
    ff_track.add([then(ff_joins[0][0], steps[0][0], ff_joins[1][0], steps[1][0])])
    ff_track.add([then(*pair) for pair in zip(steps[0][1:], steps[1][1:])])

    def square_track(order, out, acc, landing, zland, wide):
        track, spread = Track(), Spread(link, order, width, out, acc, landing)
        q_rows, q_cols = spread.piece // deep, width // lanes

        def quarter(first, t):
            return (
                rows_at(first + lax.div(t, lanes) * q_rows, q_rows, 16),
                pl.ds(pl.multiple_of(lax.rem(t, lanes) * q_cols, 128), q_cols),
            )

        def there(k):
            return acc.at[quarter(spread.inside(spread.stages - 1), link.ahead(k))], zland.at[k - 1]

        def again(k):
            region = out.at[quarter(spread.offset(), link.tp)]
            return region, region

        fan, share, widen = Fan(link, there), Fan(link, again), Widen(link, wide)

        def join():
            fan.wait()
            total = acc[quarter(spread.inside(spread.stages - 1), link.tp)].astype(F32)
            for k in others:
                total = total + zland[k - 1].astype(F32)
            mine = quarter(spread.offset(), link.tp)
            out[mine] = total.astype(BF)
            widen.run(out.at[mine])
            share.start()

        collect = Collect(
            link, order, spread.offset, spread.piece, lambda first, size: out.at[rows_at(first, size, 16), :]
        )
        track.add(spread.steps())
        track.add([then(lambda: spread.finish(spread.stages - 1), fan.start), join, share.wait])
        track.add(collect.steps(), join=True)
        return track

    def owned_track(order, total_rows, source, acc, landing, out, wide):
        track, spread = Track(), Spread(link, order, total_rows, source, acc, landing)

        def region(k):
            ref = out.at[link.tp, rows_at(spread.offset(), spread.piece, 16), :]
            return ref, ref

        share, widen = Fan(link, region), Widen(link, wide)

        def last():
            spread.finish(spread.stages - 1)
            ref = region(0)[0]
            ref[...] = acc[spread.kept(), :]
            widen.run(ref)
            share.start()

        collect = Collect(
            link, order, spread.offset, spread.piece, lambda first, size: out.at[:, rows_at(first, size, 16), :]
        )
        track.add(spread.steps())
        track.add([last, share.wait])
        track.add(collect.steps(), join=True)
        return track

    o_track = square_track((0, 1, 2), go_out, o_acc, o_land, o_zland, wide_q.at[0])
    q_track = square_track((0, 2, 1), gq_out, q_acc, q_land, q_zland, wide_q.at[1])
    kv_track = owned_track((0, 1, 2), 2 * owned, kv_send, kv_acc, kv_land, gkv_out, wide_kv)
    s_track = owned_track((0, 2, 1), slots, s_send, s_acc, s_land, seq_out, wide_s)

    vec_track, vec_slot = Track(), link.take(link.bits)
    vec_fan = Fan(link, lambda k: (vec_z.at[link.tp], vec_z.at[link.tp]))

    def vec_copy(b):
        return link.remote(vec_slot + b, vec_acc.at[b], vec_land.at[b], link.partner(b))

    vec_track.add([lambda: vec_copy(0).start()])
    for b in range(link.bits):

        def vec_step(b=b):
            vec_copy(b).wait()
            total = vec_acc[b] + vec_land[b]
            if b + 1 < link.bits:
                vec_acc[b + 1] = total
                vec_copy(b + 1).start()
            else:
                vec_z[link.tp] = total
                vec_fan.start()

        vec_track.add([vec_step])

    def vec_last():
        vec_fan.wait()
        total = vec_z[0]
        for t in range(1, tp_size):
            total = total + vec_z[t]
        vec_out[...] = total

    vec_track.add([vec_last])

    block = min(256, rows)
    count = rows // block
    gain = vec[4:5, :]

    def norm_back(step, carry):
        g_gain, g_shift, g_out = carry
        here = place(step, block)
        grad, hat = dres[here, :], xhat[here, :]
        g_gain = g_gain + jnp.sum(grad * hat, axis=0, keepdims=True)
        g_shift = g_shift + jnp.sum(grad, axis=0, keepdims=True)
        scaled = grad * gain
        d_res = rstd[here, 0:1] * (
            scaled
            - jnp.mean(scaled, axis=-1, keepdims=True)
            - hat * jnp.mean(scaled * hat, axis=-1, keepdims=True)
        )
        dres[here, :] = d_res
        d_attn = d_res.astype(BF)
        dq[here, :] = d_attn
        g_out = g_out + jnp.sum(d_attn.astype(F32), axis=0, keepdims=True)
        return g_gain, g_shift, g_out

    zero = jnp.zeros((1, width), F32)
    first_load.wait()
    g_gain, g_shift, g_out = lax.fori_loop(0, count, norm_back, (zero, zero, zero))
    vec_acc[0] = part_vec[...]
    vec_acc[0, 3:4, :] = g_out
    vec_acc[0, 4:5, :] = g_gain
    vec_acc[0, 5:6, :] = g_shift
    d_attn = dq

    def weight_grad(left, right, target):
        for m in range(3):
            cols = slice(m * third, (m + 1) * third)
            target[cols, :] = dot(left[:, cols], right[...], 0, 0).astype(BF)

    weight_grad(mixed, d_attn, go_out)
    o_track.advance()
    dmix[...] = dot(d_attn[...], wo[...], 1, 1).astype(BF)
    o_track.advance()
    for load in late:
        load.wait()

    own_half = lax.div(link.tp, 2)
    parity = lax.rem(link.tp, 2)
    three = PAIRS // 2

    def pair_at(n):
        second = lax.div(n, three)
        which = (1 - own_half) * (1 - second) + own_half * second
        return which * three + lax.rem(n, three)

    def fetch(n):
        slot = lax.rem(n, 2)
        return pltpu.make_async_copy(probs.at[pair_at(n)], prob_slots.at[slot], local_sems.at[1 + slot])

    fetch(0).start()

    def attend_back(n):
        p = pair_at(n)
        cols = place(p, PAIR)

        @pl.when(n + 1 < PAIRS)
        def _():
            fetch(n + 1).start()

        fetch(n).wait()
        held = prob_slots.at[lax.rem(n, 2)]

        def part(step, carry):
            here = place(step, block)
            d_probs = dot(dmix[here, cols], vb[p], 1, 1)
            weights = held[here, :].astype(F32)
            halves = []
            for h in range(2):
                w = weights[:, h * slots : (h + 1) * slots]
                d = d_probs[:, h * slots : (h + 1) * slots]
                halves.append((w * (d - jnp.sum(w * d, axis=-1, keepdims=True))).astype(BF))
            both = jnp.concatenate(halves, axis=1)
            dl[here, :] = both
            dq[here, cols] = (dot(both, kb[p], 1, 0) * 0.125).astype(BF)
            return carry

        lax.fori_loop(0, count, part, 0)
        top, under = rows_at(p * PAIR, HEAD, HEAD), rows_at(p * PAIR + HEAD, HEAD, HEAD)
        for n, total in enumerate(
            (dot(q[:, cols], dl[...], 0, 0) * 0.125, dot(dmix[:, cols], held[...], 0, 0))
        ):
            dpart[n, top, :] = total[:HEAD, :slots].astype(BF)
            dpart[n, under, :] = total[HEAD:, slots:].astype(BF)

    d_slot = link.take(tp_size - 1)

    def d_copy(j):
        near = 2 * own_half + (1 - parity)
        peer = near if j == 2 else 2 * (1 - own_half) + lax.rem(parity + j, 2)
        block_of = dpart.at[:, rows_at(peer * owned, owned, 64), :]
        return link.remote(d_slot + j, block_of, dland.at[j], (link.dp, peer))

    def far_blocks():
        d_copy(0).start()
        d_copy(1).start()

    events = [
        lambda: o_track.advance(),
        lambda: o_track.advance(),
        then(far_blocks, ff_track.advance, o_track.advance),
        then(ff_track.advance, o_track.advance),
        then(ff_track.advance, o_track.advance),
        then(lambda: d_copy(2).start(), ff_track.advance, o_track.advance),
    ]

    def one(n, carry):
        attend_back(n)
        for i, event in enumerate(events):
            pl.when(n == i)(event)
        return carry

    lax.fori_loop(0, PAIRS, one, 0)

    weight_grad(x, dq, gq_out)
    q_track.advance()

    for j in range(tp_size - 1):
        d_copy(j).wait()
    own_block = rows_at(link.tp * owned, owned, 64)
    for n in range(2):
        total = dpart[n, own_block, :].astype(F32)
        for j in range(tp_size - 1):
            total = total + dland[j, n].astype(F32)
        dfull[n, own_block, :] = total.astype(BF)
    d_share = Fan(link, lambda k: (dfull.at[:, own_block, :], dfull.at[:, own_block, :]))
    d_share.start()
    q_track.advance()
    for n in range(2):
        kv_send[n * owned : (n + 1) * owned, :] = dot(dfull[n, own_block, :], yb[...], 1, 0).astype(BF)
    kv_track.advance()
    vec_acc[0, 0:1, :] = jnp.sum(dq[...].astype(F32), axis=0, keepdims=True)

    def input_grad(step, carry):
        here = place(step, block)
        dres[here, :] += dot(dq[here, :], wq[...], 1, 1)
        return carry

    lax.fori_loop(0, count, input_grad, 0)
    kv_track.advance()
    q_track.advance()
    o_track.advance()
    kv_track.advance()
    d_share.wait()
    backs = dot(wk[...], dfull[0], 1, 0) + dot(wv[...], dfull[1], 1, 0)
    back = backs.T.astype(BF)
    small = vec[0:8, :].astype(BF)
    bias_row = dot(small, dfull[0], 1, 0)[1:2, :] + dot(small, dfull[1], 1, 0)[2:3, :]
    bias_column = jnp.broadcast_to(bias_row, (128, slots)).T[:, 0:1]
    position = lax.broadcasted_iota(jnp.int32, (1, rows), 1) + link.tp * rows
    live = (position < len_ref[0]).astype(F32)
    s_send[...] = ((dot(back, x[...], 1, 1) + bias_column) * live).astype(BF)
    s_track.advance()
    column = ssum[...].T[0:8, :]
    column_b = column.astype(BF)
    column_low = (column - column_b.astype(F32)).astype(BF)
    for n in range(2):
        total = dot(column_b, dfull[n], 1, 1) + dot(column_low, dfull[n], 1, 1)
        vec_acc[0, 1 + n : 2 + n, :] = total[0:1, :] * (1.0 / tp_size)
    vec_track.advance()
    s_track.advance()
    kv_track.advance()

    def input_grad_last(step, carry):
        here = place(step, block)
        grad_in[here, :] = (dres[here, :] + dot(em[:, here], back, 0, 0)).astype(BF)
        return carry

    lax.fori_loop(0, count, input_grad_last, 0)
    tracks = [s_track, kv_track, q_track, vec_track, ff_track, o_track]
    while any(track.todo for track in tracks):
        for track in tracks:
            track.advance()


def back(mesh, lengths, vec, part_vec, xhat, rstd, mixed, wo, ff_pieces, dnorm, probs, *late):
    dp_size, tp_size = mesh.shape["dp"], mesh.shape["tp"]
    bits = dp_size.bit_length() - 1
    low = min(3, bits)
    wide = max(1, bits - low)
    rows, width = xhat.shape
    slots = late[4].shape[0]
    owned = width // tp_size
    others = tp_size - 1
    vmem = pl.BlockSpec(memory_space=pltpu.VMEM)
    hbm = pl.BlockSpec(memory_space=pltpu.HBM)
    shape = jax.ShapeDtypeStruct

    def landing(total):
        return sum(total >> (i + 1) for i in range(low))

    def buf(*dims, dtype=BF):
        return pltpu.VMEM(dims, dtype)

    ff_piece, kv_piece, s_piece = width >> low, 2 * owned >> low, slots >> low
    quarter = (ff_piece // (tp_size // 2), width // 2)
    return pl.pallas_call(
        functools.partial(back_kernel, dp_size, tp_size),
        out_shape=(
            shape((rows, width), BF),
            shape((2, width, width), BF),
            shape((width, width), BF),
            shape((width, width), BF),
            shape((tp_size, 2 * owned, width), BF),
            shape((tp_size, slots, rows), BF),
            shape((VECTORS, width), F32),
        ),
        in_specs=[pl.BlockSpec(memory_space=pltpu.SMEM)] + [vmem] * 7 + [hbm] * (2 + len(late)),
        out_specs=tuple([vmem] * 7),
        scratch_shapes=[pltpu.VMEM(array.shape, array.dtype) for array in late]
        + [
            buf(rows, width, dtype=F32),
            buf(rows, width),
            buf(rows, width),
            buf(rows, 2 * slots),
            buf(2, rows, 2 * slots),
            buf(2, width, slots),
            buf(others, 2, owned, slots),
            buf(2, width, slots),
            buf(2, others, ff_piece, width),
            buf(width // 2, width),
            buf(landing(width), width),
            buf(width // 2, width),
            buf(landing(width), width),
            buf(others, *quarter),
            buf(others, *quarter),
            buf(2 * owned, width),
            buf(owned, width),
            buf(landing(2 * owned), width),
            buf(slots, rows),
            buf(slots // 2, rows),
            buf(landing(slots), rows),
            buf(bits, VECTORS, width, dtype=F32),
            buf(bits, VECTORS, width, dtype=F32),
            buf(tp_size, VECTORS, width, dtype=F32),
            buf(2, wide, ff_piece, width),
            buf(2, wide, *quarter),
            buf(wide, kv_piece, width),
            buf(wide, s_piece, rows),
            pltpu.SemaphoreType.DMA((BACK_SEMS,)),
            pltpu.SemaphoreType.DMA((BACK_SEMS,)),
            pltpu.SemaphoreType.DMA((3 + len(late),)),
        ],
        compiler_params=pltpu.CompilerParams(
            collective_id=1, has_side_effects=True, vmem_limit_bytes=VMEM_LIMIT
        ),
        name="back",
    )(lengths, vec, part_vec, xhat, rstd, mixed, wo, ff_pieces, dnorm, probs, *late)


class ChunkSpread:
    def __init__(self, link, rows, sent, acc, landing):
        self.link, self.rows, self.sent, self.acc, self.landing = link, rows, sent, acc, landing
        self.orders = [[b for b in order if b < link.low] for order in ((0, 1, 2), (0, 2, 1))]
        self.stages = link.low

    def inside(self, m, i):
        first = 0
        for j in range(1, i + 1):
            first = first + self.link.bit(self.orders[m][j]) * (self.rows >> (j + 1))
        return first

    def copy(self, c, m, i):
        link, size = self.link, self.rows >> (i + 1)
        bit = self.orders[m][i]
        if i == 0:
            source = self.sent.at[m, lax.rem(c, 2), rows_at((1 - link.bit(bit)) * size, size, 16), :]
        else:
            source = self.acc.at[m, c, rows_at(self.inside(m, i - 1) + (1 - link.bit(bit)) * size, size, 16), :]
        first = sum(self.rows >> (j + 1) for j in range(i))
        slot = (i * 2 + m) * self.acc.shape[1] + c
        return link.remote(slot, source, self.landing.at[m, c, pl.ds(first, size), :], link.partner(bit))

    def start(self, c, m, i):
        self.copy(c, m, i).start()

    def finish(self, c, m, i):
        size = self.rows >> (i + 1)
        self.copy(c, m, i).wait()
        first = sum(self.rows >> (j + 1) for j in range(i))
        landed = self.landing.at[m, c, pl.ds(first, size), :]
        acc = self.acc.at[m, c]
        if i == 0:
            mine = self.link.bit(self.orders[m][0]) * size
            add_rows(acc, 0, self.sent.at[m, lax.rem(c, 2)], mine, landed, size)
        else:
            at = self.inside(m, i)
            add_rows(acc, at, acc, at, landed, size)
        if i + 1 < self.stages:
            self.start(c, m, i + 1)


def middle_kernel(
    dp_size,
    tp_size,
    vec,
    bup_all,
    xhat,
    out_grad,
    wup_all,
    wdn_all,
    layer_out,
    dnorm,
    part_vec,
    ff_pieces,
    wup,
    wdn,
    nb,
    act,
    slope,
    d_branch,
    d_acc,
    sent,
    acc,
    landing,
    send_sems,
    recv_sems,
    local_sems,
):
    link = Link(dp_size, tp_size, send_sems, recv_sems)
    rows, width = xhat.shape
    loads = []
    for c in range(tp_size):
        for n, (source, target) in enumerate(((wup_all, wup), (wdn_all, wdn))):
            loads.append(pltpu.make_async_copy(source.at[c], target.at[c], local_sems.at[n * tp_size + c]))
            loads[-1].start()
    barrier = pltpu.get_barrier_semaphore()
    for b in range(link.low):
        pl.semaphore_signal(barrier, inc=1, device_id=link.partner(b), device_id_type=MESH)
    pl.semaphore_wait(barrier, link.low)
    gain, shift, b_down, f_gain, f_shift = (vec[n : n + 1, :] for n in (4, 5, 6, 7, 8))
    block = min(256, rows)
    count = rows // block
    big = min(512, rows)

    def norm(step, carry):
        here = place(step, block)
        nb[here, :] = (xhat[here, :] * gain + shift).astype(BF)
        return carry

    lax.fori_loop(0, count, norm, 0)
    for load in loads:
        load.wait()

    per_chunk = rows // big

    def forward(step, carry):
        c = lax.div(step, per_chunk)
        here, cols = place(lax.rem(step, per_chunk), big), place(c, width)
        pre = dot(nb[here, :], wup[c], 1, 0) + bup_all[c, 0:1, :]
        cdf = 0.5 * (1.0 + lax.erf(pre * 0.7071067811865476))
        act[here, cols] = (pre * cdf).astype(BF)
        slope[here, cols] = (cdf + pre * (jnp.exp(pre * pre * -0.5) * 0.3989422804014327)).astype(BF)
        return carry

    lax.fori_loop(0, tp_size * per_chunk, forward, 0)

    def second_norm(step, carry):
        g_gain, g_shift, g_down = carry
        here = place(step, block)
        branch = dot(act[here, 0:width], wdn[0], 1, 0)
        for c in range(1, tp_size):
            branch = branch + dot(act[here, c * width : (c + 1) * width], wdn[c], 1, 0)
        res = xhat[here, :] * gain + shift + (branch + b_down)
        center = res - jnp.mean(res, axis=-1, keepdims=True)
        inverse = lax.rsqrt(jnp.mean(center * center, axis=-1, keepdims=True) + 1e-05)
        hat = center * inverse
        layer_out[here, :] = (hat * f_gain + f_shift).astype(BF)
        grad = out_grad[here, :].astype(F32)
        g_gain = g_gain + jnp.sum(grad * hat, axis=0, keepdims=True)
        g_shift = g_shift + jnp.sum(grad, axis=0, keepdims=True)
        scaled = grad * f_gain
        d_res = inverse * (
            scaled
            - jnp.mean(scaled, axis=-1, keepdims=True)
            - hat * jnp.mean(scaled * hat, axis=-1, keepdims=True)
        )
        d_acc[here, :] = d_res
        rounded = d_res.astype(BF)
        d_branch[here, :] = rounded
        g_down = g_down + jnp.sum(rounded.astype(F32), axis=0, keepdims=True)
        return g_gain, g_shift, g_down

    zero = jnp.zeros((1, width), F32)
    g_gain, g_shift, g_down = lax.fori_loop(0, count, second_norm, (zero, zero, zero))
    part_vec[...] = jnp.zeros_like(part_vec)
    part_vec[6:7, :] = g_gain
    part_vec[7:8, :] = g_shift
    part_vec[8:9, :] = g_down

    spread = ChunkSpread(link, width, sent, acc, landing)
    third = width // 3

    def weight_grad(left, first, right, cols, target):
        for m in range(3):
            mine = pl.ds(pl.multiple_of(first + m * third, third), third)
            target[m * third : (m + 1) * third, :] = dot(left[:, mine], right[:, cols], 0, 0).astype(BF)

    def backward(c, carry):
        cols = place(c, width)
        slot = lax.rem(c, 2)
        weight_grad(act, c * width, d_branch, slice(0, width), sent.at[1, slot])
        spread.start(c, 1, 0)

        def through(step, total):
            here = place(step, big)
            grad = (dot(d_branch[here, :], wdn[c], 1, 1) * slope[here, cols].astype(F32)).astype(BF)
            slope[here, cols] = grad
            return total + jnp.sum(grad.astype(F32), axis=0, keepdims=True)

        part_vec[pl.ds(9 + c, 1), :] = lax.fori_loop(0, rows // big, through, zero)
        weight_grad(nb, 0, slope, cols, sent.at[0, slot])
        spread.start(c, 0, 0)
        for back_by in range(1, spread.stages + 1):

            @pl.when(c >= back_by)
            def _():
                for m in (1, 0):
                    spread.finish(c - back_by, m, back_by - 1)

        return carry

    lax.fori_loop(0, tp_size, backward, 0)

    def input_grad(step, carry):
        here = place(step, big)
        total = d_acc[here, :]
        for c in range(tp_size):
            total = total + dot(slope[here, c * width : (c + 1) * width], wup[c], 1, 1)
        d_acc[here, :] = total
        return carry

    half = rows // big // 2
    lax.fori_loop(0, half, input_grad, 0)
    for c in range(max(0, tp_size - spread.stages), tp_size):
        stage = tp_size - 1 - c
        for m in (1, 0):
            spread.finish(c, m, stage)
    lax.fori_loop(half, rows // big, input_grad, 0)
    store = pltpu.make_async_copy(d_acc, dnorm, local_sems.at[2 * tp_size])
    store.start()
    for late in range(1, spread.stages):
        for c in range(max(0, tp_size - spread.stages) + late, tp_size):
            stage = tp_size - 1 - c + late
            for m in (1, 0):
                spread.finish(c, m, stage)
    piece = width >> spread.stages
    for m in range(2):
        at = spread.inside(m, spread.stages - 1)
        for c in range(tp_size):
            ff_pieces[m, c] = acc[m, c, rows_at(at, piece, 16), :]
    store.wait()


def middle(mesh, vec, bup_all, xhat, out_grad, wup_all, wdn_all):
    dp_size, tp_size = mesh.shape["dp"], mesh.shape["tp"]
    low = min(3, dp_size.bit_length() - 1)
    rows, width = xhat.shape
    hidden = tp_size * width
    vmem = pl.BlockSpec(memory_space=pltpu.VMEM)
    hbm = pl.BlockSpec(memory_space=pltpu.HBM)
    shape = jax.ShapeDtypeStruct

    def buf(*dims, dtype=BF):
        return pltpu.VMEM(dims, dtype)

    sems = 2 * low * tp_size
    return pl.pallas_call(
        functools.partial(middle_kernel, dp_size, tp_size),
        out_shape=(
            shape((rows, width), BF),
            shape((rows, width), F32),
            shape((VECTORS, width), F32),
            shape((2, tp_size, width >> low, width), BF),
        ),
        in_specs=[vmem] * 4 + [hbm] * 2,
        out_specs=(vmem, hbm, vmem, vmem),
        scratch_shapes=[
            buf(tp_size, width, width),
            buf(tp_size, width, width),
            buf(rows, width),
            buf(rows, hidden),
            buf(rows, hidden),
            buf(rows, width),
            buf(rows, width, dtype=F32),
            buf(2, 2, width, width),
            buf(2, tp_size, width // 2, width),
            buf(2, tp_size, sum(width >> (i + 1) for i in range(low)), width),
            pltpu.SemaphoreType.DMA((sems,)),
            pltpu.SemaphoreType.DMA((sems,)),
            pltpu.SemaphoreType.DMA((2 * tp_size + 1,)),
        ],
        compiler_params=pltpu.CompilerParams(
            collective_id=2, has_side_effects=True, vmem_limit_bytes=VMEM_LIMIT
        ),
        name="middle",
    )(vec, bup_all, xhat, out_grad, wup_all, wdn_all)


def finish_kernel(
    tp_size, ff, gq, go, gkv, seq, vec, layer_out, grad_in,
    o_up, o_dn, o_q, o_o, o_k, o_v, o_seq, o_layer, o_grad, *rest,
):
    vectors, (in_up, in_dn, in_q, in_o, in_kv, in_seq, f_up, f_dn, f_q, f_o, f_k, f_v, f_seq, turn, pass_a, pass_b, in_sems, out_sems) = rest[:10], rest[10:]
    pairs = [(gq, in_q), (go, in_o), (ff.at[0], in_up), (ff.at[1], in_dn), (gkv, in_kv), (seq, in_seq), (layer_out, pass_a), (grad_in, pass_b)]
    loads = []
    for n, (source, target) in enumerate(pairs):
        loads.append(pltpu.make_async_copy(source, target, in_sems.at[n]))
        loads[-1].start()
    stores = []

    def put(staged, out):
        copy = pltpu.make_async_copy(staged, out, out_sems.at[len(stores)])
        copy.start()
        stores.append(copy)

    for n, (held, out) in enumerate(((pass_a, o_layer), (pass_b, o_grad))):
        loads[6 + n].wait()
        put(held, out)
    for n, row in enumerate((0, 1, 2, 3, 4, 5, 6, 7, 8)):
        vectors[n][...] = vec[row, :]
    vectors[9][...] = vec[pl.ds(9 + lax.axis_index("tp"), 1), :][0]
    width = gq.shape[0]
    for n, (narrow, wide, out) in enumerate(
        ((in_q, f_q, o_q), (in_o, f_o, o_o), (in_up, f_up, o_up), (in_dn, f_dn, o_dn))
    ):
        loads[n].wait()
        wide[...] = narrow[...].astype(F32)
        put(wide, out)
    loads[4].wait()
    owned = width // tp_size
    for n, (wide, out) in enumerate(((f_k, o_k), (f_v, o_v))):
        for c in range(tp_size):
            turn[c * owned : (c + 1) * owned, :] = in_kv[c, n * owned : (n + 1) * owned, :]
        for c in range(3):
            cols = slice(c * (width // 3), (c + 1) * (width // 3))
            wide[:, cols] = turn[cols, :].astype(F32).T
        put(wide, out)
    loads[5].wait()
    rows = in_seq.shape[2]
    for c in range(tp_size):
        f_seq[:, c * rows : (c + 1) * rows] = in_seq[c].astype(F32)
    put(f_seq, o_seq)
    for copy in stores:
        copy.wait()


def finish(tp_size, ff, gq, go, gkv, seq, vec, layer_out, grad_in):
    width = gq.shape[0]
    _, slots, rows = seq.shape
    square, flat = (width, width), (slots, tp_size * rows)
    vmem = pl.BlockSpec(memory_space=pltpu.VMEM)
    hbm = pl.BlockSpec(memory_space=pltpu.HBM)
    shape = jax.ShapeDtypeStruct
    return pl.pallas_call(
        functools.partial(finish_kernel, tp_size),
        out_shape=tuple([shape(square, F32)] * 6 + [shape(flat, F32)] + [shape(layer_out.shape, BF)] * 2 + [shape((width,), F32)] * 10),
        in_specs=[hbm] * 5 + [vmem] + [hbm] * 2,
        out_specs=tuple([hbm] * 9 + [vmem] * 10),
        scratch_shapes=[pltpu.VMEM(square, BF)] * 4
        + [pltpu.VMEM(gkv.shape, BF), pltpu.VMEM(seq.shape, BF)]
        + [pltpu.VMEM(square, F32)] * 6
        + [pltpu.VMEM(flat, F32), pltpu.VMEM(square, BF)]
        + [pltpu.VMEM(layer_out.shape, BF)] * 2
        + [pltpu.SemaphoreType.DMA((8,)), pltpu.SemaphoreType.DMA((9,))],
        compiler_params=pltpu.CompilerParams(vmem_limit_bytes=VMEM_LIMIT),
        name="finish",
    )(ff, gq, go, gkv, seq, vec, layer_out, grad_in)


def on_device(
    mesh,
    layer_in,
    out_grad,
    lengths,
    w_query,
    b_query,
    w_key,
    b_key,
    w_value,
    b_value,
    w_out,
    b_out,
    seq_proj,
    attn_gain,
    attn_shift,
    w_up,
    b_up,
    w_down,
    b_down,
    ffn_gain,
    ffn_shift,
):
    row_count, width = layer_in.shape
    tp_size = mesh.shape["tp"]
    vectors = (b_query, b_key, b_value, b_out, attn_gain, attn_shift, b_down, ffn_gain, ffn_shift)
    vec, xhat, rstd, mixed, queries, probs, kb, vb, folded, ssum, own_proj, bup_all, up_all, down_all = front(
        mesh, lengths, layer_in, w_query, w_key, w_value, w_out, w_up, w_down, seq_proj, vectors, b_up
    )
    layer_out, d_normed, part_vec, ff_pieces = middle(mesh, vec, bup_all, xhat, out_grad, up_all, down_all)
    grad_in, g_ff, g_q, g_o, g_kv, g_seq, vec_sum = back(
        mesh, lengths, vec, part_vec, xhat, rstd, mixed, w_out, ff_pieces, d_normed, probs,
        layer_in, queries, kb, vb, folded, ssum, own_proj, w_query, w_key, w_value
    )
    (
        g_w_up, g_w_down, g_w_query, g_w_out, g_w_key, g_w_value, g_seq_proj, layer_out, grad_in,
        g_b_query, g_b_key, g_b_value, g_b_out, g_attn_gain, g_attn_shift, g_ffn_gain, g_ffn_shift, g_b_down, g_b_up,
    ) = finish(tp_size, g_ff, g_q, g_o, g_kv, g_seq, vec_sum, layer_out, grad_in)
    return (
        layer_out,
        grad_in,
        g_w_query,
        g_b_query,
        g_w_key,
        g_b_key,
        g_w_value,
        g_b_value,
        g_w_out,
        g_b_out,
        g_seq_proj,
        g_attn_gain,
        g_attn_shift,
        g_w_up,
        g_b_up,
        g_w_down,
        g_b_down,
        g_ffn_gain,
        g_ffn_shift,
    )


def solution(mesh):
    in_specs = (
        P(("dp", "tp"), None),
        P(("dp", "tp"), None),
        P("dp"),
        *([P()] * 11),
        P(None, "tp"),
        P("tp"),
        P("tp", None),
        P(),
        P(),
        P(),
    )
    out_specs = (
        P(("dp", "tp"), None),
        P(("dp", "tp"), None),
        *([P()] * 11),
        P(None, "tp"),
        P("tp"),
        P("tp", None),
        P(),
        P(),
        P(),
    )
    return jax.shard_map(
        functools.partial(on_device, mesh), mesh=mesh, in_specs=in_specs, out_specs=out_specs, check_vma=False
    )
```

time: 381 us -> 331 us (0.87)
  Pallas kernels: 271 us -> 328 us
  matrix products: 50.8 us -> 0 us
  other arithmetic: 39.5 us -> 0 us
  local copies, waits for them, and re-layouts: 14.3 us -> 0 us
    pallas_call x0 -> x1, Pallas kernels: none -> 79.9 us  [middle(): pl.pallas_call(functools.partial(middle_kernel, dp_size, tp_size), out_sh...]
    dot_general x15 -> x0, matrix products: 50.8 us -> none  [dot(): lax.dot_general(left, right, (((left_dim,), (right_dim,)), ((), ())), pre...]
    convert_element_type x8 -> x0, other arithmetic: 32 us -> none  [the longest x1 27.5 us: on_device(): hidden_b = hidden_act.astype(BF)]
    pallas_call x1, Pallas kernels: 175 us -> 149 us  [back(): pl.pallas_call(functools.partial(back_kernel, dp_size, tp_size), out_shap...]
    another operation x20 -> x0, local copies, waits for them, and re-layouts: 7.58 us -> none  [the longest x10 6.26 us: on_device(): jnp.stack([b_query, b_key, b_value, b_out, attn_gain, attn_shift, b_down,...]
    reduce_sum x4 -> x0, other arithmetic: 4.74 us -> none  [the longest x1 2.59 us: layer_norm(): center = hidden - jnp.mean(hidden, axis=-1, keepdims=True)]
    unnamed x31 -> x0, local copies, waits for them, and re-layouts: 4.43 us -> none
where the time goes in v3:
time: 331 us; the launch traced here: 330 us
  Pallas kernels  328 us (99%)
    pallas_call x1, Pallas kernels, back(): pl.pallas_call(functools.partial(back_kernel, dp_size, tp_size), out_shap...  149 us
    pallas_call x1, Pallas kernels, front(): pl.pallas_call(functools.partial(front_kernel, dp_size, tp_size), out_sha...  85.6 us
    pallas_call x1, Pallas kernels, middle(): pl.pallas_call(functools.partial(middle_kernel, dp_size, tp_size), out_sh...  79.9 us
    pallas_call x1, Pallas kernels, finish(): pl.pallas_call(functools.partial(finish_kernel, tp_size), out_shape=tuple...  13.1 us

profile of v3, /device:TPU:0, one launch (start us, length us, event | category | flops | bytes accessed | tf_op | source)
XLA Modules:
  0.0 329.6 jit_solution(4770373017360669531)
XLA Ops:
  1.3 85.6 %front.1 = (f32[16,768]{1,0:T(8,128)}, f32[1024,768]{1,0:T(8,128)}, f32[1024,128]{1,0:T(8,128)}, bf16[1024,768]{1,0:T(8,128)(2,1)}, bf16[1024,768]{1,0:T(8,128)(...) custom-call(s32[1]{0:T(128)S(6)} %copy.39.len_ref, ...), custom_call_target="tpu_custom_call" | custom-call | tf_op jit(solution)/shard_map/front/pallas_call | solution.py:299
  87.0 79.9 %middle.1 = (bf16[1024,768]{1,0:T(8,128)(2,1)}, f32[1024,768]{1,0:T(8,128)}, f32[16,768]{1,0:T(8,128)}, bf16[2,4,96,768]{3,2,1,0:T(8,128)(2,1)}) custom-call(f32[16,768]{1,0:T(8,128)} %get-tuple-element.63.vec, f32[4,8,768]{2,1,0:T(8,128)} %get-tuple-element.64.bup_all, f32[1024,768]{1,0:T(8,128)} %get-tuple-element.65.xhat, bf16[1024,768]{1,0:T(8,128)(2,1)} %out_grad.1, ...), custom_call_target="tpu_custom_call" | custom-call | tf_op jit(solution)/shard_map/middle/pallas_call | solution.py:1192
  166.8 149.5 %back.1 = (bf16[1024,768]{1,0:T(8,128)(2,1)}, bf16[2,768,768]{2,1,0:T(8,128)(2,1)}, bf16[768,768]{1,0:T(8,128)(2,1)}, bf16[768,768]{1,0:T(8,128)(2,1)}, bf16[4,3...) custom-call(s32[1]{0:T(128)S(6)} %copy.39.len_ref, f32[16,768]{1,0:T(8,128)} %get-tuple-element.63.vec, ...), custom_call_target="tpu_custom_call" | custom-call | tf_op jit(solution)/shard_map/back/pallas_call | solution.py:921
  316.3 13.1 %finish.1 = (f32[768,768]{1,0:T(8,128)}, f32[768,768]{1,0:T(8,128)}, f32[768,768]{1,0:T(8,128)}, f32[768,768]{1,0:T(8,128)}, f32[768,768]{1,0:T(8,128)}, /*index...) custom-call(bf16[2,768,768]{2,1,0:T(8,128)(2,1)} %get-tuple-element., ...), custom_call_target="tpu_custom_call" | custom-call | tf_op jit(solution)/shard_map/finish/pallas_call | solution.py:1279

commit v4 on v3

--- a/solution.py
+++ b/solution.py
@@ -86,128 +86,127 @@
 VECTORS = 16
 
 
-def gather_order(name):
-    return (1, 2, 0) if name == "up" else (2, 1, 0)
-
-
-class WeightGather:
-    def __init__(self, link, name, shard, whole):
-        self.link, self.shard, self.whole = link, shard, whole
-        self.rows = shard.shape[0]
-        self.order = [b for b in gather_order(name) if b < link.low]
-        self.piece = self.rows >> len(self.order)
-        offset, size = 0, self.piece
-        for b in self.order:
-            offset = offset + link.bit(b) * size
-            size *= 2
-        self.offset = offset
-        self.step = {}
-        self.waiting = {}
-
-    def across(self, k):
-        link = self.link
-        rows = rows_at(self.offset, self.piece, self.piece)
-        self.waiting[k] = link.send(
-            self.shard.at[rows, :], self.whole.at[link.tp, rows, :], (link.dp, link.ahead(k))
-        )
-        self.step[k] = 0
-
-    def advance(self, k):
-        link, done = self.link, self.step[k]
-        if done > len(self.order):
-            return
-        self.waiting[k].wait()
-        self.step[k] = done + 1
-        if done == len(self.order):
-            return
-        size = self.piece << done
-        first = self.offset - lax.rem(self.offset, size)
-        rows = rows_at(first, size, self.piece)
-        region = self.whole.at[link.behind(k), rows, :]
-        self.waiting[k] = link.send(region, region, link.partner(self.order[done]))
-
-
-def front_kernel(
-    dp_size,
-    tp_size,
-    len_ref,
-    x,
-    wq,
-    wk,
-    wv,
-    wo,
-    wup,
-    wdn,
-    e,
-    *rest,
-):
-    names, b_up, rest = rest[:9], rest[9], rest[10:]
-    front_body(dp_size, tp_size, len_ref, x, wq, wk, wv, wo, wup, wdn, e, names, b_up, *rest)
-
-
-def front_body(
-    dp_size,
-    tp_size,
-    len_ref,
-    x,
-    wq,
-    wk,
-    wv,
-    wo,
-    wup,
-    wdn,
-    e,
-    vectors,
-    b_up,
-    vec,
-    xhat,
-    rstd,
-    mixed,
-    q,
-    probs,
-    kb,
-    vb,
-    yb,
-    ssum,
-    em,
-    bup_all,
-    wup_all,
-    wdn_all,
-    bup,
-    ysend,
-    yrecv,
-    send_sems,
-    recv_sems,
-    local_sems,
-):
+def half_orders(low):
+    return [[b for b in order if b < low] for order in ((1, 2, 0), (2, 1, 0))]
+
+
+def half_offset(link, order, piece):
+    first, size = 0, piece
+    for b in order:
+        first = first + link.bit(b) * size
+        size *= 2
+    return first
+
+
+class WeightCollect:
+    def __init__(self, link, part, whole):
+        self.link, self.whole, self.part = link, whole, part
+        self.orders = half_orders(link.low)
+        self.piece = self.part >> link.low
+        self.stages = link.low
+        self.slot = link.take(2 * (link.tp_size - 1) * link.low)
+
+    def rows(self, h, i):
+        size = self.piece << i
+        first = half_offset(self.link, self.orders[h], self.piece)
+        return rows_at(h * self.part + first - lax.rem(first, size), size, 16)
+
+    def copies(self, k, i):
+        for h in range(2):
+            region = self.whole(k).at[self.rows(h, i), :]
+            slot = self.slot + ((k - 1) * self.stages + i) * 2 + h
+            yield self.link.remote(slot, region, region, self.link.partner(self.orders[h][i]))
+
+    def step(self, k, j):
+        if j > 0:
+            for copy in self.copies(k, j - 1):
+                copy.wait()
+        if j < self.stages:
+            for copy in self.copies(k, j):
+                copy.start()
+
+
+class Cross:
+    def __init__(self, link, collect, shard):
+        self.link, self.collect, self.shard = link, collect, shard
+        self.slot = link.take(2 * (link.tp_size - 1))
+
+    def copies(self, k):
+        for h in range(2):
+            rows = self.collect.rows(h, 0)
+            yield self.link.remote(
+                self.slot + 2 * (k - 1) + h,
+                self.shard.at[rows, :],
+                self.collect.whole(k).at[rows, :],
+                (self.link.dp, self.link.ahead(k)),
+            )
+
+    def start(self, k):
+        for copy in self.copies(k):
+            copy.start()
+
+    def wait(self, k):
+        for copy in self.copies(k):
+            copy.wait()
+
+
+FRONT_TICKS = (
+    ((3, 0),),
+    (),
+    ((3, 1),),
+    (),
+    ((3, 2),),
+    (),
+    ((3, 3),),
+)
+
+
+def front_kernel(dp_size, tp_size, n_vectors, len_ref, x, wq, e, wk_hbm, wv_hbm, wo_hbm, wup, *rest):
+    vectors, b_up, rest = rest[:n_vectors], rest[n_vectors], rest[n_vectors + 1 :]
+    outs, scratch = rest[:13], rest[13:]
+    (vec, xhat, rstd, bup_all, mixed_out, q_out, probs_out, kb_out, vb_out, yb_out, ssum_out, em_out, ups) = outs
+    (wk, wv, wo, e_all, mixed, q, probs, kb, vb, yb, ssum, em, bup, ysend, yrecv, send_sems, recv_sems, local_sems) = scratch
     link = Link(dp_size, tp_size, send_sems, recv_sems)
     rows, width = x.shape
-    slots, total = e.shape
+    slots, total = e_all.shape
     quarter = slots // tp_size
     others = range(1, tp_size)
+    used = [0]
+
+    def local(source, target):
+        copy = pltpu.make_async_copy(source, target, local_sems.at[used[0]])
+        used[0] += 1
+        copy.start()
+        return copy
+
+    own_first = link.tp * rows
+    e_own = local(e.at[:, rows_at(own_first, rows, rows)], em)
+    late = [local(e, e_all), local(wk_hbm, wk), local(wv_hbm, wv), local(wo_hbm, wo)]
     link.greet(link.low)
 
-    own_up = pltpu.make_async_copy(wup, wup_all.at[link.tp], local_sems.at[0])
-    own_dn = pltpu.make_async_copy(wdn, wdn_all.at[link.tp], local_sems.at[1])
-    own_up.start()
-    own_dn.start()
+    collect = WeightCollect(link, wup.shape[0] // 2, lambda k: ups.at[k - 1])
+    cross = Cross(link, collect, wup)
+    cross.start(1)
     vec[...] = jnp.zeros_like(vec)
     for n, vector in enumerate(vectors):
         vec[n : n + 1, :] = vector[...].astype(F32).reshape(1, width)
     bup[...] = jnp.broadcast_to(b_up[...].astype(F32).reshape(1, width), bup.shape)
     bup_all[link.tp] = bup[...]
     length = len_ref[0]
-    own_first = link.tp * rows
     position = lax.broadcasted_iota(jnp.int32, (1, rows), 1) + own_first
     live = (position < length).astype(F32)
-    em[...] = (e[:, rows_at(own_first, rows, rows)].astype(F32) * live).astype(BF)
+    e_own.wait()
+    em[...] = (em[...].astype(F32) * live).astype(BF)
     ysend[...] = dot(em[...], x[...], 1, 0).astype(ysend.dtype)
     reduce = [
         link.send(ysend.at[place(link.ahead(k), quarter), :], yrecv.at[k - 1], (link.dp, link.ahead(k)))
         for k in others
     ]
     biases = [link.send(bup, bup_all.at[link.tp], (link.dp, link.ahead(k))) for k in others]
+    cross.wait(1)
+    collect.step(1, 0)
     q[...] = (dot(x[...], wq[...], 1, 0) + vec[0:1, :]).astype(BF)
+    collect.step(1, 1)
     own_slots = place(link.tp, quarter)
     for copy in reduce:
         copy.wait()
@@ -218,16 +217,20 @@
     share = [
         link.send(yb.at[own_slots, :], yb.at[own_slots, :], (link.dp, link.ahead(k))) for k in others
     ]
-    gathers = [WeightGather(link, "up", wup, wup_all), WeightGather(link, "down", wdn, wdn_all)]
-    for k in others:
-        for gather in gathers:
-            gather.across(k)
+    for k in (3, 2):
+        cross.start(k)
+    collect.step(1, 2)
+    stores = [local(q, q_out), local(em, em_out)]
     row_live = (lax.broadcasted_iota(jnp.int32, (total, 128), 0) < length).astype(F32).astype(BF)
-    ssum[...] = dot(e[...], row_live, 1, 0)
+    for load in late:
+        load.wait()
+    ssum[...] = dot(e_all[...], row_live, 1, 0)
     for copy in share:
         copy.wait()
     for copy in biases:
         copy.wait()
+    collect.step(1, 3)
+    stores += [local(yb, yb_out), local(ssum, ssum_out)]
 
     lane = lax.broadcasted_iota(jnp.int32, (1, PAIR), 1)
     first_half = (lane < HEAD).astype(F32)
@@ -236,43 +239,54 @@
         full = dot(yb[...], weight[...], 1, 0)
         for p in range(PAIRS):
             cols = slice(p * PAIR, (p + 1) * PAIR)
-            part = full[:, cols] + ssum[...] * vec[bias_row : bias_row + 1, cols]
-            blocks[p, 0:slots, :] = (part * first_half).astype(BF)
-            blocks[p, slots : 2 * slots, :] = (part * (1.0 - first_half)).astype(BF)
+            both = full[:, cols] + ssum[...] * vec[bias_row : bias_row + 1, cols]
+            blocks[p, 0:slots, :] = (both * first_half).astype(BF)
+            blocks[p, slots : 2 * slots, :] = (both * (1.0 - first_half)).astype(BF)
 
     project(wk, 1, kb)
     project(wv, 2, vb)
+    stores += [local(kb, kb_out), local(vb, vb_out)]
 
     block = min(256, rows)
-
-    def attend(step, carry):
-        p = lax.div(step, rows // block)
-        here = place(lax.rem(step, rows // block), block)
+    per_pair = rows // block
+    probs_sem = used[0]
+
+    def tick(ticks):
+        for k, j in ticks:
+            if j == 0:
+                cross.wait(k)
+            collect.step(k, j)
+
+    def attend(p, carry):
         cols = place(p, PAIR)
-        logits = dot(q[here, cols], kb[p], 1, 1) * 0.125
-        halves = []
-        for half in range(2):
-            part = logits[:, half * slots : (half + 1) * slots]
-            peak = jnp.max(part, axis=-1, keepdims=True)
-            raised = jnp.exp(part - peak)
-            halves.append((raised * (1.0 / jnp.sum(raised, axis=-1, keepdims=True))).astype(BF))
-        both = jnp.concatenate(halves, axis=1)
-        probs[p, here, :] = both
-        mixed[here, cols] = dot(both, vb[p], 1, 0).astype(BF)
+
+        def one(step, carry):
+            here = place(step, block)
+            logits = dot(q[here, cols], kb[p], 1, 1) * 0.125
+            halves = []
+            for half in range(2):
+                part = logits[:, half * slots : (half + 1) * slots]
+                peak = jnp.max(part, axis=-1, keepdims=True)
+                raised = jnp.exp(part - peak)
+                halves.append((raised * (1.0 / jnp.sum(raised, axis=-1, keepdims=True))).astype(BF))
+            both = jnp.concatenate(halves, axis=1)
+            probs[p, here, :] = both
+            mixed[here, cols] = dot(both, vb[p], 1, 0).astype(BF)
+            return carry
+
+        lax.fori_loop(0, per_pair, one, 0)
+        pltpu.make_async_copy(probs.at[p], probs_out.at[p], local_sems.at[probs_sem + p]).start()
+        for n, ticks in enumerate(FRONT_TICKS[:-1]):
+
+            @pl.when(p == n)
+            def _():
+                tick(ticks)
+
         return carry
 
-    def advance(*ks):
-        for k in ks:
-            for gather in gathers:
-                gather.advance(k)
-
-    per_pair = rows // block
-    lax.fori_loop(0, 2 * per_pair, attend, 0)
-    advance(1)
-    lax.fori_loop(2 * per_pair, 4 * per_pair, attend, 0)
-    advance(2, 1)
-    lax.fori_loop(4 * per_pair, 6 * per_pair, attend, 0)
-    advance(3, 2, 1)
+    lax.fori_loop(0, PAIRS, attend, 0)
+    used[0] += PAIRS
+    stores.append(local(mixed, mixed_out))
 
     def finish(step, carry):
         here = place(step, block)
@@ -283,52 +297,63 @@
         rstd[here, :] = jnp.broadcast_to(inverse, (block, 128))
         return carry
 
-    lax.fori_loop(0, rows // block, finish, 0)
-    advance(3, 2, 3, 1, 2, 3)
-    own_up.wait()
-    own_dn.wait()
-
-
-def front(mesh, lengths, x, wq, wk, wv, wo, wup, wdn, e, vectors, b_up):
+    lax.fori_loop(0, per_pair, finish, 0)
+    tick(FRONT_TICKS[-1])
+    cross.wait(2)
+    for copy in stores:
+        copy.wait()
+    for p in range(PAIRS):
+        pltpu.make_async_copy(probs.at[p], probs_out.at[p], local_sems.at[probs_sem + p]).wait()
+
+
+def front(mesh, lengths, x, wq, e, wk, wv, wo, wup, vectors, b_up):
     dp_size, tp_size = mesh.shape["dp"], mesh.shape["tp"]
+    low = min(3, dp_size.bit_length() - 1)
     rows, width = x.shape
     slots = e.shape[0]
     vmem = pl.BlockSpec(memory_space=pltpu.VMEM)
     hbm = pl.BlockSpec(memory_space=pltpu.HBM)
     shape = jax.ShapeDtypeStruct
+    moved = (
+        ((rows, width), BF),
+        ((rows, width), BF),
+        ((PAIRS, rows, 2 * slots), BF),
+        ((PAIRS, 2 * slots, PAIR), BF),
+        ((PAIRS, 2 * slots, PAIR), BF),
+        ((slots, width), BF),
+        ((slots, 128), F32),
+        ((slots, rows), BF),
+    )
+    kept = (
+        ((VECTORS, width), F32),
+        ((rows, width), F32),
+        ((rows, 128), F32),
+        ((tp_size, 8, width), F32),
+    )
     return pl.pallas_call(
-        functools.partial(front_kernel, dp_size, tp_size),
-        out_shape=(
-            shape((VECTORS, width), F32),
-            shape((rows, width), F32),
-            shape((rows, 128), F32),
-            shape((rows, width), BF),
-            shape((rows, width), BF),
-            shape((PAIRS, rows, 2 * slots), BF),
-            shape((PAIRS, 2 * slots, PAIR), BF),
-            shape((PAIRS, 2 * slots, PAIR), BF),
-            shape((slots, width), BF),
-            shape((slots, 128), F32),
-            shape((slots, rows), BF),
-            shape((tp_size, 8, width), F32),
-            shape((tp_size, *wup.shape), BF),
-            shape((tp_size, *wdn.shape), BF),
-        ),
-        in_specs=[pl.BlockSpec(memory_space=pltpu.SMEM)] + [vmem] * (9 + len(vectors)),
-        out_specs=tuple([vmem] * 12 + [hbm] * 2),
-        scratch_shapes=[
+        functools.partial(front_kernel, dp_size, tp_size, len(vectors)),
+        out_shape=tuple(shape(*s) for s in kept + moved)
+        + (shape((tp_size - 1, *wup.shape), BF),),
+        in_specs=[pl.BlockSpec(memory_space=pltpu.SMEM)]
+        + [vmem] * 2
+        + [hbm] * 5
+        + [vmem] * (len(vectors) + 1),
+        out_specs=tuple([vmem] * len(kept) + [hbm] * (len(moved) + 1)),
+        scratch_shapes=[pltpu.VMEM(w.shape, BF) for w in (wk, wv, wo, e)]
+        + [pltpu.VMEM(*s) for s in moved]
+        + [
             pltpu.VMEM((8, width), F32),
             pltpu.VMEM((slots, width), BF),
             pltpu.VMEM((tp_size - 1, slots // tp_size, width), BF),
             pltpu.SemaphoreType.DMA((FRONT_SEMS,)),
             pltpu.SemaphoreType.DMA((FRONT_SEMS,)),
-            pltpu.SemaphoreType.DMA((2,)),
+            pltpu.SemaphoreType.DMA((24,)),
         ],
         compiler_params=pltpu.CompilerParams(
             collective_id=0, has_side_effects=True, vmem_limit_bytes=VMEM_LIMIT
         ),
         name="front",
-    )(lengths, x, wq, wk, wv, wo, wup, wdn, e, *vectors, b_up)
+    )(lengths, x, wq, e, wk, wv, wo, wup, *vectors, b_up)
 
 
 BACK_SEMS = 128
@@ -495,7 +520,10 @@
     rstd,
     mixed,
     wo,
-    ff_pieces,
+    ff_far,
+    ff_own,
+    ff_landed,
+    ff_near,
     dnorm,
     probs,
     x_hbm,
@@ -508,13 +536,16 @@
     wq_hbm,
     wk_hbm,
     wv_hbm,
-    grad_in,
-    ff_out,
+    grad_hbm,
+    ff_hbm,
+    go_hbm,
     gq_out,
-    go_out,
     gkv_out,
     seq_out,
     vec_out,
+    grad_in,
+    ff_out,
+    go_out,
     x,
     q,
     kb,
@@ -534,6 +565,10 @@
     dland,
     dfull,
     ff_zland,
+    far_acc,
+    far_land,
+    own_acc,
+    own_land,
     o_acc,
     o_land,
     q_acc,
@@ -581,44 +616,75 @@
     owned = width // tp_size
 
     ff_track, ff_orders = Track(), ((0, 1, 2), (0, 2, 1))
-    ff_rows = ff_pieces.shape[2]
-    ff_fans, ff_joins = [], []
+    ff_rows = width >> 3
+    ff_parts = []
     for m in range(2):
-
-        def ends(k, m=m):
-            return ff_pieces.at[m, link.ahead(k)], ff_zland.at[m, k - 1]
-
-        def offset(m=m):
-            first, size = 0, width >> 1
-            for b in ff_orders[m]:
-                if b < low:
-                    first = first + link.bit(b) * size
-                    size = size >> 1
-            return first
-
-        fan = Fan(link, ends)
+        first, second, third_bit = ff_orders[m]
+        far = Spread(link, (third_bit,), width >> 2, ff_far.at[m], far_acc.at[m], far_land.at[m])
+        own = Spread(link, (second, third_bit), width >> 1, ff_own.at[m], own_acc.at[m], own_land.at[m])
+        slot = link.take(2)
+
+        def piece_copy(n, m=m, slot=slot):
+            source, k = ((far_acc, 3), (ff_near, 2))[n]
+            return link.remote(slot + n, source.at[m], ff_zland.at[m, n], (link.dp, link.behind(k)))
+
+        def offset(m=m, own=own):
+            return link.bit(ff_orders[m][0]) * (width >> 1) + own.offset()
+
         widen = Widen(link, wide_ff.at[m])
 
-        def join(m=m, fan=fan, widen=widen, offset=offset):
-            fan.wait()
-            total = ff_pieces[m, link.tp].astype(F32)
-            for k in others:
-                total = total + ff_zland[m, k - 1].astype(F32)
-            own = rows_at(offset(), ff_rows, 16)
-            ff_out[m, own, :] = total.astype(BF)
-            widen.run(ff_out.at[m, own, :])
+        def join(m=m, own=own, piece_copy=piece_copy, offset=offset, widen=widen):
+            total = own_acc[m, own.kept(), :].astype(F32) + ff_landed[m].astype(F32)
+            for n in range(2):
+                piece_copy(n).wait()
+                total = total + ff_zland[m, n].astype(F32)
+            mine = rows_at(offset(), ff_rows, 16)
+            ff_out[m, mine, :] = total.astype(BF)
+            widen.run(ff_out.at[m, mine, :])
 
         collect = Collect(
             link, ff_orders[m], offset, ff_rows,
             lambda first, size, m=m: ff_out.at[m, rows_at(first, size, 16), :],
         )
-        ff_fans.append(fan)
-        ff_joins.append((join, collect))
-    for fan in ff_fans:
-        fan.start()
-    steps = [list(collect.steps()) for _, collect in ff_joins]
-    ff_track.add([then(ff_joins[0][0], steps[0][0], ff_joins[1][0], steps[1][0])])
-    ff_track.add([then(*pair) for pair in zip(steps[0][1:], steps[1][1:])])
+        ff_parts.append((far, own, piece_copy, join, list(collect.steps())))
+
+    def ff_begin():
+        for far, own, piece_copy, _, _ in ff_parts:
+            far.start(0)
+            own.start(0)
+            piece_copy(1).start()
+
+    def ff_second():
+        for far, own, piece_copy, _, _ in ff_parts:
+            far.finish(0)
+            piece_copy(0).start()
+
+    def ff_second_own():
+        for far, own, piece_copy, _, _ in ff_parts:
+            own.finish(0)
+            own.start(1)
+
+    def ff_third():
+        for _, own, _, join, collects in ff_parts:
+            own.finish(1)
+
+    def ff_join():
+        for _, _, _, join, collects in ff_parts:
+            join()
+            collects[0]()
+
+    stores = []
+
+    def store(n, source, target):
+        copy = pltpu.make_async_copy(source, target, local_sems.at[13 + n])
+        stores.append(copy)
+        return copy
+
+    ff_store, go_store, grad_store = store(0, ff_out, ff_hbm), store(1, go_out, go_hbm), store(2, grad_in, grad_hbm)
+    ff_begin()
+    ff_track.add([ff_second, ff_second_own, then(ff_third, ff_join)])
+    ff_track.add([then(*pair) for pair in zip(ff_parts[0][4][1:], ff_parts[1][4][1:])])
+    ff_track.add([ff_store.start], join=True)
 
     def square_track(order, out, acc, landing, zland, wide):
         track, spread = Track(), Spread(link, order, width, out, acc, landing)
@@ -657,11 +723,12 @@
         track.add(collect.steps(), join=True)
         return track
 
-    def owned_track(order, total_rows, source, acc, landing, out, wide):
+    def owned_track(order, total_rows, cols, source, acc, landing, out, wide):
+        source, acc, landing = source.at[:, cols], acc.at[:, cols], landing.at[:, cols]
         track, spread = Track(), Spread(link, order, total_rows, source, acc, landing)
 
         def region(k):
-            ref = out.at[link.tp, rows_at(spread.offset(), spread.piece, 16), :]
+            ref = out.at[link.tp, rows_at(spread.offset(), spread.piece, 16), cols]
             return ref, ref
 
         share, widen = Fan(link, region), Widen(link, wide)
@@ -674,7 +741,7 @@
             share.start()
 
         collect = Collect(
-            link, order, spread.offset, spread.piece, lambda first, size: out.at[:, rows_at(first, size, 16), :]
+            link, order, spread.offset, spread.piece, lambda first, size: out.at[:, rows_at(first, size, 16), cols]
         )
         track.add(spread.steps())
         track.add([last, share.wait])
@@ -682,9 +749,19 @@
         return track
 
     o_track = square_track((0, 1, 2), go_out, o_acc, o_land, o_zland, wide_q.at[0])
+    o_track.add([go_store.start], join=True)
     q_track = square_track((0, 2, 1), gq_out, q_acc, q_land, q_zland, wide_q.at[1])
-    kv_track = owned_track((0, 1, 2), 2 * owned, kv_send, kv_acc, kv_land, gkv_out, wide_kv)
-    s_track = owned_track((0, 2, 1), slots, s_send, s_acc, s_land, seq_out, wide_s)
+    def halves(total_rows, source, acc, landing, out, wide):
+        tracks = []
+        for h, order in enumerate(((0, 1, 2), (0, 2, 1))):
+            cols = slice(h * source.shape[1] // 2, (h + 1) * source.shape[1] // 2)
+            tracks.append(owned_track(order, total_rows, cols, source, acc, landing, out, wide.at[h]))
+        both = Track()
+        both.add([then(*pair) for pair in zip(tracks[0].todo, tracks[1].todo)])
+        return both
+
+    kv_track = halves(2 * owned, kv_send, kv_acc, kv_land, gkv_out, wide_kv)
+    s_track = halves(slots, s_send, s_acc, s_land, seq_out, wide_s)
 
     vec_track, vec_slot = Track(), link.take(link.bits)
     vec_fan = Fan(link, lambda k: (vec_z.at[link.tp], vec_z.at[link.tp]))
@@ -754,6 +831,7 @@
 
     weight_grad(mixed, d_attn, go_out)
     o_track.advance()
+    ff_track.advance()
     dmix[...] = dot(d_attn[...], wo[...], 1, 1).astype(BF)
     o_track.advance()
     for load in late:
@@ -766,7 +844,8 @@
     def pair_at(n):
         second = lax.div(n, three)
         which = (1 - own_half) * (1 - second) + own_half * second
-        return which * three + lax.rem(n, three)
+        along = lax.rem(n, three)
+        return which * three + along * parity + (three - 1 - along) * (1 - parity)
 
     def fetch(n):
         slot = lax.rem(n, 2)
@@ -815,17 +894,13 @@
         block_of = dpart.at[:, rows_at(peer * owned, owned, 64), :]
         return link.remote(d_slot + j, block_of, dland.at[j], (link.dp, peer))
 
-    def far_blocks():
-        d_copy(0).start()
-        d_copy(1).start()
-
     events = [
-        lambda: o_track.advance(),
-        lambda: o_track.advance(),
-        then(far_blocks, ff_track.advance, o_track.advance),
-        then(ff_track.advance, o_track.advance),
-        then(ff_track.advance, o_track.advance),
-        then(lambda: d_copy(2).start(), ff_track.advance, o_track.advance),
+        then(),
+        then(lambda: d_copy(1).start(), ff_track.advance),
+        lambda: d_copy(0).start(),
+        o_track.advance,
+        then(lambda: d_copy(2).start(), ff_track.advance),
+        then(),
     ]
 
     def one(n, carry):
@@ -838,6 +913,16 @@
 
     weight_grad(x, dq, gq_out)
     q_track.advance()
+    ff_track.advance()
+
+    def input_grad(step, carry):
+        here = place(step, block)
+        dres[here, :] += dot(dq[here, :], wq[...], 1, 1)
+        return carry
+
+    lax.fori_loop(0, count, input_grad, 0)
+    q_track.advance()
+    vec_acc[0, 0:1, :] = jnp.sum(dq[...].astype(F32), axis=0, keepdims=True)
 
     for j in range(tp_size - 1):
         d_copy(j).wait()
@@ -849,22 +934,18 @@
         dfull[n, own_block, :] = total.astype(BF)
     d_share = Fan(link, lambda k: (dfull.at[:, own_block, :], dfull.at[:, own_block, :]))
     d_share.start()
-    q_track.advance()
+    ff_track.advance()
     for n in range(2):
         kv_send[n * owned : (n + 1) * owned, :] = dot(dfull[n, own_block, :], yb[...], 1, 0).astype(BF)
     kv_track.advance()
-    vec_acc[0, 0:1, :] = jnp.sum(dq[...].astype(F32), axis=0, keepdims=True)
-
-    def input_grad(step, carry):
-        here = place(step, block)
-        dres[here, :] += dot(dq[here, :], wq[...], 1, 1)
-        return carry
-
-    lax.fori_loop(0, count, input_grad, 0)
+    q_track.advance()
+    ff_track.advance()
+    kv_track.advance()
+    o_track.advance()
     kv_track.advance()
     q_track.advance()
+    kv_track.advance()
     o_track.advance()
-    kv_track.advance()
     d_share.wait()
     backs = dot(wk[...], dfull[0], 1, 0) + dot(wv[...], dfull[1], 1, 0)
     back = backs.T.astype(BF)
@@ -883,7 +964,6 @@
         vec_acc[0, 1 + n : 2 + n, :] = total[0:1, :] * (1.0 / tp_size)
     vec_track.advance()
     s_track.advance()
-    kv_track.advance()
 
     def input_grad_last(step, carry):
         here = place(step, block)
@@ -891,13 +971,16 @@
         return carry
 
     lax.fori_loop(0, count, input_grad_last, 0)
-    tracks = [s_track, kv_track, q_track, vec_track, ff_track, o_track]
+    grad_store.start()
+    tracks = [s_track, kv_track, q_track, o_track, vec_track, ff_track]
     while any(track.todo for track in tracks):
         for track in tracks:
             track.advance()
-
-
-def back(mesh, lengths, vec, part_vec, xhat, rstd, mixed, wo, ff_pieces, dnorm, probs, *late):
+    for copy in stores:
+        copy.wait()
+
+
+def back(mesh, lengths, vec, part_vec, xhat, rstd, mixed, wo, ff_far, ff_own, ff_landed, ff_near, dnorm, probs, *late):
     dp_size, tp_size = mesh.shape["dp"], mesh.shape["tp"]
     bits = dp_size.bit_length() - 1
     low = min(3, bits)
@@ -929,9 +1012,10 @@
             shape((tp_size, slots, rows), BF),
             shape((VECTORS, width), F32),
         ),
-        in_specs=[pl.BlockSpec(memory_space=pltpu.SMEM)] + [vmem] * 7 + [hbm] * (2 + len(late)),
-        out_specs=tuple([vmem] * 7),
-        scratch_shapes=[pltpu.VMEM(array.shape, array.dtype) for array in late]
+        in_specs=[pl.BlockSpec(memory_space=pltpu.SMEM)] + [vmem] * 9 + [hbm] * (3 + len(late)),
+        out_specs=tuple([hbm] * 3 + [vmem] * 4),
+        scratch_shapes=[buf(rows, width), buf(2, width, width), buf(width, width)]
+        + [pltpu.VMEM(array.shape, array.dtype) for array in late]
         + [
             buf(rows, width, dtype=F32),
             buf(rows, width),
@@ -941,7 +1025,11 @@
             buf(2, width, slots),
             buf(others, 2, owned, slots),
             buf(2, width, slots),
-            buf(2, others, ff_piece, width),
+            buf(2, 2, ff_piece, width),
+            buf(2, width >> 3, width),
+            buf(2, width >> 3, width),
+            buf(2, width >> 2, width),
+            buf(2, (width >> 2) + (width >> 3), width),
             buf(width // 2, width),
             buf(landing(width), width),
             buf(width // 2, width),
@@ -959,17 +1047,17 @@
             buf(tp_size, VECTORS, width, dtype=F32),
             buf(2, wide, ff_piece, width),
             buf(2, wide, *quarter),
-            buf(wide, kv_piece, width),
-            buf(wide, s_piece, rows),
+            buf(2, wide, kv_piece, width // 2),
+            buf(2, wide, s_piece, rows // 2),
             pltpu.SemaphoreType.DMA((BACK_SEMS,)),
             pltpu.SemaphoreType.DMA((BACK_SEMS,)),
-            pltpu.SemaphoreType.DMA((3 + len(late),)),
+            pltpu.SemaphoreType.DMA((6 + len(late),)),
         ],
         compiler_params=pltpu.CompilerParams(
             collective_id=1, has_side_effects=True, vmem_limit_bytes=VMEM_LIMIT
         ),
         name="back",
-    )(lengths, vec, part_vec, xhat, rstd, mixed, wo, ff_pieces, dnorm, probs, *late)
+    )(lengths, vec, part_vec, xhat, rstd, mixed, wo, ff_far, ff_own, ff_landed, ff_near, dnorm, probs, *late)
 
 
 class ChunkSpread:
@@ -977,6 +1065,7 @@
         self.link, self.rows, self.sent, self.acc, self.landing = link, rows, sent, acc, landing
         self.orders = [[b for b in order if b < link.low] for order in ((0, 1, 2), (0, 2, 1))]
         self.stages = link.low
+        self.slot = link.take(2 * link.low * acc.shape[1])
 
     def inside(self, m, i):
         first = 0
@@ -992,7 +1081,7 @@
         else:
             source = self.acc.at[m, c, rows_at(self.inside(m, i - 1) + (1 - link.bit(bit)) * size, size, 16), :]
         first = sum(self.rows >> (j + 1) for j in range(i))
-        slot = (i * 2 + m) * self.acc.shape[1] + c
+        slot = self.slot + (i * 2 + m) * self.acc.shape[1] + c
         return link.remote(slot, source, self.landing.at[m, c, pl.ds(first, size), :], link.partner(bit))
 
     def start(self, c, m, i):
@@ -1010,8 +1099,19 @@
         else:
             at = self.inside(m, i)
             add_rows(acc, at, acc, at, landed, size)
-        if i + 1 < self.stages:
-            self.start(c, m, i + 1)
+
+
+MIDDLE_SEMS = 96
+MIDDLE_TICKS = (
+    (),
+    ((0, 2, 1), (1, 1, 0), (1, 3, 0)),
+    ((1, 1, 1),),
+    ((0, 2, 2), (1, 3, 1), (1, 2, 0)),
+    ((1, 1, 2),),
+    ((0, 2, 3), (1, 3, 2), (1, 2, 1)),
+    ((1, 1, 3),),
+    ((1, 2, 2), (1, 3, 3), (1, 2, 3)),
+)
 
 
 def middle_kernel(
@@ -1020,15 +1120,19 @@
     vec,
     bup_all,
     xhat,
-    out_grad,
-    wup_all,
-    wdn_all,
+    out_grad_hbm,
+    own_up,
+    own_dn,
+    ups,
     layer_out,
     dnorm,
     part_vec,
-    ff_pieces,
-    wup,
-    wdn,
+    ff_landed,
+    ff_near,
+    ff_far,
+    ff_own,
+    whole,
+    out_grad,
     nb,
     act,
     slope,
@@ -1043,19 +1147,33 @@
 ):
     link = Link(dp_size, tp_size, send_sems, recv_sems)
     rows, width = xhat.shape
-    loads = []
-    for c in range(tp_size):
-        for n, (source, target) in enumerate(((wup_all, wup), (wdn_all, wdn))):
-            loads.append(pltpu.make_async_copy(source.at[c], target.at[c], local_sems.at[n * tp_size + c]))
-            loads[-1].start()
-    barrier = pltpu.get_barrier_semaphore()
-    for b in range(link.low):
-        pl.semaphore_signal(barrier, inc=1, device_id=link.partner(b), device_id_type=MESH)
-    pl.semaphore_wait(barrier, link.low)
+    used = [0]
+
+    def local(source, target):
+        copy = pltpu.make_async_copy(source, target, local_sems.at[used[0]])
+        used[0] += 1
+        copy.start()
+        return copy
+
+    collect = WeightCollect(link, width // 2, lambda k: whole.at[1, k])
+    cross = Cross(link, collect, own_dn)
+    up_last = WeightCollect(link, width // 2, lambda k: whole.at[0, 2])
+    placed = [
+        local(ups.at[1, up_last.rows(h, 0), :], whole.at[0, 2, up_last.rows(h, 0), :]) for h in range(2)
+    ]
+    owns = [local(own_up, whole.at[0, 0])]
+    owns += [local(ups.at[k - 1], whole.at[0, k]) for k in (1, 3)]
+    owns += [local(own_dn, whole.at[1, 0]), local(out_grad_hbm, out_grad)]
+    link.greet(link.low)
+    for k in (1, 3, 2):
+        cross.start(k)
+    for copy in placed:
+        copy.wait()
+    up_last.step(2, 0)
     gain, shift, b_down, f_gain, f_shift = (vec[n : n + 1, :] for n in (4, 5, 6, 7, 8))
     block = min(256, rows)
     count = rows // block
-    big = min(512, rows)
+    big = rows // 2
 
     def norm(step, carry):
         here = place(step, block)
@@ -1063,28 +1181,38 @@
         return carry
 
     lax.fori_loop(0, count, norm, 0)
-    for load in loads:
-        load.wait()
-
-    per_chunk = rows // big
+    for copy in owns[:3]:
+        copy.wait()
 
     def forward(step, carry):
-        c = lax.div(step, per_chunk)
-        here, cols = place(lax.rem(step, per_chunk), big), place(c, width)
-        pre = dot(nb[here, :], wup[c], 1, 0) + bup_all[c, 0:1, :]
+        n = lax.div(step, 2)
+        k = n + lax.div(n, 2) * (7 - 2 * n - 2)
+        here, cols = place(lax.rem(step, 2), big), place(k, width)
+        pre = dot(nb[here, :], whole[0, k], 1, 0) + bup_all[link.behind(k), 0:1, :]
         cdf = 0.5 * (1.0 + lax.erf(pre * 0.7071067811865476))
         act[here, cols] = (pre * cdf).astype(BF)
         slope[here, cols] = (cdf + pre * (jnp.exp(pre * pre * -0.5) * 0.3989422804014327)).astype(BF)
+        for n, ticks in enumerate(MIDDLE_TICKS):
+
+            @pl.when(step == n)
+            def _():
+                for m, shard, j in ticks:
+                    if m == 1 and j == 0:
+                        cross.wait(shard)
+                    (up_last, collect)[m].step(shard, j)
+
         return carry
 
-    lax.fori_loop(0, tp_size * per_chunk, forward, 0)
+    lax.fori_loop(0, 2 * tp_size, forward, 0)
+    for copy in owns[3:]:
+        copy.wait()
 
     def second_norm(step, carry):
         g_gain, g_shift, g_down = carry
         here = place(step, block)
-        branch = dot(act[here, 0:width], wdn[0], 1, 0)
-        for c in range(1, tp_size):
-            branch = branch + dot(act[here, c * width : (c + 1) * width], wdn[c], 1, 0)
+        branch = dot(act[here, 0:width], whole[1, 0], 1, 0)
+        for k in range(1, tp_size):
+            branch = branch + dot(act[here, k * width : (k + 1) * width], whole[1, k], 1, 0)
         res = xhat[here, :] * gain + shift + (branch + b_down)
         center = res - jnp.mean(res, axis=-1, keepdims=True)
         inverse = lax.rsqrt(jnp.mean(center * center, axis=-1, keepdims=True) + 1e-05)
@@ -1120,28 +1248,37 @@
             mine = pl.ds(pl.multiple_of(first + m * third, third), third)
             target[m * third : (m + 1) * third, :] = dot(left[:, mine], right[:, cols], 0, 0).astype(BF)
 
-    def backward(c, carry):
-        cols = place(c, width)
-        slot = lax.rem(c, 2)
-        weight_grad(act, c * width, d_branch, slice(0, width), sent.at[1, slot])
-        spread.start(c, 1, 0)
+    def settle(n, steps):
+        for m, late, stage in steps:
+
+            @pl.when(n >= late)
+            def _():
+                spread.finish(n - late, m, stage)
+
+            if stage < 2:
+
+                @pl.when(jnp.logical_and(n >= late, n - late < 3 - stage))
+                def _():
+                    spread.start(n - late, m, stage + 1)
+
+    def backward(n, carry):
+        k = lax.rem(n + 1, tp_size)
+        cols = place(k, width)
+        slot = lax.rem(n, 2)
+        weight_grad(act, k * width, d_branch, slice(0, width), sent.at[1, slot])
+        spread.start(n, 1, 0)
+        settle(n, ((0, 1, 0), (1, 2, 1)))
 
         def through(step, total):
             here = place(step, big)
-            grad = (dot(d_branch[here, :], wdn[c], 1, 1) * slope[here, cols].astype(F32)).astype(BF)
+            grad = (dot(d_branch[here, :], whole[1, k], 1, 1) * slope[here, cols].astype(F32)).astype(BF)
             slope[here, cols] = grad
             return total + jnp.sum(grad.astype(F32), axis=0, keepdims=True)
 
-        part_vec[pl.ds(9 + c, 1), :] = lax.fori_loop(0, rows // big, through, zero)
+        part_vec[pl.ds(9 + link.behind(k), 1), :] = lax.fori_loop(0, 2, through, zero)
+        settle(n, ((1, 0, 0), (0, 2, 1)))
         weight_grad(nb, 0, slope, cols, sent.at[0, slot])
-        spread.start(c, 0, 0)
-        for back_by in range(1, spread.stages + 1):
-
-            @pl.when(c >= back_by)
-            def _():
-                for m in (1, 0):
-                    spread.finish(c - back_by, m, back_by - 1)
-
+        spread.start(n, 0, 0)
         return carry
 
     lax.fori_loop(0, tp_size, backward, 0)
@@ -1149,36 +1286,42 @@
     def input_grad(step, carry):
         here = place(step, big)
         total = d_acc[here, :]
-        for c in range(tp_size):
-            total = total + dot(slope[here, c * width : (c + 1) * width], wup[c], 1, 1)
+        for k in range(tp_size):
+            total = total + dot(slope[here, k * width : (k + 1) * width], whole[0, k], 1, 1)
         d_acc[here, :] = total
         return carry
 
-    half = rows // big // 2
-    lax.fori_loop(0, half, input_grad, 0)
-    for c in range(max(0, tp_size - spread.stages), tp_size):
-        stage = tp_size - 1 - c
-        for m in (1, 0):
-            spread.finish(c, m, stage)
-    lax.fori_loop(half, rows // big, input_grad, 0)
-    store = pltpu.make_async_copy(d_acc, dnorm, local_sems.at[2 * tp_size])
-    store.start()
-    for late in range(1, spread.stages):
-        for c in range(max(0, tp_size - spread.stages) + late, tp_size):
-            stage = tp_size - 1 - c + late
-            for m in (1, 0):
-                spread.finish(c, m, stage)
-    piece = width >> spread.stages
+    slot = link.take(2)
+    crossing = []
+    lax.fori_loop(0, 1, input_grad, 0)
+    for m in (1, 0):
+        spread.finish(0, m, 2)
+        at = rows_at(spread.inside(m, 2), width >> 3, 16)
+        crossing.append(
+            link.remote(slot + m, acc.at[m, 0, at, :], ff_landed.at[m], (link.dp, link.behind(1)))
+        )
+        crossing[-1].start()
+    spread.finish(3, 0, 0)
+    spread.finish(2, 1, 1)
+    stores = [local(acc.at[m, 3], ff_own.at[m]) for m in range(2)]
+    lax.fori_loop(1, 2, input_grad, 0)
+    stores.append(local(d_acc, dnorm))
+    spread.finish(2, 0, 1)
+    for m in (1, 0):
+        spread.finish(1, m, 2)
     for m in range(2):
-        at = spread.inside(m, spread.stages - 1)
-        for c in range(tp_size):
-            ff_pieces[m, c] = acc[m, c, rows_at(at, piece, 16), :]
-    store.wait()
-
-
-def middle(mesh, vec, bup_all, xhat, out_grad, wup_all, wdn_all):
+        at = rows_at(spread.inside(m, 2), width >> 3, 16)
+        stores.append(local(acc.at[m, 1, at, :], ff_near.at[m]))
+        at = rows_at(spread.inside(m, 1), width >> 2, 16)
+        stores.append(local(acc.at[m, 2, at, :], ff_far.at[m]))
+    for copy in crossing + stores:
+        copy.wait()
+
+
+def middle(mesh, vec, bup_all, xhat, out_grad, w_up, w_dn, ups):
     dp_size, tp_size = mesh.shape["dp"], mesh.shape["tp"]
     low = min(3, dp_size.bit_length() - 1)
+    assert low == 3 and tp_size == 4
     rows, width = xhat.shape
     hidden = tp_size * width
     vmem = pl.BlockSpec(memory_space=pltpu.VMEM)
@@ -1188,20 +1331,22 @@
     def buf(*dims, dtype=BF):
         return pltpu.VMEM(dims, dtype)
 
-    sems = 2 * low * tp_size
     return pl.pallas_call(
         functools.partial(middle_kernel, dp_size, tp_size),
         out_shape=(
             shape((rows, width), BF),
             shape((rows, width), F32),
             shape((VECTORS, width), F32),
-            shape((2, tp_size, width >> low, width), BF),
+            shape((2, width >> 3, width), BF),
+            shape((2, width >> 3, width), BF),
+            shape((2, width >> 2, width), BF),
+            shape((2, width >> 1, width), BF),
         ),
-        in_specs=[vmem] * 4 + [hbm] * 2,
-        out_specs=(vmem, hbm, vmem, vmem),
+        in_specs=[vmem] * 3 + [hbm] * 4,
+        out_specs=(vmem, hbm, vmem, hbm, hbm, hbm, hbm),
         scratch_shapes=[
-            buf(tp_size, width, width),
-            buf(tp_size, width, width),
+            buf(2, tp_size, width, width),
+            buf(rows, width),
             buf(rows, width),
             buf(rows, hidden),
             buf(rows, hidden),
@@ -1210,15 +1355,15 @@
             buf(2, 2, width, width),
             buf(2, tp_size, width // 2, width),
             buf(2, tp_size, sum(width >> (i + 1) for i in range(low)), width),
-            pltpu.SemaphoreType.DMA((sems,)),
-            pltpu.SemaphoreType.DMA((sems,)),
-            pltpu.SemaphoreType.DMA((2 * tp_size + 1,)),
+            pltpu.SemaphoreType.DMA((MIDDLE_SEMS,)),
+            pltpu.SemaphoreType.DMA((MIDDLE_SEMS,)),
+            pltpu.SemaphoreType.DMA((24,)),
         ],
         compiler_params=pltpu.CompilerParams(
             collective_id=2, has_side_effects=True, vmem_limit_bytes=VMEM_LIMIT
         ),
         name="middle",
-    )(vec, bup_all, xhat, out_grad, wup_all, wdn_all)
+    )(vec, bup_all, xhat, out_grad, w_up, w_dn, ups)
 
 
 def finish_kernel(
@@ -1318,12 +1463,14 @@
     row_count, width = layer_in.shape
     tp_size = mesh.shape["tp"]
     vectors = (b_query, b_key, b_value, b_out, attn_gain, attn_shift, b_down, ffn_gain, ffn_shift)
-    vec, xhat, rstd, mixed, queries, probs, kb, vb, folded, ssum, own_proj, bup_all, up_all, down_all = front(
-        mesh, lengths, layer_in, w_query, w_key, w_value, w_out, w_up, w_down, seq_proj, vectors, b_up
+    vec, xhat, rstd, bup_all, mixed, queries, probs, kb, vb, folded, ssum, own_proj, ups = front(
+        mesh, lengths, layer_in, w_query, seq_proj, w_key, w_value, w_out, w_up, vectors, b_up
     )
-    layer_out, d_normed, part_vec, ff_pieces = middle(mesh, vec, bup_all, xhat, out_grad, up_all, down_all)
-    grad_in, g_ff, g_q, g_o, g_kv, g_seq, vec_sum = back(
-        mesh, lengths, vec, part_vec, xhat, rstd, mixed, w_out, ff_pieces, d_normed, probs,
+    layer_out, d_normed, part_vec, ff_landed, ff_near, ff_far, ff_own = middle(
+        mesh, vec, bup_all, xhat, out_grad, w_up, w_down, ups
+    )
+    grad_in, g_ff, g_o, g_q, g_kv, g_seq, vec_sum = back(
+        mesh, lengths, vec, part_vec, xhat, rstd, mixed, w_out, ff_far, ff_own, ff_landed, ff_near, d_normed, probs,
         layer_in, queries, kb, vb, folded, ssum, own_proj, w_query, w_key, w_value
     )
     (

time: 331 us -> 270 us (0.82)
  Pallas kernels: 328 us -> 268 us
    pallas_call x1, Pallas kernels: 85.6 us -> 52 us  [front(): pl.pallas_call(functools.partial(front_kernel, dp_size, tp_size, len(vect...]
    pallas_call x1, Pallas kernels: 149 us -> 117 us  [back(): pl.pallas_call(functools.partial(back_kernel, dp_size, tp_size), out_shap...]
    pallas_call x1, Pallas kernels: 79.9 us -> 86.8 us  [middle(): pl.pallas_call(functools.partial(middle_kernel, dp_size, tp_size), out_sh...]
where the time goes in v4:
time: 270 us
  Pallas kernels  268 us (99%)
    pallas_call x1, Pallas kernels, back(): pl.pallas_call(functools.partial(back_kernel, dp_size, tp_size), out_shap...  117 us
    pallas_call x1, Pallas kernels, middle(): pl.pallas_call(functools.partial(middle_kernel, dp_size, tp_size), out_sh...  86.8 us
    pallas_call x1, Pallas kernels, front(): pl.pallas_call(functools.partial(front_kernel, dp_size, tp_size, len(vect...  52 us
    pallas_call x1, Pallas kernels, finish(): pl.pallas_call(functools.partial(finish_kernel, tp_size), out_shape=tuple...  13.1 us

profile of v4, /device:TPU:0, one launch (start us, length us, event | category | flops | bytes accessed | tf_op | source)
XLA Modules:
  0.0 269.9 jit_solution(807774843104215547)
XLA Ops:
  1.3 52.0 %front.1 = (f32[16,768]{1,0:T(8,128)}, f32[1024,768]{1,0:T(8,128)}, f32[1024,128]{1,0:T(8,128)}, f32[4,8,768]{2,1,0:T(8,128)}, bf16[1024,768]{1,0:T(8,128)(2,1)}...) custom-call(s32[1]{0:T(128)S(6)} %copy.39.len_ref, ...), custom_call_target="tpu_custom_call" | custom-call | tf_op jit(solution)/shard_map/front/pallas_call | solution.py:333
  53.3 86.8 %middle.1 = (bf16[1024,768]{1,0:T(8,128)(2,1)}, f32[1024,768]{1,0:T(8,128)}, f32[16,768]{1,0:T(8,128)}, bf16[2,96,768]{2,1,0:T(8,128)(2,1)}, bf16[2,96,768]{2,1,...) custom-call(f32[16,768]{1,0:T(8,128)} %get-tuple-element.65.vec, ...), custom_call_target="tpu_custom_call" | custom-call | tf_op jit(solution)/shard_map/middle/pallas_call | solution.py:1334
  140.1 116.5 %back.1 = (bf16[1024,768]{1,0:T(8,128)(2,1)}, bf16[2,768,768]{2,1,0:T(8,128)(2,1)}, bf16[768,768]{1,0:T(8,128)(2,1)}, bf16[768,768]{1,0:T(8,128)(2,1)}, bf16[4,3...) custom-call(s32[1]{0:T(128)S(6)} %copy.39.len_ref, f32[16,768]{1,0:T(8,128)} %get-tuple-element.65.vec, ...), custom_call_target="tpu_custom_call" | custom-call | tf_op jit(solution)/shard_map/back/pallas_call | solution.py:1004
  256.6 13.1 %finish.1 = (f32[768,768]{1,0:T(8,128)}, f32[768,768]{1,0:T(8,128)}, f32[768,768]{1,0:T(8,128)}, f32[768,768]{1,0:T(8,128)}, f32[768,768]{1,0:T(8,128)}, /*index...) custom-call(bf16[2,768,768]{2,1,0:T(8,128)(2,1)} %get-tuple-element., ...), custom_call_target="tpu_custom_call" | custom-call | tf_op jit(solution)/shard_map/finish/pallas_call | solution.py:1424

commit v5 on v4

--- a/solution.py
+++ b/solution.py
@@ -15,6 +15,7 @@
 F32 = jnp.float32
 MESH = pl.DeviceIdType.MESH
 VMEM_LIMIT = 67_043_328
+BLOCK_F, BLOCK_M, BLOCK_B, GRAD_SPLIT = 1024, 512, 1024, 2
 
 
 def dot(left, right, left_dim, right_dim):
@@ -39,17 +40,24 @@
         self.low = min(3, self.bits)
         self.send_sems, self.recv_sems = send_sems, recv_sems
         self.used = 0
+        self.bit_values = [lax.rem(lax.div(self.dp, 1 << b), 2) for b in range(self.bits)]
+        self.partners = [
+            (self.dp + (1 - 2 * self.bit_values[b]) * (1 << b), self.tp) for b in range(self.bits)
+        ]
+        self.aheads = [lax.rem(self.tp + k, tp_size) for k in range(tp_size)]
 
     def bit(self, b):
-        return lax.rem(lax.div(self.dp, 1 << b), 2)
+        return self.bit_values[b]
 
     def partner(self, b):
-        return (self.dp + (1 - 2 * self.bit(b)) * (1 << b), self.tp)
+        return self.partners[b]
 
     def ahead(self, k):
-        return lax.rem(self.tp + k, self.tp_size)
+        return self.aheads[k]
 
     def behind(self, k):
+        if isinstance(k, int):
+            return self.aheads[(self.tp_size - k) % self.tp_size]
         return lax.rem(self.tp + self.tp_size - k, self.tp_size)
 
     def greet(self, dp_bits):
@@ -90,14 +98,6 @@
     return [[b for b in order if b < low] for order in ((1, 2, 0), (2, 1, 0))]
 
 
-def half_offset(link, order, piece):
-    first, size = 0, piece
-    for b in order:
-        first = first + link.bit(b) * size
-        size *= 2
-    return first
-
-
 class WeightCollect:
     def __init__(self, link, part, whole):
         self.link, self.whole, self.part = link, whole, part
@@ -105,11 +105,16 @@
         self.piece = self.part >> link.low
         self.stages = link.low
         self.slot = link.take(2 * (link.tp_size - 1) * link.low)
+        self.firsts = []
+        for h in range(2):
+            first, size, starts = h * part, self.piece, []
+            for b in self.orders[h]:
+                starts.append(size * link.bit(b))
+                size *= 2
+            self.firsts.append([sum(starts[i:], first) for i in range(self.stages)])
 
     def rows(self, h, i):
-        size = self.piece << i
-        first = half_offset(self.link, self.orders[h], self.piece)
-        return rows_at(h * self.part + first - lax.rem(first, size), size, 16)
+        return rows_at(self.firsts[h][i], self.piece << i, 16)
 
     def copies(self, k, i):
         for h in range(2):
@@ -127,8 +132,8 @@
 
 
 class Cross:
-    def __init__(self, link, collect, shard):
-        self.link, self.collect, self.shard = link, collect, shard
+    def __init__(self, link, collect, shard, target):
+        self.link, self.collect, self.shard, self.target = link, collect, shard, target
         self.slot = link.take(2 * (link.tp_size - 1))
 
     def copies(self, k):
@@ -137,7 +142,7 @@
             yield self.link.remote(
                 self.slot + 2 * (k - 1) + h,
                 self.shard.at[rows, :],
-                self.collect.whole(k).at[rows, :],
+                self.target(k, h, rows),
                 (self.link.dp, self.link.ahead(k)),
             )
 
@@ -161,11 +166,11 @@
 )
 
 
-def front_kernel(dp_size, tp_size, n_vectors, len_ref, x, wq, e, wk_hbm, wv_hbm, wo_hbm, wup, *rest):
+def front_kernel(dp_size, tp_size, n_vectors, len_ref, x_hbm, wq_hbm, e, wk_hbm, wv_hbm, wo_hbm, wup, wdn, *rest):
     vectors, b_up, rest = rest[:n_vectors], rest[n_vectors], rest[n_vectors + 1 :]
-    outs, scratch = rest[:13], rest[13:]
-    (vec, xhat, rstd, bup_all, mixed_out, q_out, probs_out, kb_out, vb_out, yb_out, ssum_out, em_out, ups) = outs
-    (wk, wv, wo, e_all, mixed, q, probs, kb, vb, yb, ssum, em, bup, ysend, yrecv, send_sems, recv_sems, local_sems) = scratch
+    outs, scratch = rest[:14], rest[14:]
+    (vec, bup_all, xhat_out, rstd_out, mixed_out, q_out, probs_out, kb_out, vb_out, yb_out, ssum_out, em_out, ups, pieces) = outs
+    (x, wq, wk, wv, wo, e_all, xhat, rstd, mixed, q, probs, kb, vb, yb, ssum, em, bup, ysend, yrecv, send_sems, recv_sems, local_sems) = scratch
     link = Link(dp_size, tp_size, send_sems, recv_sems)
     rows, width = x.shape
     slots, total = e_all.shape
@@ -181,11 +186,13 @@
 
     own_first = link.tp * rows
     e_own = local(e.at[:, rows_at(own_first, rows, rows)], em)
+    early = [local(x_hbm, x), local(wq_hbm, wq)]
     late = [local(e, e_all), local(wk_hbm, wk), local(wv_hbm, wv), local(wo_hbm, wo)]
     link.greet(link.low)
 
     collect = WeightCollect(link, wup.shape[0] // 2, lambda k: ups.at[k - 1])
-    cross = Cross(link, collect, wup)
+    cross = Cross(link, collect, wup, lambda k, h, rows: ups.at[k - 1, rows, :])
+    cross_down = Cross(link, collect, wdn, lambda k, h, rows: pieces.at[k - 1, h])
     cross.start(1)
     vec[...] = jnp.zeros_like(vec)
     for n, vector in enumerate(vectors):
@@ -196,6 +203,7 @@
     position = lax.broadcasted_iota(jnp.int32, (1, rows), 1) + own_first
     live = (position < length).astype(F32)
     e_own.wait()
+    early[0].wait()
     em[...] = (em[...].astype(F32) * live).astype(BF)
     ysend[...] = dot(em[...], x[...], 1, 0).astype(ysend.dtype)
     reduce = [
@@ -205,6 +213,7 @@
     biases = [link.send(bup, bup_all.at[link.tp], (link.dp, link.ahead(k))) for k in others]
     cross.wait(1)
     collect.step(1, 0)
+    early[1].wait()
     q[...] = (dot(x[...], wq[...], 1, 0) + vec[0:1, :]).astype(BF)
     collect.step(1, 1)
     own_slots = place(link.tp, quarter)
@@ -219,6 +228,8 @@
     ]
     for k in (3, 2):
         cross.start(k)
+    for k in (1, 3, 2):
+        cross_down.start(k)
     collect.step(1, 2)
     stores = [local(q, q_out), local(em, em_out)]
     row_live = (lax.broadcasted_iota(jnp.int32, (total, 128), 0) < length).astype(F32).astype(BF)
@@ -247,7 +258,7 @@
     project(wv, 2, vb)
     stores += [local(kb, kb_out), local(vb, vb_out)]
 
-    block = min(256, rows)
+    block = min(BLOCK_F, rows)
     per_pair = rows // block
     probs_sem = used[0]
 
@@ -298,15 +309,18 @@
         return carry
 
     lax.fori_loop(0, per_pair, finish, 0)
+    stores += [local(xhat, xhat_out), local(rstd, rstd_out)]
     tick(FRONT_TICKS[-1])
     cross.wait(2)
+    for k in others:
+        cross_down.wait(k)
     for copy in stores:
         copy.wait()
     for p in range(PAIRS):
         pltpu.make_async_copy(probs.at[p], probs_out.at[p], local_sems.at[probs_sem + p]).wait()
 
 
-def front(mesh, lengths, x, wq, e, wk, wv, wo, wup, vectors, b_up):
+def front(mesh, lengths, x, wq, e, wk, wv, wo, wup, wdn, vectors, b_up):
     dp_size, tp_size = mesh.shape["dp"], mesh.shape["tp"]
     low = min(3, dp_size.bit_length() - 1)
     rows, width = x.shape
@@ -315,6 +329,8 @@
     hbm = pl.BlockSpec(memory_space=pltpu.HBM)
     shape = jax.ShapeDtypeStruct
     moved = (
+        ((rows, width), F32),
+        ((rows, 128), F32),
         ((rows, width), BF),
         ((rows, width), BF),
         ((PAIRS, rows, 2 * slots), BF),
@@ -326,20 +342,20 @@
     )
     kept = (
         ((VECTORS, width), F32),
-        ((rows, width), F32),
-        ((rows, 128), F32),
         ((tp_size, 8, width), F32),
     )
     return pl.pallas_call(
         functools.partial(front_kernel, dp_size, tp_size, len(vectors)),
         out_shape=tuple(shape(*s) for s in kept + moved)
-        + (shape((tp_size - 1, *wup.shape), BF),),
+        + (
+            shape((tp_size - 1, *wup.shape), BF),
+            shape((tp_size - 1, 2, wup.shape[0] >> (low + 1), width), BF),
+        ),
         in_specs=[pl.BlockSpec(memory_space=pltpu.SMEM)]
-        + [vmem] * 2
-        + [hbm] * 5
+        + [hbm] * 8
         + [vmem] * (len(vectors) + 1),
-        out_specs=tuple([vmem] * len(kept) + [hbm] * (len(moved) + 1)),
-        scratch_shapes=[pltpu.VMEM(w.shape, BF) for w in (wk, wv, wo, e)]
+        out_specs=tuple([vmem] * len(kept) + [hbm] * (len(moved) + 2)),
+        scratch_shapes=[pltpu.VMEM(w.shape, BF) for w in (x, wq, wk, wv, wo, e)]
         + [pltpu.VMEM(*s) for s in moved]
         + [
             pltpu.VMEM((8, width), F32),
@@ -347,13 +363,13 @@
             pltpu.VMEM((tp_size - 1, slots // tp_size, width), BF),
             pltpu.SemaphoreType.DMA((FRONT_SEMS,)),
             pltpu.SemaphoreType.DMA((FRONT_SEMS,)),
-            pltpu.SemaphoreType.DMA((24,)),
+            pltpu.SemaphoreType.DMA((32,)),
         ],
         compiler_params=pltpu.CompilerParams(
             collective_id=0, has_side_effects=True, vmem_limit_bytes=VMEM_LIMIT
         ),
         name="front",
-    )(lengths, x, wq, e, wk, wv, wo, wup, *vectors, b_up)
+    )(lengths, x, wq, e, wk, wv, wo, wup, wdn, *vectors, b_up)
 
 
 BACK_SEMS = 128
@@ -382,18 +398,22 @@
         self.stages = len(self.order)
         self.slot = link.take(self.stages)
         self.piece = rows >> self.stages
+        self.insides, self.others, first = [0], [(1 - link.bit(self.order[0])) * (rows >> 1)], 0
+        for j in range(1, self.stages):
+            size = rows >> (j + 1)
+            self.others.append(first + (1 - link.bit(self.order[j])) * size)
+            first = first + link.bit(self.order[j]) * size
+            self.insides.append(first)
+        self.at = link.bit(self.order[0]) * (rows >> 1) + first
 
     def inside(self, i):
-        first = 0
-        for j in range(1, i + 1):
-            first = first + self.link.bit(self.order[j]) * (self.rows >> (j + 1))
-        return first
+        return self.insides[i]
 
     def kept(self):
         return rows_at(self.inside(self.stages - 1), self.piece, 16)
 
     def offset(self):
-        return self.link.bit(self.order[0]) * (self.rows >> 1) + self.inside(self.stages - 1)
+        return self.at
 
     def landed(self, i):
         first = sum(self.rows >> (j + 1) for j in range(i))
@@ -401,8 +421,7 @@
 
     def copy(self, i):
         link, size = self.link, self.rows >> (i + 1)
-        where, base = (self.source, 0) if i == 0 else (self.acc, self.inside(i - 1))
-        other = base + (1 - link.bit(self.order[i])) * size
+        where, other = self.source if i == 0 else self.acc, self.others[i]
         return link.remote(
             self.slot + i, where.at[rows_at(other, size, 16), :], self.landed(i), link.partner(self.order[i])
         )
@@ -435,11 +454,14 @@
         self.link, self.offset, self.piece, self.region = link, offset, piece, region
         self.order = [b for b in order if b < link.low][::-1]
         self.slot = link.take(len(self.order))
+        starts, size = [], piece
+        for b in self.order:
+            starts.append(link.bit(b) * size)
+            size *= 2
+        self.firsts = [sum(starts[i:], 0) for i in range(len(self.order))]
 
     def copy(self, i):
-        size = self.piece << i
-        first = self.offset()
-        first = first - lax.rem(first, size)
+        size, first = self.piece << i, self.firsts[i]
         ref = self.region(first, size)
         return self.link.remote(self.slot + i, ref, ref, self.link.partner(self.order[i]))
 
@@ -516,16 +538,16 @@
     len_ref,
     vec,
     part_vec,
-    xhat,
-    rstd,
-    mixed,
-    wo,
-    ff_far,
-    ff_own,
-    ff_landed,
     ff_near,
     dnorm,
     probs,
+    far_hbm,
+    own_hbm,
+    xhat_hbm,
+    rstd_hbm,
+    mixed_hbm,
+    wo_hbm,
+    landed_hbm,
     x_hbm,
     q_hbm,
     kb_hbm,
@@ -546,6 +568,13 @@
     grad_in,
     ff_out,
     go_out,
+    ff_far,
+    ff_own,
+    xhat,
+    rstd,
+    mixed,
+    wo,
+    ff_landed,
     x,
     q,
     kb,
@@ -602,7 +631,8 @@
     late = []
     for n, (source, target) in enumerate(
         (
-            (q_hbm, q), (kb_hbm, kb), (vb_hbm, vb), (x_hbm, x), (yb_hbm, yb),
+            (far_hbm, ff_far), (own_hbm, ff_own), (xhat_hbm, xhat), (rstd_hbm, rstd), (mixed_hbm, mixed),
+            (wo_hbm, wo), (landed_hbm, ff_landed), (q_hbm, q), (kb_hbm, kb), (vb_hbm, vb), (x_hbm, x), (yb_hbm, yb),
             (wq_hbm, wq), (wk_hbm, wk), (wv_hbm, wv), (ssum_hbm, ssum), (em_hbm, em),
         )
     ):
@@ -612,7 +642,7 @@
 
     lanes = 2
     deep = tp_size // lanes
-    third = width // 3
+    third = width // GRAD_SPLIT
     owned = width // tp_size
 
     ff_track, ff_orders = Track(), ((0, 1, 2), (0, 2, 1))
@@ -628,8 +658,10 @@
             source, k = ((far_acc, 3), (ff_near, 2))[n]
             return link.remote(slot + n, source.at[m], ff_zland.at[m, n], (link.dp, link.behind(k)))
 
-        def offset(m=m, own=own):
-            return link.bit(ff_orders[m][0]) * (width >> 1) + own.offset()
+        at = link.bit(ff_orders[m][0]) * (width >> 1) + own.offset()
+
+        def offset(at=at):
+            return at
 
         widen = Widen(link, wide_ff.at[m])
 
@@ -676,11 +708,13 @@
     stores = []
 
     def store(n, source, target):
-        copy = pltpu.make_async_copy(source, target, local_sems.at[13 + n])
+        copy = pltpu.make_async_copy(source, target, local_sems.at[20 + n])
         stores.append(copy)
         return copy
 
     ff_store, go_store, grad_store = store(0, ff_out, ff_hbm), store(1, go_out, go_hbm), store(2, grad_in, grad_hbm)
+    late[0].wait()
+    late[1].wait()
     ff_begin()
     ff_track.add([ff_second, ff_second_own, then(ff_third, ff_join)])
     ff_track.add([then(*pair) for pair in zip(ff_parts[0][4][1:], ff_parts[1][4][1:])])
@@ -689,28 +723,30 @@
     def square_track(order, out, acc, landing, zland, wide):
         track, spread = Track(), Spread(link, order, width, out, acc, landing)
         q_rows, q_cols = spread.piece // deep, width // lanes
-
-        def quarter(first, t):
+        row_of = [lax.div(t, lanes) * q_rows for t in link.aheads]
+        col_of = [lax.rem(t, lanes) * q_cols for t in link.aheads]
+
+        def quarter(first, k):
             return (
-                rows_at(first + lax.div(t, lanes) * q_rows, q_rows, 16),
-                pl.ds(pl.multiple_of(lax.rem(t, lanes) * q_cols, 128), q_cols),
+                rows_at(first + row_of[k], q_rows, 16),
+                pl.ds(pl.multiple_of(col_of[k], 128), q_cols),
             )
 
         def there(k):
-            return acc.at[quarter(spread.inside(spread.stages - 1), link.ahead(k))], zland.at[k - 1]
+            return acc.at[quarter(spread.inside(spread.stages - 1), k)], zland.at[k - 1]
 
         def again(k):
-            region = out.at[quarter(spread.offset(), link.tp)]
+            region = out.at[quarter(spread.offset(), 0)]
             return region, region
 
         fan, share, widen = Fan(link, there), Fan(link, again), Widen(link, wide)
 
         def join():
             fan.wait()
-            total = acc[quarter(spread.inside(spread.stages - 1), link.tp)].astype(F32)
+            total = acc[quarter(spread.inside(spread.stages - 1), 0)].astype(F32)
             for k in others:
                 total = total + zland[k - 1].astype(F32)
-            mine = quarter(spread.offset(), link.tp)
+            mine = quarter(spread.offset(), 0)
             out[mine] = total.astype(BF)
             widen.run(out.at[mine])
             share.start()
@@ -793,7 +829,7 @@
 
     vec_track.add([vec_last])
 
-    block = min(256, rows)
+    block = min(BLOCK_B, rows)
     count = rows // block
     gain = vec[4:5, :]
 
@@ -817,6 +853,8 @@
 
     zero = jnp.zeros((1, width), F32)
     first_load.wait()
+    late[2].wait()
+    late[3].wait()
     g_gain, g_shift, g_out = lax.fori_loop(0, count, norm_back, (zero, zero, zero))
     vec_acc[0] = part_vec[...]
     vec_acc[0, 3:4, :] = g_out
@@ -825,16 +863,18 @@
     d_attn = dq
 
     def weight_grad(left, right, target):
-        for m in range(3):
+        for m in range(GRAD_SPLIT):
             cols = slice(m * third, (m + 1) * third)
             target[cols, :] = dot(left[:, cols], right[...], 0, 0).astype(BF)
 
+    for load in late[4:7]:
+        load.wait()
     weight_grad(mixed, d_attn, go_out)
     o_track.advance()
     ff_track.advance()
     dmix[...] = dot(d_attn[...], wo[...], 1, 1).astype(BF)
     o_track.advance()
-    for load in late:
+    for load in late[7:]:
         load.wait()
 
     own_half = lax.div(link.tp, 2)
@@ -887,10 +927,10 @@
             dpart[n, under, :] = total[HEAD:, slots:].astype(BF)
 
     d_slot = link.take(tp_size - 1)
+    d_peers = [2 * (1 - own_half) + parity, 2 * (1 - own_half) + (1 - parity), 2 * own_half + (1 - parity)]
 
     def d_copy(j):
-        near = 2 * own_half + (1 - parity)
-        peer = near if j == 2 else 2 * (1 - own_half) + lax.rem(parity + j, 2)
+        peer = d_peers[j]
         block_of = dpart.at[:, rows_at(peer * owned, owned, 64), :]
         return link.remote(d_slot + j, block_of, dland.at[j], (link.dp, peer))
 
@@ -980,13 +1020,13 @@
         copy.wait()
 
 
-def back(mesh, lengths, vec, part_vec, xhat, rstd, mixed, wo, ff_far, ff_own, ff_landed, ff_near, dnorm, probs, *late):
+def back(mesh, lengths, vec, part_vec, ff_near, dnorm, probs, *late):
     dp_size, tp_size = mesh.shape["dp"], mesh.shape["tp"]
     bits = dp_size.bit_length() - 1
     low = min(3, bits)
     wide = max(1, bits - low)
-    rows, width = xhat.shape
-    slots = late[4].shape[0]
+    rows, width = dnorm.shape
+    slots = late[11].shape[0]
     owned = width // tp_size
     others = tp_size - 1
     vmem = pl.BlockSpec(memory_space=pltpu.VMEM)
@@ -1012,7 +1052,7 @@
             shape((tp_size, slots, rows), BF),
             shape((VECTORS, width), F32),
         ),
-        in_specs=[pl.BlockSpec(memory_space=pltpu.SMEM)] + [vmem] * 9 + [hbm] * (3 + len(late)),
+        in_specs=[pl.BlockSpec(memory_space=pltpu.SMEM)] + [vmem] * 2 + [hbm] * (3 + len(late)),
         out_specs=tuple([hbm] * 3 + [vmem] * 4),
         scratch_shapes=[buf(rows, width), buf(2, width, width), buf(width, width)]
         + [pltpu.VMEM(array.shape, array.dtype) for array in late]
@@ -1057,7 +1097,7 @@
             collective_id=1, has_side_effects=True, vmem_limit_bytes=VMEM_LIMIT
         ),
         name="back",
-    )(lengths, vec, part_vec, xhat, rstd, mixed, wo, ff_far, ff_own, ff_landed, ff_near, dnorm, probs, *late)
+    )(lengths, vec, part_vec, ff_near, dnorm, probs, *late)
 
 
 class ChunkSpread:
@@ -1066,20 +1106,27 @@
         self.orders = [[b for b in order if b < link.low] for order in ((0, 1, 2), (0, 2, 1))]
         self.stages = link.low
         self.slot = link.take(2 * link.low * acc.shape[1])
+        self.insides, self.others = [], []
+        for order in self.orders:
+            inside, other, first = [0], [(1 - link.bit(order[0])) * (rows >> 1)], 0
+            for j in range(1, self.stages):
+                size = rows >> (j + 1)
+                other.append(first + (1 - link.bit(order[j])) * size)
+                first = first + link.bit(order[j]) * size
+                inside.append(first)
+            self.insides.append(inside)
+            self.others.append(other)
 
     def inside(self, m, i):
-        first = 0
-        for j in range(1, i + 1):
-            first = first + self.link.bit(self.orders[m][j]) * (self.rows >> (j + 1))
-        return first
+        return self.insides[m][i]
 
     def copy(self, c, m, i):
         link, size = self.link, self.rows >> (i + 1)
         bit = self.orders[m][i]
         if i == 0:
-            source = self.sent.at[m, lax.rem(c, 2), rows_at((1 - link.bit(bit)) * size, size, 16), :]
+            source = self.sent.at[m, lax.rem(c, 2), rows_at(self.others[m][i], size, 16), :]
         else:
-            source = self.acc.at[m, c, rows_at(self.inside(m, i - 1) + (1 - link.bit(bit)) * size, size, 16), :]
+            source = self.acc.at[m, c, rows_at(self.others[m][i], size, 16), :]
         first = sum(self.rows >> (j + 1) for j in range(i))
         slot = self.slot + (i * 2 + m) * self.acc.shape[1] + c
         return link.remote(slot, source, self.landing.at[m, c, pl.ds(first, size), :], link.partner(bit))
@@ -1103,12 +1150,12 @@
 
 MIDDLE_SEMS = 96
 MIDDLE_TICKS = (
-    (),
-    ((0, 2, 1), (1, 1, 0), (1, 3, 0)),
-    ((1, 1, 1),),
-    ((0, 2, 2), (1, 3, 1), (1, 2, 0)),
-    ((1, 1, 2),),
-    ((0, 2, 3), (1, 3, 2), (1, 2, 1)),
+    ((0, 2, 1),),
+    ((1, 1, 1), (1, 3, 0)),
+    ((0, 2, 2),),
+    ((1, 1, 2), (1, 3, 1), (1, 2, 0)),
+    ((0, 2, 3),),
+    ((1, 3, 2), (1, 2, 1)),
     ((1, 1, 3),),
     ((1, 2, 2), (1, 3, 3), (1, 2, 3)),
 )
@@ -1119,12 +1166,13 @@
     tp_size,
     vec,
     bup_all,
-    xhat,
+    xhat_hbm,
     out_grad_hbm,
     own_up,
     own_dn,
     ups,
-    layer_out,
+    pieces,
+    layer_hbm,
     dnorm,
     part_vec,
     ff_landed,
@@ -1132,6 +1180,8 @@
     ff_far,
     ff_own,
     whole,
+    xhat,
+    layer_out,
     out_grad,
     nb,
     act,
@@ -1156,22 +1206,25 @@
         return copy
 
     collect = WeightCollect(link, width // 2, lambda k: whole.at[1, k])
-    cross = Cross(link, collect, own_dn)
+    xhat_load = local(xhat_hbm, xhat)
     up_last = WeightCollect(link, width // 2, lambda k: whole.at[0, 2])
     placed = [
         local(ups.at[1, up_last.rows(h, 0), :], whole.at[0, 2, up_last.rows(h, 0), :]) for h in range(2)
+    ]
+    placed += [
+        local(pieces.at[k - 1, h], whole.at[1, k, collect.rows(h, 0), :]) for k in (1, 3, 2) for h in range(2)
     ]
     owns = [local(own_up, whole.at[0, 0])]
     owns += [local(ups.at[k - 1], whole.at[0, k]) for k in (1, 3)]
     owns += [local(own_dn, whole.at[1, 0]), local(out_grad_hbm, out_grad)]
     link.greet(link.low)
-    for k in (1, 3, 2):
-        cross.start(k)
     for copy in placed:
         copy.wait()
     up_last.step(2, 0)
+    collect.step(1, 0)
+    xhat_load.wait()
     gain, shift, b_down, f_gain, f_shift = (vec[n : n + 1, :] for n in (4, 5, 6, 7, 8))
-    block = min(256, rows)
+    block = min(BLOCK_M, rows)
     count = rows // block
     big = rows // 2
 
@@ -1197,8 +1250,6 @@
             @pl.when(step == n)
             def _():
                 for m, shard, j in ticks:
-                    if m == 1 and j == 0:
-                        cross.wait(shard)
                     (up_last, collect)[m].step(shard, j)
 
         return carry
@@ -1235,16 +1286,17 @@
 
     zero = jnp.zeros((1, width), F32)
     g_gain, g_shift, g_down = lax.fori_loop(0, count, second_norm, (zero, zero, zero))
+    layer_store = local(layer_out, layer_hbm)
     part_vec[...] = jnp.zeros_like(part_vec)
     part_vec[6:7, :] = g_gain
     part_vec[7:8, :] = g_shift
     part_vec[8:9, :] = g_down
 
     spread = ChunkSpread(link, width, sent, acc, landing)
-    third = width // 3
+    third = width // GRAD_SPLIT
 
     def weight_grad(left, first, right, cols, target):
-        for m in range(3):
+        for m in range(GRAD_SPLIT):
             mine = pl.ds(pl.multiple_of(first + m * third, third), third)
             target[m * third : (m + 1) * third, :] = dot(left[:, mine], right[:, cols], 0, 0).astype(BF)
 
@@ -1314,11 +1366,11 @@
         stores.append(local(acc.at[m, 1, at, :], ff_near.at[m]))
         at = rows_at(spread.inside(m, 1), width >> 2, 16)
         stores.append(local(acc.at[m, 2, at, :], ff_far.at[m]))
-    for copy in crossing + stores:
+    for copy in crossing + stores + [layer_store]:
         copy.wait()
 
 
-def middle(mesh, vec, bup_all, xhat, out_grad, w_up, w_dn, ups):
+def middle(mesh, vec, bup_all, xhat, out_grad, w_up, w_dn, ups, pieces):
     dp_size, tp_size = mesh.shape["dp"], mesh.shape["tp"]
     low = min(3, dp_size.bit_length() - 1)
     assert low == 3 and tp_size == 4
@@ -1342,10 +1394,12 @@
             shape((2, width >> 2, width), BF),
             shape((2, width >> 1, width), BF),
         ),
-        in_specs=[vmem] * 3 + [hbm] * 4,
-        out_specs=(vmem, hbm, vmem, hbm, hbm, hbm, hbm),
+        in_specs=[vmem] * 2 + [hbm] * 6,
+        out_specs=(hbm, hbm, vmem, hbm, hbm, hbm, hbm),
         scratch_shapes=[
             buf(2, tp_size, width, width),
+            buf(rows, width, dtype=F32),
+            buf(rows, width),
             buf(rows, width),
             buf(rows, width),
             buf(rows, hidden),
@@ -1357,13 +1411,13 @@
             buf(2, tp_size, sum(width >> (i + 1) for i in range(low)), width),
             pltpu.SemaphoreType.DMA((MIDDLE_SEMS,)),
             pltpu.SemaphoreType.DMA((MIDDLE_SEMS,)),
-            pltpu.SemaphoreType.DMA((24,)),
+            pltpu.SemaphoreType.DMA((32,)),
         ],
         compiler_params=pltpu.CompilerParams(
             collective_id=2, has_side_effects=True, vmem_limit_bytes=VMEM_LIMIT
         ),
         name="middle",
-    )(vec, bup_all, xhat, out_grad, w_up, w_dn, ups)
+    )(vec, bup_all, xhat, out_grad, w_up, w_dn, ups, pieces)
 
 
 def finish_kernel(
@@ -1463,14 +1517,14 @@
     row_count, width = layer_in.shape
     tp_size = mesh.shape["tp"]
     vectors = (b_query, b_key, b_value, b_out, attn_gain, attn_shift, b_down, ffn_gain, ffn_shift)
-    vec, xhat, rstd, bup_all, mixed, queries, probs, kb, vb, folded, ssum, own_proj, ups = front(
-        mesh, lengths, layer_in, w_query, seq_proj, w_key, w_value, w_out, w_up, vectors, b_up
+    vec, bup_all, xhat, rstd, mixed, queries, probs, kb, vb, folded, ssum, own_proj, ups, pieces = front(
+        mesh, lengths, layer_in, w_query, seq_proj, w_key, w_value, w_out, w_up, w_down, vectors, b_up
     )
     layer_out, d_normed, part_vec, ff_landed, ff_near, ff_far, ff_own = middle(
-        mesh, vec, bup_all, xhat, out_grad, w_up, w_down, ups
+        mesh, vec, bup_all, xhat, out_grad, w_up, w_down, ups, pieces
     )
     grad_in, g_ff, g_o, g_q, g_kv, g_seq, vec_sum = back(
-        mesh, lengths, vec, part_vec, xhat, rstd, mixed, w_out, ff_far, ff_own, ff_landed, ff_near, d_normed, probs,
+        mesh, lengths, vec, part_vec, ff_near, d_normed, probs, ff_far, ff_own, xhat, rstd, mixed, w_out, ff_landed,
         layer_in, queries, kb, vb, folded, ssum, own_proj, w_query, w_key, w_value
     )
     (

time: 270 us -> 265 us (0.981)
  Pallas kernels: 268 us -> 263 us
    pallas_call x1, Pallas kernels: 117 us -> 113 us  [back(): pl.pallas_call(functools.partial(back_kernel, dp_size, tp_size), out_shap...]
    pallas_call x1, Pallas kernels: 86.8 us -> 83.2 us  [middle(): pl.pallas_call(functools.partial(middle_kernel, dp_size, tp_size), out_sh...]
where the time goes in v5:
time: 265 us
  Pallas kernels  263 us (99%)
    pallas_call x1, Pallas kernels, back(): pl.pallas_call(functools.partial(back_kernel, dp_size, tp_size), out_shap...  113 us
    pallas_call x1, Pallas kernels, middle(): pl.pallas_call(functools.partial(middle_kernel, dp_size, tp_size), out_sh...  83.2 us
    pallas_call x1, Pallas kernels, front(): pl.pallas_call(functools.partial(front_kernel, dp_size, tp_size, len(vect...  54.5 us
    pallas_call x1, Pallas kernels, finish(): pl.pallas_call(functools.partial(finish_kernel, tp_size), out_shape=tuple...  13.1 us

profile of v5, /device:TPU:0, one launch (start us, length us, event | category | flops | bytes accessed | tf_op | source)
XLA Modules:
  0.0 264.8 jit_solution(800927122281532147)
XLA Ops:
  1.3 54.5 %front.1 = (f32[16,768]{1,0:T(8,128)}, f32[4,8,768]{2,1,0:T(8,128)}, f32[1024,768]{1,0:T(8,128)}, f32[1024,128]{1,0:T(8,128)}, bf16[1024,768]{1,0:T(8,128)(2,1)}...) custom-call(s32[1]{0:T(128)S(6)} %copy.39.len_ref, ...), custom_call_target="tpu_custom_call" | custom-call | tf_op jit(solution)/shard_map/front/pallas_call | solution.py:347
  55.8 83.2 %middle.1 = (bf16[1024,768]{1,0:T(8,128)(2,1)}, f32[1024,768]{1,0:T(8,128)}, f32[16,768]{1,0:T(8,128)}, bf16[2,96,768]{2,1,0:T(8,128)(2,1)}, bf16[2,96,768]{2,1,...) custom-call(f32[16,768]{1,0:T(8,128)} %get-tuple-element.66.vec, ...), custom_call_target="tpu_custom_call" | custom-call | tf_op jit(solution)/shard_map/middle/pallas_call | solution.py:1386
  139.0 112.6 %back.1 = (bf16[1024,768]{1,0:T(8,128)(2,1)}, bf16[2,768,768]{2,1,0:T(8,128)(2,1)}, bf16[768,768]{1,0:T(8,128)(2,1)}, bf16[768,768]{1,0:T(8,128)(2,1)}, bf16[4,3...) custom-call(s32[1]{0:T(128)S(6)} %copy.39.len_ref, f32[16,768]{1,0:T(8,128)} %get-tuple-element.66.vec, ...), custom_call_target="tpu_custom_call" | custom-call | tf_op jit(solution)/shard_map/back/pallas_call | solution.py:1044
  251.6 13.1 %finish.1 = (f32[768,768]{1,0:T(8,128)}, f32[768,768]{1,0:T(8,128)}, f32[768,768]{1,0:T(8,128)}, f32[768,768]{1,0:T(8,128)}, f32[768,768]{1,0:T(8,128)}, /*index...) custom-call(bf16[2,768,768]{2,1,0:T(8,128)(2,1)} %get-tuple-element., ...), custom_call_target="tpu_custom_call" | custom-call | tf_op jit(solution)/shard_map/finish/pallas_call | solution.py:1478

commit v6 on v5

--- a/solution.py
+++ b/solution.py
@@ -155,21 +155,16 @@
             copy.wait()
 
 
-FRONT_TICKS = (
-    ((3, 0),),
-    (),
-    ((3, 1),),
-    (),
-    ((3, 2),),
-    (),
-    ((3, 3),),
-)
+EARLY_TICKS = ((0, 1, 0), (1, 1, 0), (0, 1, 1), (1, 3, 0), (1, 1, 1), (0, 1, 2), (1, 3, 1), (1, 1, 2))
+SHARE_TICKS = ((0, 1, 3), (1, 3, 2), (1, 1, 3), (1, 3, 3))
+PAIR_TICKS = {1: ((0, 3, 0),), 3: ((0, 3, 1),), 5: ((0, 3, 2), (0, 2, 0))}
+LAST_TICKS = ((0, 3, 3), (0, 2, -2), (1, 2, -1))
 
 
 def front_kernel(dp_size, tp_size, n_vectors, len_ref, x_hbm, wq_hbm, e, wk_hbm, wv_hbm, wo_hbm, wup, wdn, *rest):
     vectors, b_up, rest = rest[:n_vectors], rest[n_vectors], rest[n_vectors + 1 :]
     outs, scratch = rest[:14], rest[14:]
-    (vec, bup_all, xhat_out, rstd_out, mixed_out, q_out, probs_out, kb_out, vb_out, yb_out, ssum_out, em_out, ups, pieces) = outs
+    (vec, bup_all, xhat_out, rstd_out, mixed_out, q_out, probs_out, kb_out, vb_out, yb_out, ssum_out, em_out, ups, downs) = outs
     (x, wq, wk, wv, wo, e_all, xhat, rstd, mixed, q, probs, kb, vb, yb, ssum, em, bup, ysend, yrecv, send_sems, recv_sems, local_sems) = scratch
     link = Link(dp_size, tp_size, send_sems, recv_sems)
     rows, width = x.shape
@@ -192,8 +187,21 @@
 
     collect = WeightCollect(link, wup.shape[0] // 2, lambda k: ups.at[k - 1])
     cross = Cross(link, collect, wup, lambda k, h, rows: ups.at[k - 1, rows, :])
-    cross_down = Cross(link, collect, wdn, lambda k, h, rows: pieces.at[k - 1, h])
+    cross_down = Cross(link, collect, wdn, lambda k, h, rows: downs.at[k - 1, rows, :])
+    collect_down = WeightCollect(link, wdn.shape[0] // 2, lambda k: downs.at[k - 1])
+    def tick(ticks):
+        for m, k, j in ticks:
+            if -1 <= j <= 0:
+                (cross, cross_down)[m].wait(k)
+            if j == -2:
+                for copy in (collect, collect_down)[m].copies(k, 0):
+                    copy.wait()
+            elif j >= 0:
+                (collect, collect_down)[m].step(k, j)
+
     cross.start(1)
+    cross_down.start(1)
+    cross_down.start(3)
     vec[...] = jnp.zeros_like(vec)
     for n, vector in enumerate(vectors):
         vec[n : n + 1, :] = vector[...].astype(F32).reshape(1, width)
@@ -211,11 +219,9 @@
         for k in others
     ]
     biases = [link.send(bup, bup_all.at[link.tp], (link.dp, link.ahead(k))) for k in others]
-    cross.wait(1)
-    collect.step(1, 0)
     early[1].wait()
     q[...] = (dot(x[...], wq[...], 1, 0) + vec[0:1, :]).astype(BF)
-    collect.step(1, 1)
+    tick(EARLY_TICKS)
     own_slots = place(link.tp, quarter)
     for copy in reduce:
         copy.wait()
@@ -228,9 +234,8 @@
     ]
     for k in (3, 2):
         cross.start(k)
-    for k in (1, 3, 2):
-        cross_down.start(k)
-    collect.step(1, 2)
+    cross_down.start(2)
+    tick(SHARE_TICKS)
     stores = [local(q, q_out), local(em, em_out)]
     row_live = (lax.broadcasted_iota(jnp.int32, (total, 128), 0) < length).astype(F32).astype(BF)
     for load in late:
@@ -240,7 +245,6 @@
         copy.wait()
     for copy in biases:
         copy.wait()
-    collect.step(1, 3)
     stores += [local(yb, yb_out), local(ssum, ssum_out)]
 
     lane = lax.broadcasted_iota(jnp.int32, (1, PAIR), 1)
@@ -261,12 +265,6 @@
     block = min(BLOCK_F, rows)
     per_pair = rows // block
     probs_sem = used[0]
-
-    def tick(ticks):
-        for k, j in ticks:
-            if j == 0:
-                cross.wait(k)
-            collect.step(k, j)
 
     def attend(p, carry):
         cols = place(p, PAIR)
@@ -287,7 +285,7 @@
 
         lax.fori_loop(0, per_pair, one, 0)
         pltpu.make_async_copy(probs.at[p], probs_out.at[p], local_sems.at[probs_sem + p]).start()
-        for n, ticks in enumerate(FRONT_TICKS[:-1]):
+        for n, ticks in PAIR_TICKS.items():
 
             @pl.when(p == n)
             def _():
@@ -310,10 +308,7 @@
 
     lax.fori_loop(0, per_pair, finish, 0)
     stores += [local(xhat, xhat_out), local(rstd, rstd_out)]
-    tick(FRONT_TICKS[-1])
-    cross.wait(2)
-    for k in others:
-        cross_down.wait(k)
+    tick(LAST_TICKS)
     for copy in stores:
         copy.wait()
     for p in range(PAIRS):
@@ -349,7 +344,7 @@
         out_shape=tuple(shape(*s) for s in kept + moved)
         + (
             shape((tp_size - 1, *wup.shape), BF),
-            shape((tp_size - 1, 2, wup.shape[0] >> (low + 1), width), BF),
+            shape((tp_size - 1, *wdn.shape), BF),
         ),
         in_specs=[pl.BlockSpec(memory_space=pltpu.SMEM)]
         + [hbm] * 8
@@ -1149,16 +1144,7 @@
 
 
 MIDDLE_SEMS = 96
-MIDDLE_TICKS = (
-    ((0, 2, 1),),
-    ((1, 1, 1), (1, 3, 0)),
-    ((0, 2, 2),),
-    ((1, 1, 2), (1, 3, 1), (1, 2, 0)),
-    ((0, 2, 3),),
-    ((1, 3, 2), (1, 2, 1)),
-    ((1, 1, 3),),
-    ((1, 2, 2), (1, 3, 3), (1, 2, 3)),
-)
+MIDDLE_TICKS = {3: ((1, 1),), 5: ((0, 2), (0, 3)), 7: ((1, 2), (1, 3))}
 
 
 def middle_kernel(
@@ -1171,7 +1157,7 @@
     own_up,
     own_dn,
     ups,
-    pieces,
+    downs,
     layer_hbm,
     dnorm,
     part_vec,
@@ -1207,21 +1193,23 @@
 
     collect = WeightCollect(link, width // 2, lambda k: whole.at[1, k])
     xhat_load = local(xhat_hbm, xhat)
-    up_last = WeightCollect(link, width // 2, lambda k: whole.at[0, 2])
+    up_last = WeightCollect(link, width // 2, lambda k: whole.at[0, k])
     placed = [
-        local(ups.at[1, up_last.rows(h, 0), :], whole.at[0, 2, up_last.rows(h, 0), :]) for h in range(2)
+        local(ups.at[1, up_last.rows(h, 1), :], whole.at[0, 2, up_last.rows(h, 1), :]) for h in range(2)
     ]
     placed += [
-        local(pieces.at[k - 1, h], whole.at[1, k, collect.rows(h, 0), :]) for k in (1, 3, 2) for h in range(2)
+        local(downs.at[1, collect.rows(h, 0), :], whole.at[1, 2, collect.rows(h, 0), :]) for h in range(2)
     ]
     owns = [local(own_up, whole.at[0, 0])]
     owns += [local(ups.at[k - 1], whole.at[0, k]) for k in (1, 3)]
-    owns += [local(own_dn, whole.at[1, 0]), local(out_grad_hbm, out_grad)]
+    owns += [local(own_dn, whole.at[1, 0])] + [local(downs.at[k - 1], whole.at[1, k]) for k in (1, 3)]
+    owns.append(local(out_grad_hbm, out_grad))
     link.greet(link.low)
     for copy in placed:
         copy.wait()
-    up_last.step(2, 0)
-    collect.step(1, 0)
+    collect.step(2, 0)
+    for copy in up_last.copies(2, 1):
+        copy.start()
     xhat_load.wait()
     gain, shift, b_down, f_gain, f_shift = (vec[n : n + 1, :] for n in (4, 5, 6, 7, 8))
     block = min(BLOCK_M, rows)
@@ -1234,7 +1222,7 @@
         return carry
 
     lax.fori_loop(0, count, norm, 0)
-    for copy in owns[:3]:
+    for copy in owns[: tp_size - 1]:
         copy.wait()
 
     def forward(step, carry):
@@ -1245,17 +1233,17 @@
         cdf = 0.5 * (1.0 + lax.erf(pre * 0.7071067811865476))
         act[here, cols] = (pre * cdf).astype(BF)
         slope[here, cols] = (cdf + pre * (jnp.exp(pre * pre * -0.5) * 0.3989422804014327)).astype(BF)
-        for n, ticks in enumerate(MIDDLE_TICKS):
+        for n, ticks in MIDDLE_TICKS.items():
 
             @pl.when(step == n)
             def _():
-                for m, shard, j in ticks:
-                    (up_last, collect)[m].step(shard, j)
+                for m, j in ticks:
+                    (up_last, collect)[m].step(2, j)
 
         return carry
 
     lax.fori_loop(0, 2 * tp_size, forward, 0)
-    for copy in owns[3:]:
+    for copy in owns[tp_size - 1 :]:
         copy.wait()
 
     def second_norm(step, carry):
@@ -1370,7 +1358,7 @@
         copy.wait()
 
 
-def middle(mesh, vec, bup_all, xhat, out_grad, w_up, w_dn, ups, pieces):
+def middle(mesh, vec, bup_all, xhat, out_grad, w_up, w_dn, ups, downs):
     dp_size, tp_size = mesh.shape["dp"], mesh.shape["tp"]
     low = min(3, dp_size.bit_length() - 1)
     assert low == 3 and tp_size == 4
@@ -1417,7 +1405,7 @@
             collective_id=2, has_side_effects=True, vmem_limit_bytes=VMEM_LIMIT
         ),
         name="middle",
-    )(vec, bup_all, xhat, out_grad, w_up, w_dn, ups, pieces)
+    )(vec, bup_all, xhat, out_grad, w_up, w_dn, ups, downs)
 
 
 def finish_kernel(
@@ -1517,11 +1505,11 @@
     row_count, width = layer_in.shape
     tp_size = mesh.shape["tp"]
     vectors = (b_query, b_key, b_value, b_out, attn_gain, attn_shift, b_down, ffn_gain, ffn_shift)
-    vec, bup_all, xhat, rstd, mixed, queries, probs, kb, vb, folded, ssum, own_proj, ups, pieces = front(
+    vec, bup_all, xhat, rstd, mixed, queries, probs, kb, vb, folded, ssum, own_proj, ups, downs = front(
         mesh, lengths, layer_in, w_query, seq_proj, w_key, w_value, w_out, w_up, w_down, vectors, b_up
     )
     layer_out, d_normed, part_vec, ff_landed, ff_near, ff_far, ff_own = middle(
-        mesh, vec, bup_all, xhat, out_grad, w_up, w_down, ups, pieces
+        mesh, vec, bup_all, xhat, out_grad, w_up, w_down, ups, downs
     )
     grad_in, g_ff, g_o, g_q, g_kv, g_seq, vec_sum = back(
         mesh, lengths, vec, part_vec, ff_near, d_normed, probs, ff_far, ff_own, xhat, rstd, mixed, w_out, ff_landed,

time: 265 us -> 257 us (0.970)
  Pallas kernels: 263 us -> 255 us
    pallas_call x1, Pallas kernels: 83.2 us -> 70.3 us  [middle(): pl.pallas_call(functools.partial(middle_kernel, dp_size, tp_size), out_sh...]
    pallas_call x1, Pallas kernels: 54.5 us -> 57.6 us  [front(): pl.pallas_call(functools.partial(front_kernel, dp_size, tp_size, len(vect...]
where the time goes in v6:
time: 257 us; the launch traced here: 256 us
  Pallas kernels  255 us (99%)
    pallas_call x1, Pallas kernels, back(): pl.pallas_call(functools.partial(back_kernel, dp_size, tp_size), out_shap...  114 us
    pallas_call x1, Pallas kernels, middle(): pl.pallas_call(functools.partial(middle_kernel, dp_size, tp_size), out_sh...  70.3 us
    pallas_call x1, Pallas kernels, front(): pl.pallas_call(functools.partial(front_kernel, dp_size, tp_size, len(vect...  57.6 us
    pallas_call x1, Pallas kernels, finish(): pl.pallas_call(functools.partial(finish_kernel, tp_size), out_shape=tuple...  13.1 us

profile of v6, /device:TPU:0, one launch (start us, length us, event | category | flops | bytes accessed | tf_op | source)
XLA Modules:
  0.0 256.2 jit_solution(6738748920559874634)
XLA Ops:
  1.3 57.6 %front.1 = (f32[16,768]{1,0:T(8,128)}, f32[4,8,768]{2,1,0:T(8,128)}, f32[1024,768]{1,0:T(8,128)}, f32[1024,128]{1,0:T(8,128)}, bf16[1024,768]{1,0:T(8,128)(2,1)}...) custom-call(s32[1]{0:T(128)S(6)} %copy.39.len_ref, ...), custom_call_target="tpu_custom_call" | custom-call | tf_op jit(solution)/shard_map/front/pallas_call | solution.py:342
  58.9 70.3 %middle.1 = (bf16[1024,768]{1,0:T(8,128)(2,1)}, f32[1024,768]{1,0:T(8,128)}, f32[16,768]{1,0:T(8,128)}, bf16[2,96,768]{2,1,0:T(8,128)(2,1)}, bf16[2,96,768]{2,1,...) custom-call(f32[16,768]{1,0:T(8,128)} %get-tuple-element.66.vec, ...), custom_call_target="tpu_custom_call" | custom-call | tf_op jit(solution)/shard_map/middle/pallas_call | solution.py:1374
  129.3 113.7 %back.1 = (bf16[1024,768]{1,0:T(8,128)(2,1)}, bf16[2,768,768]{2,1,0:T(8,128)(2,1)}, bf16[768,768]{1,0:T(8,128)(2,1)}, bf16[768,768]{1,0:T(8,128)(2,1)}, bf16[4,3...) custom-call(s32[1]{0:T(128)S(6)} %copy.39.len_ref, f32[16,768]{1,0:T(8,128)} %get-tuple-element.66.vec, ...), custom_call_target="tpu_custom_call" | custom-call | tf_op jit(solution)/shard_map/back/pallas_call | solution.py:1039
  243.0 13.1 %finish.1 = (f32[768,768]{1,0:T(8,128)}, f32[768,768]{1,0:T(8,128)}, f32[768,768]{1,0:T(8,128)}, f32[768,768]{1,0:T(8,128)}, f32[768,768]{1,0:T(8,128)}, /*index...) custom-call(bf16[2,768,768]{2,1,0:T(8,128)(2,1)} %get-tuple-element., ...), custom_call_target="tpu_custom_call" | custom-call | tf_op jit(solution)/shard_map/finish/pallas_call | solution.py:1466

commit v7 on v6

--- a/solution.py
+++ b/solution.py
@@ -587,6 +587,7 @@
     prob_slots,
     dpart,
     dland,
+    dcross,
     dfull,
     ff_zland,
     far_acc,
@@ -715,43 +716,48 @@
     ff_track.add([then(*pair) for pair in zip(ff_parts[0][4][1:], ff_parts[1][4][1:])])
     ff_track.add([ff_store.start], join=True)
 
-    def square_track(order, out, acc, landing, zland, wide):
-        track, spread = Track(), Spread(link, order, width, out, acc, landing)
-        q_rows, q_cols = spread.piece // deep, width // lanes
-        row_of = [lax.div(t, lanes) * q_rows for t in link.aheads]
-        col_of = [lax.rem(t, lanes) * q_cols for t in link.aheads]
-
-        def quarter(first, k):
-            return (
-                rows_at(first + row_of[k], q_rows, 16),
-                pl.ds(pl.multiple_of(col_of[k], 128), q_cols),
+    def square_track(out, acc, landing, zland, wide):
+        track, spreads, collects = Track(), [], []
+        q_cols = width // lanes
+        for h, order in enumerate(((0, 1, 2), (0, 2, 1))):
+            cols = slice(h * q_cols, (h + 1) * q_cols)
+            spread = Spread(link, order, width, out.at[:, cols], acc.at[:, cols], landing.at[:, cols])
+            spreads.append(spread)
+            collects.append(
+                Collect(
+                    link, order, spread.offset, spread.piece,
+                    lambda first, size, cols=cols: out.at[rows_at(first, size, 16), cols],
+                )
             )
-
-        def there(k):
-            return acc.at[quarter(spread.inside(spread.stages - 1), k)], zland.at[k - 1]
-
-        def again(k):
-            region = out.at[quarter(spread.offset(), 0)]
-            return region, region
-
-        fan, share, widen = Fan(link, there), Fan(link, again), Widen(link, wide)
+        q_rows = spreads[0].piece // deep
+        halves = [lax.rem(t, lanes) for t in link.aheads]
+
+        def quarter(firsts, k):
+            first = firsts[0] + halves[k] * (firsts[1] - firsts[0]) + lax.div(link.aheads[k], lanes) * q_rows
+            return rows_at(first, q_rows, 16), pl.ds(pl.multiple_of(halves[k] * q_cols, 128), q_cols)
+
+        inner = [quarter([spread.inside(spread.stages - 1) for spread in spreads], k) for k in range(tp_size)]
+        mine = quarter([spread.offset() for spread in spreads], 0)
+        fan = Fan(link, lambda k: (acc.at[inner[k]], zland.at[k - 1]))
+        share, widen = Fan(link, lambda k: (out.at[mine], out.at[mine])), Widen(link, wide)
 
         def join():
             fan.wait()
-            total = acc[quarter(spread.inside(spread.stages - 1), 0)].astype(F32)
+            total = acc[inner[0]].astype(F32)
             for k in others:
                 total = total + zland[k - 1].astype(F32)
-            mine = quarter(spread.offset(), 0)
             out[mine] = total.astype(BF)
             widen.run(out.at[mine])
             share.start()
 
-        collect = Collect(
-            link, order, spread.offset, spread.piece, lambda first, size: out.at[rows_at(first, size, 16), :]
-        )
-        track.add(spread.steps())
-        track.add([then(lambda: spread.finish(spread.stages - 1), fan.start), join, share.wait])
-        track.add(collect.steps(), join=True)
+        def summed():
+            for spread in spreads:
+                spread.finish(spread.stages - 1)
+            fan.start()
+
+        track.add([then(*pair) for pair in zip(spreads[0].steps(), spreads[1].steps())])
+        track.add([summed, join, share.wait])
+        track.add([then(*pair) for pair in zip(collects[0].steps(), collects[1].steps())], join=True)
         return track
 
     def owned_track(order, total_rows, cols, source, acc, landing, out, wide):
@@ -779,9 +785,9 @@
         track.add(collect.steps(), join=True)
         return track
 
-    o_track = square_track((0, 1, 2), go_out, o_acc, o_land, o_zland, wide_q.at[0])
+    o_track = square_track(go_out, o_acc, o_land, o_zland, wide_q.at[0])
     o_track.add([go_store.start], join=True)
-    q_track = square_track((0, 2, 1), gq_out, q_acc, q_land, q_zland, wide_q.at[1])
+    q_track = square_track(gq_out, q_acc, q_land, q_zland, wide_q.at[1])
     def halves(total_rows, source, acc, landing, out, wide):
         tracks = []
         for h, order in enumerate(((0, 1, 2), (0, 2, 1))):
@@ -922,25 +928,33 @@
             dpart[n, under, :] = total[HEAD:, slots:].astype(BF)
 
     d_slot = link.take(tp_size - 1)
-    d_peers = [2 * (1 - own_half) + parity, 2 * (1 - own_half) + (1 - parity), 2 * own_half + (1 - parity)]
+    sibling = 2 * own_half + (1 - parity)
+    far_same = rows_at((2 * (1 - own_half) + parity) * owned, owned, 64)
+    far_other = rows_at((2 * (1 - own_half) + (1 - parity)) * owned, owned, 64)
+    d_peers = [2 * (1 - own_half) + parity, sibling, sibling]
+    d_sources = [
+        dcross, dpart.at[:, far_other, :], dpart.at[:, rows_at(sibling * owned, owned, 64), :],
+    ]
 
     def d_copy(j):
-        peer = d_peers[j]
-        block_of = dpart.at[:, rows_at(peer * owned, owned, 64), :]
-        return link.remote(d_slot + j, block_of, dland.at[j], (link.dp, peer))
-
-    events = [
-        then(),
-        then(lambda: d_copy(1).start(), ff_track.advance),
-        lambda: d_copy(0).start(),
-        o_track.advance,
-        then(lambda: d_copy(2).start(), ff_track.advance),
-        then(),
-    ]
+        return link.remote(d_slot + j, d_sources[j], dland.at[j], (link.dp, d_peers[j]))
+
+    def d_across():
+        d_copy(1).wait()
+        for n in range(2):
+            dcross[n] = (dpart[n, far_same, :].astype(F32) + dland[1, n].astype(F32)).astype(BF)
+        d_copy(0).start()
+
+    events = {
+        1: lambda: d_copy(1).start(),
+        2: ff_track.advance,
+        4: lambda: d_copy(2).start(),
+        5: then(d_across, o_track.advance),
+    }
 
     def one(n, carry):
         attend_back(n)
-        for i, event in enumerate(events):
+        for i, event in events.items():
             pl.when(n == i)(event)
         return carry
 
@@ -958,30 +972,43 @@
     lax.fori_loop(0, count, input_grad, 0)
     q_track.advance()
     vec_acc[0, 0:1, :] = jnp.sum(dq[...].astype(F32), axis=0, keepdims=True)
-
-    for j in range(tp_size - 1):
+    o_track.advance()
+
+    for j in (0, 2):
         d_copy(j).wait()
     own_block = rows_at(link.tp * owned, owned, 64)
     for n in range(2):
         total = dpart[n, own_block, :].astype(F32)
-        for j in range(tp_size - 1):
+        for j in (0, 2):
             total = total + dland[j, n].astype(F32)
         dfull[n, own_block, :] = total.astype(BF)
-    d_share = Fan(link, lambda k: (dfull.at[:, own_block, :], dfull.at[:, own_block, :]))
-    d_share.start()
+    share_slot = link.take(3)
+    share_plan = ((own_block, d_peers[0]), (own_block, sibling), (far_same, sibling))
+
+    def share_copy(n):
+        block_rows, peer = share_plan[n]
+        return link.remote(
+            share_slot + n, dfull.at[:, block_rows, :], dfull.at[:, block_rows, :], (link.dp, peer)
+        )
+
+    share_copy(0).start()
+    share_copy(1).start()
     ff_track.advance()
     for n in range(2):
         kv_send[n * owned : (n + 1) * owned, :] = dot(dfull[n, own_block, :], yb[...], 1, 0).astype(BF)
     kv_track.advance()
+    o_track.advance()
+    q_track.advance()
+    kv_track.advance()
+    ff_track.advance()
+    share_copy(0).wait()
+    share_copy(2).start()
+    kv_track.advance()
     q_track.advance()
     ff_track.advance()
     kv_track.advance()
-    o_track.advance()
-    kv_track.advance()
-    q_track.advance()
-    kv_track.advance()
-    o_track.advance()
-    d_share.wait()
+    share_copy(1).wait()
+    share_copy(2).wait()
     backs = dot(wk[...], dfull[0], 1, 0) + dot(wv[...], dfull[1], 1, 0)
     back = backs.T.astype(BF)
     small = vec[0:8, :].astype(BF)
@@ -1007,7 +1034,10 @@
 
     lax.fori_loop(0, count, input_grad_last, 0)
     grad_store.start()
-    tracks = [s_track, kv_track, q_track, o_track, vec_track, ff_track]
+    tracks = {"s": s_track, "k": kv_track, "q": q_track, "o": o_track, "v": vec_track, "f": ff_track}
+    for name in "oqskvosqkvoqskvqsokvsqs":
+        tracks[name].advance()
+    tracks = list(tracks.values())
     while any(track.todo for track in tracks):
         for track in tracks:
             track.advance()
@@ -1059,6 +1089,7 @@
             buf(2, rows, 2 * slots),
             buf(2, width, slots),
             buf(others, 2, owned, slots),
+            buf(2, owned, slots),
             buf(2, width, slots),
             buf(2, 2, ff_piece, width),
             buf(2, width >> 3, width),

time: 257 us -> 251 us (0.977)
  Pallas kernels: 255 us -> 248 us
    pallas_call x1, Pallas kernels: 114 us -> 108 us  [back(): pl.pallas_call(functools.partial(back_kernel, dp_size, tp_size), out_shap...]
where the time goes in v7:
time: 251 us; the launch traced here: 250 us
  Pallas kernels  248 us (99%)
    pallas_call x1, Pallas kernels, back(): pl.pallas_call(functools.partial(back_kernel, dp_size, tp_size), out_shap...  108 us
    pallas_call x1, Pallas kernels, middle(): pl.pallas_call(functools.partial(middle_kernel, dp_size, tp_size), out_sh...  70.3 us
    pallas_call x1, Pallas kernels, front(): pl.pallas_call(functools.partial(front_kernel, dp_size, tp_size, len(vect...  57.6 us
    pallas_call x1, Pallas kernels, finish(): pl.pallas_call(functools.partial(finish_kernel, tp_size), out_shape=tuple...  13.1 us

profile of v7, /device:TPU:0, one launch (start us, length us, event | category | flops | bytes accessed | tf_op | source)
XLA Modules:
  0.0 250.0 jit_solution(3918742551452296861)
XLA Ops:
  1.3 57.6 %front.1 = (f32[16,768]{1,0:T(8,128)}, f32[4,8,768]{2,1,0:T(8,128)}, f32[1024,768]{1,0:T(8,128)}, f32[1024,128]{1,0:T(8,128)}, bf16[1024,768]{1,0:T(8,128)(2,1)}...) custom-call(s32[1]{0:T(128)S(6)} %copy.39.len_ref, ...), custom_call_target="tpu_custom_call" | custom-call | tf_op jit(solution)/shard_map/front/pallas_call | solution.py:342
  58.9 70.3 %middle.1 = (bf16[1024,768]{1,0:T(8,128)(2,1)}, f32[1024,768]{1,0:T(8,128)}, f32[16,768]{1,0:T(8,128)}, bf16[2,96,768]{2,1,0:T(8,128)(2,1)}, bf16[2,96,768]{2,1,...) custom-call(f32[16,768]{1,0:T(8,128)} %get-tuple-element.66.vec, ...), custom_call_target="tpu_custom_call" | custom-call | tf_op jit(solution)/shard_map/middle/pallas_call | solution.py:1405
  129.3 107.5 %back.1 = (bf16[1024,768]{1,0:T(8,128)(2,1)}, bf16[2,768,768]{2,1,0:T(8,128)(2,1)}, bf16[768,768]{1,0:T(8,128)(2,1)}, bf16[768,768]{1,0:T(8,128)(2,1)}, bf16[4,3...) custom-call(s32[1]{0:T(128)S(6)} %copy.39.len_ref, f32[16,768]{1,0:T(8,128)} %get-tuple-element.66.vec, ...), custom_call_target="tpu_custom_call" | custom-call | tf_op jit(solution)/shard_map/back/pallas_call | solution.py:1069
  236.8 13.1 %finish.1 = (f32[768,768]{1,0:T(8,128)}, f32[768,768]{1,0:T(8,128)}, f32[768,768]{1,0:T(8,128)}, f32[768,768]{1,0:T(8,128)}, f32[768,768]{1,0:T(8,128)}, /*index...) custom-call(bf16[2,768,768]{2,1,0:T(8,128)(2,1)} %get-tuple-element., ...), custom_call_target="tpu_custom_call" | custom-call | tf_op jit(solution)/shard_map/finish/pallas_call | solution.py:1497

commit v8 on v7

--- a/solution.py
+++ b/solution.py
@@ -651,7 +651,7 @@
         slot = link.take(2)
 
         def piece_copy(n, m=m, slot=slot):
-            source, k = ((far_acc, 3), (ff_near, 2))[n]
+            source, k = ((far_acc, 3), (ff_near, 1))[n]
             return link.remote(slot + n, source.at[m], ff_zland.at[m, n], (link.dp, link.behind(k)))
 
         at = link.bit(ff_orders[m][0]) * (width >> 1) + own.offset()
@@ -1333,7 +1333,7 @@
                     spread.start(n - late, m, stage + 1)
 
     def backward(n, carry):
-        k = lax.rem(n + 1, tp_size)
+        k = 2 - n + lax.div(n, 2) * (7 - 2 * n)
         cols = place(k, width)
         slot = lax.rem(n, 2)
         weight_grad(act, k * width, d_branch, slice(0, width), sent.at[1, slot])
@@ -1369,7 +1369,7 @@
         spread.finish(0, m, 2)
         at = rows_at(spread.inside(m, 2), width >> 3, 16)
         crossing.append(
-            link.remote(slot + m, acc.at[m, 0, at, :], ff_landed.at[m], (link.dp, link.behind(1)))
+            link.remote(slot + m, acc.at[m, 0, at, :], ff_landed.at[m], (link.dp, link.behind(2)))
         )
         crossing[-1].start()
     spread.finish(3, 0, 0)

time: 251 us -> 250 us (level)
    pallas_call x1, Pallas kernels: 108 us -> 100 us  [back(): pl.pallas_call(functools.partial(back_kernel, dp_size, tp_size), out_shap...]
    pallas_call x1, Pallas kernels: 70.3 us -> 76.7 us  [middle(): pl.pallas_call(functools.partial(middle_kernel, dp_size, tp_size), out_sh...]
where the time goes in v8:
time: 250 us; the launch traced here: 249 us
  Pallas kernels  248 us (99%)
    pallas_call x1, Pallas kernels, back(): pl.pallas_call(functools.partial(back_kernel, dp_size, tp_size), out_shap...  100 us
    pallas_call x1, Pallas kernels, middle(): pl.pallas_call(functools.partial(middle_kernel, dp_size, tp_size), out_sh...  76.7 us
    pallas_call x1, Pallas kernels, front(): pl.pallas_call(functools.partial(front_kernel, dp_size, tp_size, len(vect...  57.6 us
    pallas_call x1, Pallas kernels, finish(): pl.pallas_call(functools.partial(finish_kernel, tp_size), out_shape=tuple...  13.1 us

profile of v8, /device:TPU:0, one launch (start us, length us, event | category | flops | bytes accessed | tf_op | source)
XLA Modules:
  0.0 249.3 jit_solution(6525313570575424674)
XLA Ops:
  1.3 57.6 %front.1 = (f32[16,768]{1,0:T(8,128)}, f32[4,8,768]{2,1,0:T(8,128)}, f32[1024,768]{1,0:T(8,128)}, f32[1024,128]{1,0:T(8,128)}, bf16[1024,768]{1,0:T(8,128)(2,1)}...) custom-call(s32[1]{0:T(128)S(6)} %copy.39.len_ref, ...), custom_call_target="tpu_custom_call" | custom-call | tf_op jit(solution)/shard_map/front/pallas_call | solution.py:342
  58.9 76.7 %middle.1 = (bf16[1024,768]{1,0:T(8,128)(2,1)}, f32[1024,768]{1,0:T(8,128)}, f32[16,768]{1,0:T(8,128)}, bf16[2,96,768]{2,1,0:T(8,128)(2,1)}, bf16[2,96,768]{2,1,...) custom-call(f32[16,768]{1,0:T(8,128)} %get-tuple-element.66.vec, ...), custom_call_target="tpu_custom_call" | custom-call | tf_op jit(solution)/shard_map/middle/pallas_call | solution.py:1405
  135.6 100.4 %back.1 = (bf16[1024,768]{1,0:T(8,128)(2,1)}, bf16[2,768,768]{2,1,0:T(8,128)(2,1)}, bf16[768,768]{1,0:T(8,128)(2,1)}, bf16[768,768]{1,0:T(8,128)(2,1)}, bf16[4,3...) custom-call(s32[1]{0:T(128)S(6)} %copy.39.len_ref, f32[16,768]{1,0:T(8,128)} %get-tuple-element.66.vec, ...), custom_call_target="tpu_custom_call" | custom-call | tf_op jit(solution)/shard_map/back/pallas_call | solution.py:1069
  236.0 13.1 %finish.1 = (f32[768,768]{1,0:T(8,128)}, f32[768,768]{1,0:T(8,128)}, f32[768,768]{1,0:T(8,128)}, f32[768,768]{1,0:T(8,128)}, f32[768,768]{1,0:T(8,128)}, /*index...) custom-call(bf16[2,768,768]{2,1,0:T(8,128)(2,1)} %get-tuple-element., ...), custom_call_target="tpu_custom_call" | custom-call | tf_op jit(solution)/shard_map/finish/pallas_call | solution.py:1497

commit v9 on v8

--- a/solution.py
+++ b/solution.py
@@ -1364,7 +1364,6 @@
 
     slot = link.take(2)
     crossing = []
-    lax.fori_loop(0, 1, input_grad, 0)
     for m in (1, 0):
         spread.finish(0, m, 2)
         at = rows_at(spread.inside(m, 2), width >> 3, 16)
@@ -1372,6 +1371,7 @@
             link.remote(slot + m, acc.at[m, 0, at, :], ff_landed.at[m], (link.dp, link.behind(2)))
         )
         crossing[-1].start()
+    lax.fori_loop(0, 1, input_grad, 0)
     spread.finish(3, 0, 0)
     spread.finish(2, 1, 1)
     stores = [local(acc.at[m, 3], ff_own.at[m]) for m in range(2)]

time: 250 us -> 248 us (level)
  no operation moved by 1% of the time
where the time goes in v9:
time: 248 us
  Pallas kernels  246 us (99%)
    pallas_call x1, Pallas kernels, back(): pl.pallas_call(functools.partial(back_kernel, dp_size, tp_size), out_shap...  101 us
    pallas_call x1, Pallas kernels, middle(): pl.pallas_call(functools.partial(middle_kernel, dp_size, tp_size), out_sh...  74.7 us
    pallas_call x1, Pallas kernels, front(): pl.pallas_call(functools.partial(front_kernel, dp_size, tp_size, len(vect...  57.6 us
    pallas_call x1, Pallas kernels, finish(): pl.pallas_call(functools.partial(finish_kernel, tp_size), out_shape=tuple...  13.1 us

profile of v9, /device:TPU:0, one launch (start us, length us, event | category | flops | bytes accessed | tf_op | source)
XLA Modules:
  0.0 247.8 jit_solution(13204119678336710363)
XLA Ops:
  1.3 57.6 %front.1 = (f32[16,768]{1,0:T(8,128)}, f32[4,8,768]{2,1,0:T(8,128)}, f32[1024,768]{1,0:T(8,128)}, f32[1024,128]{1,0:T(8,128)}, bf16[1024,768]{1,0:T(8,128)(2,1)}...) custom-call(s32[1]{0:T(128)S(6)} %copy.39.len_ref, ...), custom_call_target="tpu_custom_call" | custom-call | tf_op jit(solution)/shard_map/front/pallas_call | solution.py:342
  58.9 74.7 %middle.1 = (bf16[1024,768]{1,0:T(8,128)(2,1)}, f32[1024,768]{1,0:T(8,128)}, f32[16,768]{1,0:T(8,128)}, bf16[2,96,768]{2,1,0:T(8,128)(2,1)}, bf16[2,96,768]{2,1,...) custom-call(f32[16,768]{1,0:T(8,128)} %get-tuple-element.66.vec, ...), custom_call_target="tpu_custom_call" | custom-call | tf_op jit(solution)/shard_map/middle/pallas_call | solution.py:1405
  133.6 100.9 %back.1 = (bf16[1024,768]{1,0:T(8,128)(2,1)}, bf16[2,768,768]{2,1,0:T(8,128)(2,1)}, bf16[768,768]{1,0:T(8,128)(2,1)}, bf16[768,768]{1,0:T(8,128)(2,1)}, bf16[4,3...) custom-call(s32[1]{0:T(128)S(6)} %copy.39.len_ref, f32[16,768]{1,0:T(8,128)} %get-tuple-element.66.vec, ...), custom_call_target="tpu_custom_call" | custom-call | tf_op jit(solution)/shard_map/back/pallas_call | solution.py:1069
  234.6 13.1 %finish.1 = (f32[768,768]{1,0:T(8,128)}, f32[768,768]{1,0:T(8,128)}, f32[768,768]{1,0:T(8,128)}, f32[768,768]{1,0:T(8,128)}, f32[768,768]{1,0:T(8,128)}, /*index...) custom-call(bf16[2,768,768]{2,1,0:T(8,128)(2,1)} %get-tuple-element., ...), custom_call_target="tpu_custom_call" | custom-call | tf_op jit(solution)/shard_map/finish/pallas_call | solution.py:1497
